TPU v7x, 32 devices: a whole 2x2x4 slice. The times are simulated.
32 devices in a mesh: shard: 4 (over z), ctx: 4 (over x, core), tp: 2 (over y).
Axes of the slice: x: 2, y: 2, z: 4, core: 2. Of those that a mesh axis runs over, the one named last changes fastest.
Arguments:
- tokens: bfloat16 [12288, 2048], P(('shard', 'ctx')), may hold values from -6 to 6
- seg_ids: int32 [12288], P('shard'), may hold values from 0 to 4, as said below
- positions: int32 [12288], P('shard'), may hold values from 0 to 3068, as said below
- cotangent: bfloat16 [12288, 2048], P(('shard', 'ctx')), may hold values from -6 to 6
- norm_in: bfloat16 [2048], P(('shard', 'ctx')), may hold values from 0.5 to 1.5
- norm_mid: bfloat16 [2048], P(('shard', 'ctx')), may hold values from 0.5 to 1.5
- query_gain: bfloat16 [128], P(('shard', 'ctx')), may hold values from 0.8984375 to 1.5
- key_gain: bfloat16 [128], P(('shard', 'ctx')), may hold values from 0.8984375 to 1.5
- query_weight: bfloat16 [2048, 2048], P(('shard', 'ctx'), 'tp'), may hold values from -0.125 to 0.125
- key_matrix: bfloat16 [2048, 1024], P(('shard', 'ctx'), 'tp'), may hold values from -0.125 to 0.125
- value_matrix: bfloat16 [2048, 1024], P(('shard', 'ctx'), 'tp'), may hold values from -0.125 to 0.125
- head_weight: bfloat16 [2048, 16], P(('shard', 'ctx'), 'tp'), may hold values from -0.125 to 0.125
- out_weight: bfloat16 [2048, 2048], P('tp', ('shard', 'ctx')), may hold values from -3 to 3
- gate_weight: bfloat16 [2048, 6144], P(('shard', 'ctx'), 'tp'), may hold values from -0.125 to 0.125
- up_weight: bfloat16 [2048, 6144], P(('shard', 'ctx'), 'tp'), may hold values from -0.125 to 0.125
- down_weight: bfloat16 [6144, 2048], P('tp', ('shard', 'ctx')), may hold values from -0.078125 to 0.078125
Outputs:
- output: bfloat16 [12288, 2048], P(('shard', 'ctx'))
- input_grad: float32 [12288, 2048], P(('shard', 'ctx'))
- grad_norm_in: float32 [2048], P(('shard', 'ctx'))
- grad_norm_mid: float32 [2048], P(('shard', 'ctx'))
- grad_query_gain: float32 [128], P(('shard', 'ctx'))
- grad_key_gain: float32 [128], P(('shard', 'ctx'))
- grad_query: float32 [2048, 2048], P(('shard', 'ctx'), 'tp')
- grad_key: float32 [2048, 1024], P(('shard', 'ctx'), 'tp')
- grad_value: float32 [2048, 1024], P(('shard', 'ctx'), 'tp')
- grad_head: float32 [2048, 16], P(('shard', 'ctx'), 'tp')
- grad_out: float32 [2048, 2048], P('tp', ('shard', 'ctx'))
- grad_gate: float32 [2048, 6144], P(('shard', 'ctx'), 'tp')
- grad_up: float32 [2048, 6144], P(('shard', 'ctx'), 'tp')
- grad_down: float32 [6144, 2048], P('tp', ('shard', 'ctx'))
Inputs may be any that keep to these rules, and one draw needn't show every extreme that they name: `seg_ids`: in each group's blocks of 768 rows the first 512 rows have segment 0 and the others hold, block after block, a stream of 1024 rows in which continuations 1 to 4 follow in order, each one row or more. Prompt rows of a group have positions 0, 1, ... in the order of the blocks; the rows of a continuation have 2048, 2049, ... in stream order; in the first group continuations 1 to 3 have one row each.
All inputs are finite; a program needn't handle non-finite values.
Results may differ from a plain program's by a relative error of at most 0.014.
Values may be sent and summed in bfloat16 or wider, within the bound.
No kernel may reach another device: no remote copies, remote signals or barrier semaphores. Data moves between devices by JAX's collectives and lax.ppermute only.
A program may use at most 384 MiB of HBM per device.

v0:
```python
import functools
import math

import jax
import jax.numpy as jnp
import numpy as np
from jax import lax
from jax.experimental import pallas as pl
from jax.experimental.pallas import tpu as pltpu
from jax.sharding import PartitionSpec as P

HEAD = 128
LANES = 128
EPS = 1e-06
THETA = 1000000.0
MASKED = -1e30
LOG2E = 1.4426950408889634
SCALE = HEAD ** (-0.5)
KEY_TILE = 256
CHUNKS = 3

F32 = jnp.float32
BF16 = jnp.bfloat16


def matmul(a, b, dims=((1,), (0,))):
    return lax.dot_general(a, b, (dims, ((), ())), preferred_element_type=F32)


def ring_tables(n_shard, n_ctx):
    path = []
    for x in range(n_ctx // 2):
        column = range(n_shard) if x % 2 == 0 else reversed(range(n_shard))
        path += [(z, x) for z in column]
    length = len(path)

    def device(place, core):
        z, x = path[place % length]
        return z * n_ctx + x * 2 + core

    hops = [(device(r, 0), device(r + 1, 0)) for r in range(length)]
    hops += [(device(r, 1), device(r - 1, 1)) for r in range(length)]
    order = np.zeros((n_shard * n_ctx, 2 * length), np.int32)
    for r in range(length):
        for core in (0, 1):
            back = -1 if core == 0 else 1
            own = [device(r + back * s, core) for s in range(length)]
            other = [device(r - back * s, 1 - core) for s in range(length)]
            order[device(r, core)] = own + other
    return hops, order, length


RING_AXES = ("shard", "ctx")


class Ring:
    def __init__(self, n_shard, n_ctx):
        self.hops, self.order, self.length = ring_tables(n_shard, n_ctx)
        self.swaps = [(i, i ^ 1) for i in range(n_ctx)]

    def hop(self, value):
        return lax.ppermute(value, RING_AXES, self.hops)

    def swap(self, value):
        return lax.ppermute(value, "ctx", self.swaps)

    def gather(self, block):
        pieces = [block]
        for _ in range(self.length - 1):
            pieces.append(self.hop(pieces[-1]))
        return pieces

    def assemble(self, pieces):
        return jnp.concatenate(pieces + [self.swap(piece) for piece in pieces], axis=0)

    def reduce(self, kept):
        rows = kept.shape[0] // self.length
        total = kept[rows : 2 * rows]
        for step in range(2, self.length + 1):
            place = (step % self.length) * rows
            total = self.hop(total).astype(F32) + kept[place : place + rows].astype(F32)
            if step < self.length:
                total = total.astype(BF16)
        return total


def after(value, *others):
    return lax.optimization_barrier((value, *others))[0]


def tp_scatter(partial, n_tp):
    rows = partial.shape[0] // n_tp
    total = partial[:rows]
    for j in range(1, n_tp):
        sent = partial[j * rows : (j + 1) * rows].astype(BF16)
        total = total + lax.ppermute(
            sent, "tp", [(i, (i + j) % n_tp) for i in range(n_tp)]
        ).astype(F32)
    return total


def tp_gather(block, n_tp):
    blocks = [block]
    for j in range(1, n_tp):
        blocks.append(lax.ppermute(block, "tp", [(i, (i - j) % n_tp) for i in range(n_tp)]))
    return blocks


def tp_total(value, n_tp):
    total = value
    for j in range(1, n_tp):
        total = total + lax.ppermute(value, "tp", [(i, (i + j) % n_tp) for i in range(n_tp)])
    return total


def row_tile(rows):
    return next(tile for tile in (128, 96, 64, 48, 32, 16) if rows % tile == 0)


def params(mib=48):
    return pltpu.CompilerParams(vmem_limit_bytes=mib << 20)


def enter_kernel(order_ref, rows_ref, tok_ref, cot_ref, tok_out, cot_out, scale_out):
    value = tok_ref[...].astype(F32)
    scale = lax.rsqrt(jnp.mean(value * value, axis=-1, keepdims=True) + EPS)
    scale_out[...] = jnp.broadcast_to(scale, scale_out.shape)
    blocks = tok_ref.shape[1] // LANES
    for j in range(blocks):
        source = pl.multiple_of(order_ref[j] * LANES, LANES)
        here = slice(j * LANES, (j + 1) * LANES)
        tok_out[:, here] = tok_ref[:, pl.ds(source, LANES)]
        cot_out[:, here] = cot_ref[:, pl.ds(source, LANES)]


def enter(order, tiles, tile, tokens, cotangent):
    rows, width = tokens.shape
    block = pl.BlockSpec((tile, width), lambda i, order, tiles: (tiles[i], 0))
    out = pl.BlockSpec((tile, width), lambda i, order, tiles: (i, 0))
    return pl.pallas_call(
        enter_kernel,
        grid_spec=pltpu.PrefetchScalarGridSpec(
            num_scalar_prefetch=2,
            grid=(rows // tile,),
            in_specs=[block, block],
            out_specs=[
                out,
                out,
                pl.BlockSpec((tile, LANES), lambda i, order, tiles: (i, 0)),
            ],
        ),
        out_shape=[
            jax.ShapeDtypeStruct((rows, width), BF16),
            jax.ShapeDtypeStruct((rows, width), BF16),
            jax.ShapeDtypeStruct((rows, LANES), F32),
        ],
        compiler_params=params(),
        name="enter",
    )(order, tiles, tokens, cotangent)


def leave_kernel(order_ref, value_ref, out_ref):
    blocks = value_ref.shape[1] // LANES
    for j in range(blocks):
        target = pl.multiple_of(order_ref[j] * LANES, LANES)
        out_ref[:, pl.ds(target, LANES)] = value_ref[:, j * LANES : (j + 1) * LANES].astype(
            out_ref.dtype
        )


def leave(order, tiles, tile, value, dtype, name):
    rows, width = value.shape
    return pl.pallas_call(
        lambda order, tiles, value, out: leave_kernel(order, value, out),
        grid_spec=pltpu.PrefetchScalarGridSpec(
            num_scalar_prefetch=2,
            grid=(rows // tile,),
            in_specs=[pl.BlockSpec((tile, width), lambda i, order, tiles: (i, 0))],
            out_specs=pl.BlockSpec((tile, width), lambda i, order, tiles: (tiles[i], 0)),
        ),
        out_shape=jax.ShapeDtypeStruct((rows, width), dtype),
        compiler_params=params(),
        name=name,
    )(order, tiles, value)


def turn(value, cos, sin):
    return value * cos + pltpu.roll(value, HEAD // 2, 1) * sin


def heads_kernel(
    q_heads, k_heads, tiles_ref, a_ref, b_ref, cos_ref, sin_ref, qg_ref, kg_ref, q_out, kv_out, sg_out
):
    cos, sin = cos_ref[...], sin_ref[...]

    def rotated(value, gain):
        scale = lax.rsqrt(jnp.mean(value * value, axis=-1, keepdims=True) + EPS)
        return turn(value * scale * gain, cos, sin).astype(BF16)

    for h in range(q_heads):
        here = slice(h * HEAD, (h + 1) * HEAD)
        q_out[:, here] = rotated(a_ref[:, here], qg_ref[...])
    for h in range(k_heads):
        here = slice(h * HEAD, (h + 1) * HEAD)
        kv_out[:, here] = rotated(b_ref[:, here], kg_ref[...])
    kv_out[:, k_heads * HEAD :] = b_ref[:, k_heads * HEAD :].astype(BF16)
    sg_out[...] = jax.nn.sigmoid(a_ref[:, q_heads * HEAD :])


def make_heads(tiles, tile, raw_a, raw_b, cos, sin, q_gain, k_gain, q_heads, k_heads):
    rows = raw_a.shape[0]

    def at(width):
        return pl.BlockSpec((tile, width), lambda i, tiles: (i, 0))

    gain = pl.BlockSpec((1, HEAD), lambda i, tiles: (0, 0))
    return pl.pallas_call(
        functools.partial(heads_kernel, q_heads, k_heads),
        grid_spec=pltpu.PrefetchScalarGridSpec(
            num_scalar_prefetch=1,
            grid=(rows // tile,),
            in_specs=[at(raw_a.shape[1]), at(raw_b.shape[1]), at(HEAD), at(HEAD), gain, gain],
            out_specs=[
                at(q_heads * HEAD),
                pl.BlockSpec((tile, 2 * k_heads * HEAD), lambda i, tiles: (tiles[i], 0)),
                at(LANES),
            ],
        ),
        out_shape=[
            jax.ShapeDtypeStruct((rows, q_heads * HEAD), BF16),
            jax.ShapeDtypeStruct((rows, 2 * k_heads * HEAD), BF16),
            jax.ShapeDtypeStruct((rows, LANES), F32),
        ],
        compiler_params=params(),
        name="make_heads",
    )(tiles, raw_a, raw_b, cos, sin, q_gain, k_gain)


def heads_back_kernel(
    q_heads, k_heads, tiles_ref, *refs
):
    (dq_ref, dkv1_ref, dkv2_ref, dkv3_ref, dlog_ref, a_ref, b_ref, cos_ref, sin_ref, qg_ref, kg_ref) = refs[:11]
    a_out, b_out, gain_out = refs[11:]

    @pl.when(pl.program_id(0) == 0)
    def _():
        gain_out[...] = jnp.zeros_like(gain_out)

    cos, sin = cos_ref[...], -sin_ref[...]

    def back(grad, value, gain):
        scale = lax.rsqrt(jnp.mean(value * value, axis=-1, keepdims=True) + EPS)
        unit = value * scale
        turned = turn(grad, cos, sin)
        scaled = turned * gain
        result = scale * (scaled - unit * jnp.mean(scaled * unit, axis=-1, keepdims=True))
        return result.astype(BF16), jnp.sum(turned * unit, axis=0, keepdims=True)

    q_total = jnp.zeros((1, HEAD), F32)
    k_total = jnp.zeros((1, HEAD), F32)
    for h in range(q_heads):
        here = slice(h * HEAD, (h + 1) * HEAD)
        a_out[:, here], more = back(dq_ref[:, here], a_ref[:, here], qg_ref[...])
        q_total += more
    a_out[:, q_heads * HEAD :] = dlog_ref[...]

    def total(here):
        return (
            dkv1_ref[:, here].astype(F32)
            + dkv2_ref[:, here].astype(F32)
            + dkv3_ref[:, here].astype(F32)
        )

    for h in range(k_heads):
        here = slice(h * HEAD, (h + 1) * HEAD)
        b_out[:, here], more = back(total(here), b_ref[:, here], kg_ref[...])
        k_total += more
    there = slice(k_heads * HEAD, 2 * k_heads * HEAD)
    b_out[:, there] = total(there).astype(BF16)
    gain_out[0:1, :] += q_total
    gain_out[1:2, :] += k_total


def heads_back(tiles, tile, dq, dkvs, dlog, raw_a, raw_b, cos, sin, q_gain, k_gain, q_heads, k_heads):
    rows = raw_a.shape[0]

    def at(width):
        return pl.BlockSpec((tile, width), lambda i, tiles: (i, 0))

    gain = pl.BlockSpec((1, HEAD), lambda i, tiles: (0, 0))
    moved = pl.BlockSpec((tile, 2 * k_heads * HEAD), lambda i, tiles: (tiles[i], 0))
    return pl.pallas_call(
        functools.partial(heads_back_kernel, q_heads, k_heads),
        grid_spec=pltpu.PrefetchScalarGridSpec(
            num_scalar_prefetch=1,
            grid=(rows // tile,),
            in_specs=[
                at(q_heads * HEAD),
                moved,
                moved,
                moved,
                at(LANES),
                at(raw_a.shape[1]),
                at(raw_b.shape[1]),
                at(HEAD),
                at(HEAD),
                gain,
                gain,
            ],
            out_specs=[
                at(raw_a.shape[1]),
                at(raw_b.shape[1]),
                pl.BlockSpec((8, HEAD), lambda i, tiles: (0, 0)),
            ],
        ),
        out_shape=[
            jax.ShapeDtypeStruct(raw_a.shape, BF16),
            jax.ShapeDtypeStruct(raw_b.shape, BF16),
            jax.ShapeDtypeStruct((8, HEAD), F32),
        ],
        compiler_params=params(),
        name="heads_back",
    )(tiles, dq, *dkvs, dlog, raw_a, raw_b, cos, sin, q_gain, k_gain)


def load_keys(kv_refs, kv_all, sem, block_rows):
    copies = [
        pltpu.make_async_copy(ref, kv_all.at[pl.ds(m * block_rows, block_rows)], sem.at[m])
        for m, ref in enumerate(kv_refs)
    ]
    for copy in copies:
        copy.start()
    for copy in copies:
        copy.wait()


def stacked(ref, g, share):
    return jnp.concatenate(
        [ref[:, (g * share + j) * HEAD : (g * share + j + 1) * HEAD] for j in range(share)], axis=0
    )


def attend_kernel(q_heads, k_heads, blocks, flags_ref, *refs):
    q_ref, bias_ref, sg_ref = refs[:3]
    kv_refs = refs[3 : 3 + blocks]
    att_out, gated_out, lse_out = refs[3 + blocks : 6 + blocks]
    kv_all, acc, norm, sem = refs[6 + blocks :]
    share = q_heads // k_heads
    tile = q_ref.shape[0]
    step = pl.program_id(0)
    key_tiles = kv_all.shape[0] // KEY_TILE

    @pl.when(step == 0)
    def _():
        load_keys(kv_refs, kv_all, sem, kv_all.shape[0] // blocks)

    acc[...] = jnp.zeros_like(acc)
    norm[...] = jnp.zeros_like(norm)

    @pl.loop(0, key_tiles)
    def _(t):
        @pl.when(flags_ref[step * key_tiles + t] > 0)
        def _():
            rows = pl.ds(pl.multiple_of(t * KEY_TILE, KEY_TILE), KEY_TILE)
            bias = bias_ref[:, rows]
            bias = jnp.concatenate([bias] * share, axis=0)
            for g in range(k_heads):
                keys = kv_all[rows, g * HEAD : (g + 1) * HEAD]
                values = kv_all[rows, (k_heads + g) * HEAD : (k_heads + g + 1) * HEAD]
                scores = matmul(stacked(q_ref, g, share), keys, ((1,), (1,)))
                weights = jnp.exp2(scores * (SCALE * LOG2E) + bias)
                norm[g] += jnp.sum(weights, axis=1, keepdims=True)
                acc[g] += matmul(weights.astype(BF16), values)

    lane = lax.broadcasted_iota(jnp.int32, (tile, LANES), 1)
    lse = jnp.zeros((tile, LANES), F32)
    for g in range(k_heads):
        total = norm[g]
        attended = acc[g] / total
        log_total = jnp.log2(total)
        for j in range(share):
            h = g * share + j
            here = slice(h * HEAD, (h + 1) * HEAD)
            part = attended[j * tile : (j + 1) * tile]
            att_out[:, here] = part
            gated_out[:, here] = (part * sg_ref[:, h : h + 1]).astype(BF16)
            lse = jnp.where(lane == h, log_total[j * tile : (j + 1) * tile], lse)
    lse_out[...] = lse


def attend(flags, tile, queries, bias, sg, kvs, q_heads, k_heads):
    rows = queries.shape[0]
    blocks = len(kvs)
    keys = sum(kv.shape[0] for kv in kvs)
    share = q_heads // k_heads

    def at(width):
        return pl.BlockSpec((tile, width), lambda i, flags: (i, 0))

    return pl.pallas_call(
        functools.partial(attend_kernel, q_heads, k_heads, blocks),
        grid_spec=pltpu.PrefetchScalarGridSpec(
            num_scalar_prefetch=1,
            grid=(rows // tile,),
            in_specs=[at(q_heads * HEAD), at(keys), at(LANES)]
            + [pl.BlockSpec(memory_space=pl.ANY)] * blocks,
            out_specs=[at(q_heads * HEAD), at(q_heads * HEAD), at(LANES)],
            scratch_shapes=[
                pltpu.VMEM((keys, 2 * k_heads * HEAD), BF16),
                pltpu.VMEM((k_heads, share * tile, HEAD), F32),
                pltpu.VMEM((k_heads, share * tile, 1), F32),
                pltpu.SemaphoreType.DMA((blocks,)),
            ],
        ),
        out_shape=[
            jax.ShapeDtypeStruct((rows, q_heads * HEAD), F32),
            jax.ShapeDtypeStruct((rows, q_heads * HEAD), BF16),
            jax.ShapeDtypeStruct((rows, LANES), F32),
        ],
        compiler_params=params(),
        cost_estimate=pl.CostEstimate(
            flops=2 * rows * keys * HEAD * q_heads * 2,
            bytes_accessed=rows * keys * 4,
            transcendentals=rows * keys * q_heads,
        ),
        name="attend",
    )(flags, queries, bias, sg, *kvs)


def attend_back_kernel(q_heads, k_heads, blocks, flags_ref, *refs):
    q_ref, bias_ref, sg_ref, lse_ref, att_ref, dgat_ref = refs[:6]
    kv_refs = refs[6 : 6 + blocks]
    dq_out, dlog_out, keep_out, send_out = refs[6 + blocks : 10 + blocks]
    kv_all, dkv, dq, dout, delta, lses, sem = refs[10 + blocks :]
    share = q_heads // k_heads
    tile = q_ref.shape[0]
    step = pl.program_id(0)
    key_tiles = kv_all.shape[0] // KEY_TILE

    @pl.when(step == 0)
    def _():
        load_keys(kv_refs, kv_all, sem, kv_all.shape[0] // blocks)
        dkv[...] = jnp.zeros_like(dkv)

    dq[...] = jnp.zeros_like(dq)
    lane = lax.broadcasted_iota(jnp.int32, (tile, LANES), 1)
    dlog = jnp.zeros((tile, LANES), F32)
    for h in range(q_heads):
        g, j = h // share, h % share
        here = slice(h * HEAD, (h + 1) * HEAD)
        there = slice(j * tile, (j + 1) * tile)
        sg = sg_ref[:, h : h + 1]
        dgat = dgat_ref[:, here]
        att = att_ref[:, here]
        rounded = (dgat * sg).astype(BF16)
        dout[g, there] = rounded
        delta[g, there] = jnp.sum(rounded.astype(F32) * att, axis=1, keepdims=True)
        lses[g, there] = lse_ref[:, h : h + 1]
        dlog_h = jnp.sum(dgat * att, axis=1, keepdims=True) * sg * (1.0 - sg)
        dlog = jnp.where(lane == h, dlog_h, dlog)
    dlog_out[...] = dlog.astype(BF16)

    @pl.loop(0, key_tiles)
    def _(t):
        @pl.when(flags_ref[step * key_tiles + t] > 0)
        def _():
            rows = pl.ds(pl.multiple_of(t * KEY_TILE, KEY_TILE), KEY_TILE)
            bias = bias_ref[:, rows]
            bias = jnp.concatenate([bias] * share, axis=0)
            for g in range(k_heads):
                k_here = slice(g * HEAD, (g + 1) * HEAD)
                v_here = slice((k_heads + g) * HEAD, (k_heads + g + 1) * HEAD)
                keys = kv_all[rows, k_here]
                values = kv_all[rows, v_here]
                queries = stacked(q_ref, g, share)
                scores = matmul(queries, keys, ((1,), (1,)))
                probs = jnp.exp2(scores * (SCALE * LOG2E) + bias - lses[g])
                dprobs = matmul(dout[g], values, ((1,), (1,)))
                dscores = (probs * (dprobs - delta[g])).astype(BF16)
                dkv[rows, v_here] += matmul(probs.astype(BF16), dout[g], ((0,), (0,)))
                dkv[rows, k_here] += matmul(dscores, queries, ((0,), (0,)))
                dq[g] += matmul(dscores, keys)

    for h in range(q_heads):
        g, j = h // share, h % share
        dq_out[:, h * HEAD : (h + 1) * HEAD] = dq[g, j * tile : (j + 1) * tile] * SCALE

    @pl.when(step == pl.num_programs(0) - 1)
    def _():
        half = kv_all.shape[0] // 2
        k_all = slice(0, k_heads * HEAD)
        v_all = slice(k_heads * HEAD, 2 * k_heads * HEAD)
        for out, first in ((keep_out, 0), (send_out, half)):
            out[:, k_all] = (dkv[first : first + half, k_all] * SCALE).astype(BF16)
            out[:, v_all] = dkv[first : first + half, v_all].astype(BF16)


def attend_back(flags, tile, queries, bias, sg, lse, att, dgat, kvs, q_heads, k_heads):
    rows = queries.shape[0]
    blocks = len(kvs)
    keys = sum(kv.shape[0] for kv in kvs)
    share = q_heads // k_heads
    kv_width = 2 * k_heads * HEAD

    def at(width):
        return pl.BlockSpec((tile, width), lambda i, flags: (i, 0))

    whole = pl.BlockSpec((keys // 2, kv_width), lambda i, flags: (0, 0))
    return pl.pallas_call(
        functools.partial(attend_back_kernel, q_heads, k_heads, blocks),
        grid_spec=pltpu.PrefetchScalarGridSpec(
            num_scalar_prefetch=1,
            grid=(rows // tile,),
            in_specs=[
                at(q_heads * HEAD),
                at(keys),
                at(LANES),
                at(LANES),
                at(q_heads * HEAD),
                at(q_heads * HEAD),
            ]
            + [pl.BlockSpec(memory_space=pl.ANY)] * blocks,
            out_specs=[at(q_heads * HEAD), at(LANES), whole, whole],
            scratch_shapes=[
                pltpu.VMEM((keys, kv_width), BF16),
                pltpu.VMEM((keys, kv_width), F32),
                pltpu.VMEM((k_heads, share * tile, HEAD), F32),
                pltpu.VMEM((k_heads, share * tile, HEAD), BF16),
                pltpu.VMEM((k_heads, share * tile, 1), F32),
                pltpu.VMEM((k_heads, share * tile, 1), F32),
                pltpu.SemaphoreType.DMA((blocks,)),
            ],
        ),
        out_shape=[
            jax.ShapeDtypeStruct((rows, q_heads * HEAD), F32),
            jax.ShapeDtypeStruct((rows, LANES), BF16),
            jax.ShapeDtypeStruct((keys // 2, kv_width), BF16),
            jax.ShapeDtypeStruct((keys // 2, kv_width), BF16),
        ],
        compiler_params=params(),
        cost_estimate=pl.CostEstimate(
            flops=2 * rows * keys * HEAD * q_heads * 5,
            bytes_accessed=rows * keys * 4,
            transcendentals=rows * keys * q_heads,
        ),
        name="attend_back",
    )(flags, queries, bias, sg, lse, att, dgat, *kvs)


def per_device(
    sizes,
    tokens,
    seg_ids,
    positions,
    cotangent,
    norm_in,
    norm_mid,
    query_gain,
    key_gain,
    query_weight,
    key_matrix,
    value_matrix,
    head_weight,
    out_weight,
    gate_weight,
    up_weight,
    down_weight,
):
    n_shard, n_ctx, n_tp = sizes
    ring = Ring(n_shard, n_ctx)
    row_count, width = tokens.shape
    block = query_weight.shape[0]
    q_width = query_weight.shape[1]
    k_width = key_matrix.shape[1]
    q_heads, k_heads = q_width // HEAD, k_width // HEAD
    units = gate_weight.shape[1]
    chunk = units // CHUNKS
    rows = row_count // n_tp
    tile = row_tile(rows)

    here_ctx = lax.axis_index("ctx")
    here_tp = lax.axis_index("tp")
    here = lax.axis_index("shard") * n_ctx + here_ctx
    order = lax.dynamic_index_in_dim(jnp.asarray(ring.order), here, keepdims=False)
    inverse = lax.dynamic_index_in_dim(
        jnp.asarray(np.argsort(ring.order, axis=1).astype(np.int32)), here, keepdims=False
    )
    per = rows // tile
    tile_ids = np.arange(row_count // tile)
    tiles = ((here_tp + tile_ids // per) % n_tp) * per + tile_ids % per
    tiles = tiles.astype(jnp.int32)

    columns = [
        head_weight,
        norm_in[:, None],
        norm_mid[:, None],
        jnp.pad(query_gain, (0, block - query_gain.shape[0]))[:, None],
        jnp.pad(key_gain, (0, block - key_gain.shape[0]))[:, None],
    ]
    extra = sum(column.shape[1] for column in columns)
    columns.append(jnp.zeros((block, LANES - extra), BF16))
    send_a = jnp.concatenate([query_weight] + columns, axis=1)
    send_b = jnp.concatenate([key_matrix, value_matrix], axis=1)
    pieces_a = ring.gather(send_a)
    pieces_b = ring.gather(send_b)
    pieces_o = ring.gather(after(out_weight.T, pieces_a[4]))
    pieces_gu, pieces_d = [], []
    gate_after = pieces_a[5]
    for j in range(CHUNKS):
        cut = slice(j * chunk, (j + 1) * chunk)
        both = jnp.concatenate([gate_weight[:, cut], up_weight[:, cut]], axis=1)
        down = down_weight[cut].T
        both, down, _ = lax.optimization_barrier((both, down, gate_after))
        pieces_gu.append(ring.gather(both))
        pieces_d.append(ring.gather(down))
        gate_after = pieces_gu[-1][4]

    tok, cot, scale_in = enter(order, tiles, tile, tokens, cotangent)
    offset = here_ctx * row_count

    def own_rows(values):
        parts = [
            lax.dynamic_slice_in_dim(values, offset + ((here_tp + j) % n_tp) * rows, rows)
            for j in range(n_tp)
        ]
        return jnp.concatenate(parts)

    own_seg, own_pos = own_rows(seg_ids), own_rows(positions)
    block_order = sorted(range(n_ctx), key=lambda m: (m & 1, m))

    def key_rows(values):
        return jnp.concatenate(
            [
                lax.dynamic_slice_in_dim(values, (here_ctx ^ m) * row_count, row_count)
                for m in block_order
            ]
        )

    key_seg, key_pos = key_rows(seg_ids), key_rows(positions)
    allowed = ((key_seg[None, :] == 0) | (key_seg[None, :] == own_seg[:, None])) & (
        key_pos[None, :] <= own_pos[:, None]
    )
    bias = jnp.where(allowed, 0.0, MASKED).astype(F32)
    key_tiles = key_seg.shape[0] // KEY_TILE
    flags = jnp.max(
        allowed.astype(jnp.int32).reshape(row_count // tile, tile, key_tiles, KEY_TILE), axis=(1, 3)
    ).reshape(-1)
    half = HEAD // 2
    frequency = THETA ** (-(jnp.arange(half, dtype=F32) * 2.0) / HEAD)
    angles = own_pos.astype(F32)[:, None] * frequency[None, :]
    cos, sin = jnp.cos(angles), jnp.sin(angles)
    cos = jnp.concatenate([cos, cos], axis=1)
    sin = jnp.concatenate([-sin, sin], axis=1)

    weight_a = ring.assemble(pieces_a)
    weight_b = ring.assemble(pieces_b)
    tail = weight_a[:, q_width:]
    n_head = head_weight.shape[1]
    gain_in = tail[:, n_head].astype(F32)[None, :]
    gain_mid = tail[:, n_head + 1].astype(F32)[None, :]

    def whole_gain(column):
        pieces = tail[:, column].reshape(-1, block)[:, : query_gain.shape[0]]
        return jnp.take(pieces, inverse, axis=0).reshape(1, HEAD).astype(F32)

    q_gain, k_gain = whole_gain(n_head + 2), whole_gain(n_head + 3)
    scale_in = scale_in[:, :1]
    normed = (tok.astype(F32) * scale_in * gain_in).astype(BF16)
    raw_a = matmul(normed, weight_a)
    raw_b = matmul(normed, weight_b)
    queries, kv, sg = make_heads(
        tiles, tile, raw_a, raw_b, cos, sin, q_gain, k_gain, q_heads, k_heads
    )
    kvs = {0: kv}
    bit = n_ctx // 2
    while bit:
        for m in list(kvs):
            kvs[m | bit] = lax.ppermute(kvs[m], "ctx", [(i, i ^ bit) for i in range(n_ctx)])
        bit //= 2
    kvs = [kvs[m] for m in block_order]
    att, gated, lse = attend(flags, tile, queries, bias, sg, kvs, q_heads, k_heads)
    weight_o = ring.assemble(pieces_o)
    branch = tp_scatter(matmul(gated, weight_o, ((1,), (1,))), n_tp)
    middle = tok[:rows].astype(F32) + branch
    scale_mid = lax.rsqrt(jnp.mean(middle * middle, axis=-1, keepdims=True) + EPS)
    unit_mid = middle * scale_mid
    normed_mid = jnp.concatenate(tp_gather((unit_mid * gain_mid).astype(BF16), n_tp))

    own_cols = slice(0, width // 2)
    other_cols = slice(width // 2, width)

    def weight_grad(left, right):
        sent = matmul(left[:, other_cols], right, ((0,), (0,))).astype(BF16)
        kept = matmul(left[:, own_cols], right, ((0,), (0,)))
        return (kept + ring.swap(sent).astype(F32)).astype(BF16)

    mixed = None
    grad_mid = None
    sums_gu, sums_d = [], []
    for j in range(CHUNKS):
        weight_gu = ring.assemble(pieces_gu[j])
        weight_d = ring.assemble(pieces_d[j])
        both = matmul(normed_mid, weight_gu)
        gate, up = both[:, :chunk], both[:, chunk:]
        dhidden = matmul(cot, weight_d)
        sig = jax.nn.sigmoid(gate)
        hidden = (gate * sig * up).astype(BF16)
        dgate = (dhidden * up * sig * (1.0 + gate * (1.0 - sig))).astype(BF16)
        dup = (dhidden * gate * sig).astype(BF16)
        dboth = jnp.concatenate([dgate, dup], axis=1)
        sums_d.append(ring.reduce(weight_grad(cot, hidden)))
        sums_gu.append(ring.reduce(weight_grad(normed_mid, dboth)))
        part = matmul(hidden, weight_d, ((1,), (1,)))
        mixed = part if mixed is None else mixed + part
        part = matmul(dboth, weight_gu, ((1,), (1,)))
        grad_mid = part if grad_mid is None else grad_mid + part

    def norm_back(grad_unit, unit, scale):
        return scale * (grad_unit - unit * jnp.mean(grad_unit * unit, axis=-1, keepdims=True))

    dmid = cot[:rows].astype(F32) + norm_back(
        tp_scatter(grad_mid, n_tp) * gain_mid, unit_mid, scale_mid
    )
    dmid_low = jnp.concatenate(tp_gather(dmid.astype(BF16), n_tp))
    output = (middle + tp_scatter(mixed, n_tp)).astype(BF16)
    output = leave(order, tiles, tile, jnp.concatenate(tp_gather(output, n_tp)), BF16, "leave_output")

    dgat = matmul(dmid_low, weight_o)
    sum_o = ring.reduce(weight_grad(dmid_low, gated))
    dq, dlog, keep, sent = attend_back(
        flags, tile, queries, bias, sg, lse, att, dgat, kvs, q_heads, k_heads
    )
    other = ring.swap(sent)
    blocks = n_ctx // 2
    mine = keep[:row_count]
    theirs = other[:row_count]
    arrived = []
    for k in range(1, blocks):
        piece = slice(k * row_count, (k + 1) * row_count)
        away = (keep[piece].astype(F32) + other[piece].astype(F32)).astype(BF16)
        m = block_order[k]
        arrived.append(lax.ppermute(away, "ctx", [(i, i ^ m) for i in range(n_ctx)]))
    while len(arrived) > 1:
        arrived = [(arrived[0].astype(F32) + arrived[1].astype(F32)).astype(BF16)] + arrived[2:]
    d_a, d_b, gain_sums = heads_back(
        tiles,
        tile,
        dq,
        [mine, theirs, arrived[0]],
        dlog,
        raw_a,
        raw_b,
        cos,
        sin,
        q_gain,
        k_gain,
        q_heads,
        k_heads,
    )
    gain_size = query_gain.shape[0]

    def gain_column(row):
        pieces = jnp.take(gain_sums[row].reshape(-1, gain_size), order, axis=0)
        return jnp.pad(pieces, ((0, 0), (0, block - gain_size))).reshape(-1, 1)

    lane = lax.broadcasted_iota(jnp.int32, (1, d_a.shape[1]), 1)
    extra_a = jnp.where(lane == q_width + n_head, gain_column(0), 0.0) + jnp.where(
        lane == q_width + n_head + 1, gain_column(1), 0.0
    )
    sent_a = (matmul(normed[:, other_cols], d_a, ((0,), (0,))) + extra_a[width // 2 :]).astype(BF16)
    kept_a = matmul(normed[:, own_cols], d_a, ((0,), (0,))) + extra_a[: width // 2]
    sum_a = ring.reduce((kept_a + ring.swap(sent_a).astype(F32)).astype(BF16))
    sum_b = ring.reduce(weight_grad(normed, d_b))
    grad_normed = matmul(d_a, weight_a, ((1,), (1,))) + matmul(d_b, weight_b, ((1,), (1,)))
    unit_in = tok[:rows].astype(F32) * scale_in[:rows]
    dtok = dmid + norm_back(tp_scatter(grad_normed, n_tp) * gain_in, unit_in, scale_in[:rows])
    dtok = jnp.concatenate(tp_gather(dtok.astype(BF16), n_tp))
    input_grad = leave(order, tiles, tile, dtok, F32, "leave_grad")

    sum_gate = jnp.concatenate([both[:, :chunk] for both in sums_gu], axis=1)
    sum_up = jnp.concatenate([both[:, chunk:] for both in sums_gu], axis=1)
    sum_down = jnp.concatenate(sums_d, axis=1).T
    mid_share = jnp.sum(sum_gate * gate_weight.astype(F32), axis=1) + jnp.sum(
        sum_up * up_weight.astype(F32), axis=1
    )
    in_share = (
        jnp.sum(sum_a[:, :q_width] * query_weight.astype(F32), axis=1)
        + jnp.sum(sum_b[:, :k_width] * key_matrix.astype(F32), axis=1)
        + jnp.sum(sum_b[:, k_width:] * value_matrix.astype(F32), axis=1)
        + jnp.sum(sum_a[:, q_width : q_width + n_head] * head_weight.astype(F32), axis=1)
    )
    small = jnp.stack(
        [
            in_share / norm_in.astype(F32),
            mid_share / norm_mid.astype(F32),
            sum_a[:, q_width + n_head],
            sum_a[:, q_width + n_head + 1],
        ]
    )
    small = tp_total(small, n_tp)
    return (
        output,
        input_grad,
        small[0],
        small[1],
        small[2, :gain_size],
        small[3, :gain_size],
        sum_a[:, :q_width],
        sum_b[:, :k_width],
        sum_b[:, k_width:],
        sum_a[:, q_width : q_width + n_head],
        sum_o.T,
        sum_gate,
        sum_up,
        sum_down,
    )


def solution(mesh):
    sizes = (mesh.shape["shard"], mesh.shape["ctx"], mesh.shape["tp"])
    split = ("shard", "ctx")
    rows = P(split, None)
    vector = P(split)
    weight = P(split, "tp")
    turned = P("tp", split)
    return jax.shard_map(
        functools.partial(per_device, sizes),
        mesh=mesh,
        in_specs=(rows, P("shard"), P("shard"), rows)
        + (vector,) * 4
        + (weight,) * 4
        + (turned, weight, weight, turned),
        out_specs=(rows, rows) + (vector,) * 4 + (weight,) * 4 + (turned, weight, weight, turned),
        check_vma=False,
    )
```

profile of v0, /device:TPU:0, one launch (start us, length us, event | category | flops | bytes accessed | tf_op | source)
XLA Modules:
  0.0 1266.9 jit_solution(13099755247933736426)
XLA Ops:
  175.2 9.7 make_heads.1
  242.2 41.0 %collective-permute-done.95 = bf16[128,1024]{0,1:T(8,128)(2,1)S(1)} collective-permute-done((bf16[128,1024]{0,1:T(8,128)(2,1)S(1)}, bf16[128,1024]{0,1:T(8,128)(2,1)S(1)}, u32[]{:S(2)}, u32[]{:S(2)}) %collective-permute-start.95) | collective-permute-done | bytes 262176 | tf_op jit(solution)/shard_map/ppermute | solution.py:62
  290.6 13.1 %collective-permute-done.97 = bf16[128,1024]{0,1:T(8,128)(2,1)S(1)} collective-permute-done((bf16[128,1024]{0,1:T(8,128)(2,1)S(1)}, bf16[128,1024]{0,1:T(8,128)(2,1)S(1)}, u32[]{:S(2)}, u32[]{:S(2)}) %collective-permute-start.97) | collective-permute-done | bytes 262176 | tf_op jit(solution)/shard_map/ppermute | solution.py:62
  351.6 26.2 %attend.1 = (f32[768,1024]{1,0:T(8,128)}, bf16[768,1024]{1,0:T(8,128)(2,1)S(1)}, f32[768,128]{1,0:T(8,128)S(1)}) custom-call(s32[72]{0:T(128)S(1)} %reshape.212.flags_ref, bf16[768,1024]{1,0:T(8,128)(2,1)S(1)} %get-tuple-element.41.refs_0_, f32[768,3072]{1,0:T(8,128)} %and_select_fusion.refs_1_, f32[768,128]{1,0:T(8,128)S(1)} %get-tuple-element.42.refs_2_, ...), custom_call_target="tpu_custom_call" | custom-call | flops 9663676416 | bytes 9437184 | tf_op jit(solution)/shard_map/attend/pallas_call | solution.py:400
  390.0 13.9 %collective-permute-done.125 = bf16[128,1024]{0,1:T(8,128)(2,1)S(1)} collective-permute-done((bf16[128,1024]{0,1:T(8,128)(2,1)S(1)}, bf16[128,1024]{0,1:T(8,128)(2,1)S(1)}, u32[]{:S(2)}, u32[]{:S(2)}) %collective-permute-start.125) | collective-permute-done | bytes 262176 | tf_op jit(solution)/shard_map/ppermute | solution.py:62
  408.8 9.1 collective-permute-done.126
  449.3 8.0 collective-permute-done.86
  505.5 14.1 %collective-permute-done.49 = bf16[384,2048]{1,0:T(8,128)(2,1)S(1)} collective-permute-done((bf16[384,2048]{1,0:T(8,128)(2,1)S(1)}, bf16[384,2048]{1,0:T(8,128)(2,1)S(1)}, u32[]{:S(2)}, u32[]{:S(2)}) %collective-permute-start.49) | collective-permute-done | bytes 1572896 | tf_op jit(solution)/shard_map/ppermute | solution.py:105
  519.6 9.6 fusion.45
  529.2 9.0 multiply_convert_fusion.6
  538.2 8.0 fusion.89
  546.2 10.7 fusion.44
  556.9 9.7 multiply_convert_fusion.4
  566.5 8.7 fusion.90
  575.2 10.0 fusion.42
  585.2 12.0 fusion.41
  626.8 9.6 fusion.43
  636.4 8.8 multiply_convert_fusion.2
  645.1 12.6 add_add_fusion
  702.7 25.6 %collective-permute-done.140 = bf16[384,2048]{1,0:T(8,128)(2,1)S(1)} collective-permute-done((bf16[384,2048]{1,0:T(8,128)(2,1)S(1)}, bf16[384,2048]{1,0:T(8,128)(2,1)S(1)}, u32[]{:S(2)}, u32[]{:S(2)}) %collective-permute-start.140) | collective-permute-done | bytes 1572896 | tf_op jit(solution)/shard_map/ppermute | solution.py:96
  783.5 46.9 %collective-permute-done.143 = bf16[384,2048]{1,0:T(8,128)(2,1)S(1)} collective-permute-done((bf16[384,2048]{1,0:T(8,128)(2,1)}, bf16[384,2048]{1,0:T(8,128)(2,1)S(1)}, u32[]{:S(2)}, u32[]{:S(2)}) %collective-permute-start.143) | collective-permute-done | bytes 1572896 | tf_op jit(solution)/shard_map/ppermute | solution.py:105
  837.5 59.2 %attend_back.1 = (f32[768,1024]{1,0:T(8,128)}, bf16[768,128]{1,0:T(8,128)(2,1)S(1)}, bf16[1536,1024]{1,0:T(8,128)(2,1)}, bf16[1536,1024]{1,0:T(8,128)(2,1)}) custom-call(s32[72]{0:T(128)S(1)} %reshape.212.flags_ref, bf16[768,1024]{1,0:T(8,128)(2,1)S(1)} %copy-done.10, f32[768,3072]{1,0:T(8,128)} %and_select_fusion.refs_1_, ...), custom_call_target="tpu_custom_call" | custom-call | flops 24159191040 | bytes 9437184 | tf_op jit(solution)/shard_map/attend_back/pallas_call | solution.py:509
  904.1 13.4 %collective-permute-start.144 = (bf16[1536,1024]{1,0:T(8,128)(2,1)}, bf16[1536,1024]{1,0:T(8,128)(2,1)S(1)}, u32[]{:S(2)}, u32[]{:S(2)}) collective-permute-start(bf16[1536,1024]{1,0:T(8,128)(2,1)} %get-tuple-element.57), channel_id=1, source_target_pairs={{0,2},{2,0},{4,6},{6,4},{1,3},{3,1},{5,7},{7,5},{8,10},{10,8},{12,... | collective-permute-start | bytes 9437192 | tf_op jit(solution)/shard_map/ppermute | solution.py:65
  923.4 32.0 %collective-permute-done.218 = bf16[128,1024]{0,1:T(8,128)(2,1)S(1)} collective-permute-done((bf16[128,1024]{0,1:T(8,128)(2,1)S(1)}, bf16[128,1024]{0,1:T(8,128)(2,1)S(1)}, u32[]{:S(2)}, u32[]{:S(2)}) %collective-permute-start.218) | collective-permute-done | bytes 262176 | tf_op jit(solution)/shard_map/ppermute | solution.py:62
  964.1 10.7 collective-permute-done.220
  1017.9 13.8 %collective-permute-done.190 = bf16[128,1024]{1,0:T(8,128)(2,1)S(1)} collective-permute-done((bf16[128,1024]{1,0:T(8,128)(2,1)S(1)}, bf16[128,1024]{1,0:T(8,128)(2,1)S(1)}, u32[]{:S(2)}, u32[]{:S(2)}) %collective-permute-start.190) | collective-permute-done | bytes 262176 | tf_op jit(solution)/shard_map/ppermute | solution.py:62
  1040.5 13.7 %collective-permute-done.192 = bf16[128,1024]{1,0:T(8,128)(2,1)S(1)} collective-permute-done((bf16[128,1024]{1,0:T(8,128)(2,1)S(1)}, bf16[128,1024]{1,0:T(8,128)(2,1)S(1)}, u32[]{:S(2)}, u32[]{:S(2)}) %collective-permute-start.192) | collective-permute-done | bytes 262176 | tf_op jit(solution)/shard_map/ppermute | solution.py:62
  1066.6 43.8 %collective-permute-done.194 = bf16[128,1024]{1,0:T(8,128)(2,1)S(1)} collective-permute-done((bf16[128,1024]{1,0:T(8,128)(2,1)S(1)}, bf16[128,1024]{1,0:T(8,128)(2,1)S(1)}, u32[]{:S(2)}, u32[]{:S(2)}) %collective-permute-start.194) | collective-permute-done | bytes 262176 | tf_op jit(solution)/shard_map/ppermute | solution.py:62
  1120.1 9.1 collective-permute-done.196
  1136.5 11.6 heads_back.1
  1148.1 8.2 fusion.91
  1237.4 21.3 %collective-permute-done.147 = bf16[384,2048]{1,0:T(8,128)(2,1)S(1)} collective-permute-done((bf16[384,2048]{1,0:T(8,128)(2,1)S(1)}, bf16[384,2048]{1,0:T(8,128)(2,1)S(1)}, u32[]{:S(2)}, u32[]{:S(2)}) %collective-permute-start.147) | collective-permute-done | bytes 1572896 | tf_op jit(solution)/shard_map/ppermute | solution.py:105
  (1058 shorter events, 710.5 us)
Async XLA Ops:
  6.5 57.4 %collective-permute-start = (bf16[128,1152]{1,0:T(8,128)(2,1)}, bf16[128,1152]{1,0:T(8,128)(2,1)}, u32[]{:S(2)}, u32[]{:S(2)}) collective-permute-start(bf16[128,1152]{1,0:T(8,128)(2,1)} %concatenate.165), channel_id=1, source_target_pairs={{0,8},{8,16},{16,24},{24,28},{28,20},{20,12},{12,4},{4,0},{2,6},{1... | collective-permute-start | bytes 884744 | tf_op jit(solution)/shard_map/ppermute | solution.py:62
  9.5 124.5 %collective-permute-start.7 = (bf16[128,1152]{1,0:T(8,128)(2,1)}, bf16[128,1152]{1,0:T(8,128)(2,1)}, u32[]{:S(2)}, u32[]{:S(2)}) collective-permute-start(bf16[128,1152]{1,0:T(8,128)(2,1)} %concatenate.165), channel_id=1, source_target_pairs={{0,2},{2,0},{4,6},{6,4},{1,3},{3,1},{5,7},{7,5},{8,10},{10,8},{12,... | collective-permute-start | bytes 884744 | tf_op jit(solution)/shard_map/ppermute | solution.py:65
  12.8 47.7 %collective-permute-start.15 = (bf16[128,1024]{1,0:T(8,128)(2,1)}, bf16[128,1024]{1,0:T(8,128)(2,1)}, u32[]{:S(2)}, u32[]{:S(2)}) collective-permute-start(bf16[128,1024]{1,0:T(8,128)(2,1)} %get-tuple-element.159), channel_id=1, source_target_pairs={{0,8},{8,16},{16,24},{24,28},{28,20},{20,12},{12,4},{4,0},{2,6},{1... | collective-permute-start | bytes 786440 | tf_op jit(solution)/shard_map/ppermute | solution.py:62
  14.4 95.2 %collective-permute-start.22 = (bf16[128,1024]{1,0:T(8,128)(2,1)}, bf16[128,1024]{1,0:T(8,128)(2,1)}, u32[]{:S(2)}, u32[]{:S(2)}) collective-permute-start(bf16[128,1024]{1,0:T(8,128)(2,1)} %get-tuple-element.159), channel_id=1, source_target_pairs={{0,2},{2,0},{4,6},{6,4},{1,3},{3,1},{5,7},{7,5},{8,10},{10,8},{12,... | collective-permute-start | bytes 786440 | tf_op jit(solution)/shard_map/ppermute | solution.py:65
  134.0 65.0 %collective-permute-start.40 = (bf16[128,1024]{0,1:T(8,128)(2,1)}, bf16[128,1024]{0,1:T(8,128)(2,1)}, u32[]{:S(2)}, u32[]{:S(2)}) collective-permute-start(bf16[128,1024]{0,1:T(8,128)(2,1)} %bitcast.10), channel_id=1, source_target_pairs={{0,2},{2,0},{4,6},{6,4},{1,3},{3,1},{5,7},{7,5},{8,10},{10,8},{12,... | collective-permute-start | bytes 786440 | tf_op jit(solution)/shard_map/ppermute | solution.py:65
  135.6 65.6 %collective-permute-start.41 = (bf16[128,1024]{0,1:T(8,128)(2,1)}, bf16[128,1024]{0,1:T(8,128)(2,1)}, u32[]{:S(2)}, u32[]{:S(2)}) collective-permute-start(bf16[128,1024]{0,1:T(8,128)(2,1)} %collective-permute-done.33), channel_id=1, source_target_pairs={{0,2},{2,0},{4,6},{6,4},{1,3},{3,1},{5,7},{7,5},{8,10},{10,8},{12,... | collective-permute-start | bytes 786440 | tf_op jit(solution)/shard_map/ppermute | solution.py:65
  187.0 134.0 %collective-permute-start.57 = (bf16[128,2048]{1,0:T(8,128)(2,1)S(1)}, bf16[128,2048]{1,0:T(8,128)(2,1)S(1)}, u32[]{:S(2)}, u32[]{:S(2)}) collective-permute-start(bf16[128,2048]{1,0:T(8,128)(2,1)S(1)} %copy-done.35), channel_id=1, source_target_pairs={{0,2},{2,0},{4,6},{6,4},{1,3},{3,1},{5,7},{7,5},{8,10},{10,8},{12,... | collective-permute-start | bytes 1572872 | tf_op jit(solution)/shard_map/ppermute | solution.py:65
  229.0 93.5 %collective-permute-start.30 = (bf16[768,1024]{1,0:T(8,128)(2,1)S(1)}, bf16[768,1024]{1,0:T(8,128)(2,1)S(1)}, u32[]{:S(2)}, u32[]{:S(2)}) collective-permute-start(bf16[768,1024]{1,0:T(8,128)(2,1)S(1)} %get-tuple-element.43.refs_3_.refs_6_), channel_id=1, source_target_pairs={{0,4},{2,6},{4,0},{6,2},{1,5},{3,7},{5,1},{7,3},{8,12},{10,14},{12... | collective-permute-start | bytes 4718600 | tf_op jit(solution)/shard_map/ppermute | solution.py:678
  347.5 110.6 %collective-permute-start.87 = (bf16[128,2048]{1,0:T(8,128)(2,1)}, bf16[128,2048]{1,0:T(8,128)(2,1)}, u32[]{:S(2)}, u32[]{:S(2)}) collective-permute-start(bf16[128,2048]{1,0:T(8,128)(2,1)} %pad_maximum_fusion.25), channel_id=1, source_target_pairs={{0,2},{2,0},{4,6},{6,4},{1,3},{3,1},{5,7},{7,5},{8,10},{10,8},{12,... | collective-permute-start | bytes 1572872 | tf_op jit(solution)/shard_map/ppermute | solution.py:65
  348.7 57.9 %collective-permute-start.109 = (bf16[128,1024]{0,1:T(8,128)(2,1)}, bf16[128,1024]{0,1:T(8,128)(2,1)S(1)}, u32[]{:S(2)}, u32[]{:S(2)}) collective-permute-start(bf16[128,1024]{0,1:T(8,128)(2,1)} %collective-permute-done.101), channel_id=1, source_target_pairs={{0,2},{2,0},{4,6},{6,4},{1,3},{3,1},{5,7},{7,5},{8,10},{10,8},{12,... | collective-permute-start | bytes 786440 | tf_op jit(solution)/shard_map/ppermute | solution.py:65
  491.8 128.9 %collective-permute-start.117 = (bf16[128,2048]{1,0:T(8,128)(2,1)S(1)}, bf16[128,2048]{1,0:T(8,128)(2,1)S(1)}, u32[]{:S(2)}, u32[]{:S(2)}) collective-permute-start(bf16[128,2048]{1,0:T(8,128)(2,1)S(1)} %copy-done.33), channel_id=1, source_target_pairs={{0,2},{2,0},{4,6},{6,4},{1,3},{3,1},{5,7},{7,5},{8,10},{10,8},{12,... | collective-permute-start | bytes 1572872 | tf_op jit(solution)/shard_map/ppermute | solution.py:65
  495.4 125.6 %collective-permute-start.118 = (bf16[128,2048]{1,0:T(8,128)(2,1)S(1)}, bf16[128,2048]{1,0:T(8,128)(2,1)S(1)}, u32[]{:S(2)}, u32[]{:S(2)}) collective-permute-start(bf16[128,2048]{1,0:T(8,128)(2,1)S(1)} %collective-permute-done.110), channel_id=1, source_target_pairs={{0,2},{2,0},{4,6},{6,4},{1,3},{3,1},{5,7},{7,5},{8,10},{10,8},{12,... | collective-permute-start | bytes 1572872 | tf_op jit(solution)/shard_map/ppermute | solution.py:65
  497.1 124.3 %collective-permute-start.119 = (bf16[128,2048]{1,0:T(8,128)(2,1)S(1)}, bf16[128,2048]{1,0:T(8,128)(2,1)S(1)}, u32[]{:S(2)}, u32[]{:S(2)}) collective-permute-start(bf16[128,2048]{1,0:T(8,128)(2,1)S(1)} %collective-permute-done.111), channel_id=1, source_target_pairs={{0,2},{2,0},{4,6},{6,4},{1,3},{3,1},{5,7},{7,5},{8,10},{10,8},{12,... | collective-permute-start | bytes 1572872 | tf_op jit(solution)/shard_map/ppermute | solution.py:65
  504.6 117.1 %collective-permute-start.120 = (bf16[128,2048]{1,0:T(8,128)(2,1)S(1)}, bf16[128,2048]{1,0:T(8,128)(2,1)S(1)}, u32[]{:S(2)}, u32[]{:S(2)}) collective-permute-start(bf16[128,2048]{1,0:T(8,128)(2,1)S(1)} %collective-permute-done.112), channel_id=1, source_target_pairs={{0,2},{2,0},{4,6},{6,4},{1,3},{3,1},{5,7},{7,5},{8,10},{10,8},{12,... | collective-permute-start | bytes 1572872 | tf_op jit(solution)/shard_map/ppermute | solution.py:65
  519.6 91.6 %collective-permute-start.115 = (bf16[128,2048]{1,0:T(8,128)(2,1)S(1)}, bf16[128,2048]{1,0:T(8,128)(2,1)S(1)}, u32[]{:S(2)}, u32[]{:S(2)}) collective-permute-start(bf16[128,2048]{1,0:T(8,128)(2,1)S(1)} %collective-permute-done.114), channel_id=1, source_target_pairs={{0,8},{8,16},{16,24},{24,28},{28,20},{20,12},{12,4},{4,0},{2,6},{1... | collective-permute-start | bytes 1572872 | tf_op jit(solution)/shard_map/ppermute | solution.py:62
  621.0 147.1 %collective-permute-start.172 = (bf16[1024,2048]{1,0:T(8,128)(2,1)}, bf16[1024,2048]{1,0:T(8,128)(2,1)}, u32[]{:S(2)}, u32[]{:S(2)}) collective-permute-start(bf16[1024,2048]{1,0:T(8,128)(2,1)} %convolution_convert_fusion.1), channel_id=1, source_target_pairs={{0,2},{2,0},{4,6},{6,4},{1,3},{3,1},{5,7},{7,5},{8,10},{10,8},{12,... | collective-permute-start | bytes 12582920 | tf_op jit(solution)/shard_map/ppermute | solution.py:65
  621.4 46.0 %collective-permute-start.205 = (bf16[1024,1024]{0,1:T(8,128)(2,1)}, bf16[1024,1024]{0,1:T(8,128)(2,1)}, u32[]{:S(2)}, u32[]{:S(2)}) collective-permute-start(bf16[1024,1024]{0,1:T(8,128)(2,1)} %convolution_convert_fusion.4), channel_id=1, source_target_pairs={{0,2},{2,0},{4,6},{6,4},{1,3},{3,1},{5,7},{7,5},{8,10},{10,8},{12,... | collective-permute-start | bytes 6291464 | tf_op jit(solution)/shard_map/ppermute | solution.py:65
  623.7 47.6 %collective-permute-start.197 = (bf16[1024,1024]{0,1:T(8,128)(2,1)}, bf16[1024,1024]{0,1:T(8,128)(2,1)}, u32[]{:S(2)}, u32[]{:S(2)}) collective-permute-start(bf16[1024,1024]{0,1:T(8,128)(2,1)} %convolution_convert_fusion.5), channel_id=1, source_target_pairs={{0,2},{2,0},{4,6},{6,4},{1,3},{3,1},{5,7},{7,5},{8,10},{10,8},{12,... | collective-permute-start | bytes 6291464 | tf_op jit(solution)/shard_map/ppermute | solution.py:65
  678.8 49.4 %collective-permute-start.140 = (bf16[384,2048]{1,0:T(8,128)(2,1)S(1)}, bf16[384,2048]{1,0:T(8,128)(2,1)S(1)}, u32[]{:S(2)}, u32[]{:S(2)}) collective-permute-start(bf16[384,2048]{1,0:T(8,128)(2,1)S(1)} %slice.906), channel_id=1, source_target_pairs={{0,1},{1,0},{2,3},{3,2},{4,5},{5,4},{6,7},{7,6},{8,9},{9,8},{10,11... | collective-permute-start | bytes 4718600 | tf_op jit(solution)/shard_map/ppermute | solution.py:96
  698.1 77.4 %collective-permute-start.164 = (bf16[1024,2048]{1,0:T(8,128)(2,1)}, bf16[1024,2048]{1,0:T(8,128)(2,1)}, u32[]{:S(2)}, u32[]{:S(2)}) collective-permute-start(bf16[1024,2048]{1,0:T(8,128)(2,1)} %convolution_convert_fusion.2), channel_id=1, source_target_pairs={{0,2},{2,0},{4,6},{6,4},{1,3},{3,1},{5,7},{7,5},{8,10},{10,8},{12,... | collective-permute-start | bytes 12582920 | tf_op jit(solution)/shard_map/ppermute | solution.py:65
  732.3 252.1 %collective-permute-start.180 = (bf16[1024,2048]{1,0:T(8,128)(2,1)}, bf16[1024,2048]{1,0:T(8,128)(2,1)}, u32[]{:S(2)}, u32[]{:S(2)}) collective-permute-start(bf16[1024,2048]{1,0:T(8,128)(2,1)} %convolution_convert_fusion), channel_id=1, source_target_pairs={{0,2},{2,0},{4,6},{6,4},{1,3},{3,1},{5,7},{7,5},{8,10},{10,8},{12,... | collective-permute-start | bytes 12582920 | tf_op jit(solution)/shard_map/ppermute | solution.py:65
  762.9 133.8 %collective-permute-start.141 = (bf16[384,2048]{1,0:T(8,128)(2,1)}, bf16[384,2048]{1,0:T(8,128)(2,1)}, u32[]{:S(2)}, u32[]{:S(2)}) collective-permute-start(bf16[384,2048]{1,0:T(8,128)(2,1)} %get-tuple-element.139), channel_id=1, source_target_pairs={{0,1},{1,0},{2,3},{3,2},{4,5},{5,4},{6,7},{7,6},{8,9},{9,8},{10,11... | collective-permute-start | bytes 4718600 | tf_op jit(solution)/shard_map/ppermute | solution.py:105
  766.5 63.9 %collective-permute-start.143 = (bf16[384,2048]{1,0:T(8,128)(2,1)}, bf16[384,2048]{1,0:T(8,128)(2,1)S(1)}, u32[]{:S(2)}, u32[]{:S(2)}) collective-permute-start(bf16[384,2048]{1,0:T(8,128)(2,1)} %get-tuple-element.122), channel_id=1, source_target_pairs={{0,1},{1,0},{2,3},{3,2},{4,5},{5,4},{6,7},{7,6},{8,9},{9,8},{10,11... | collective-permute-start | bytes 4718600 | tf_op jit(solution)/shard_map/ppermute | solution.py:105
  768.2 149.4 %collective-permute-start.217 = (bf16[128,1024]{0,1:T(8,128)(2,1)S(1)}, bf16[128,1024]{0,1:T(8,128)(2,1)S(1)}, u32[]{:S(2)}, u32[]{:S(2)}) collective-permute-start(bf16[128,1024]{0,1:T(8,128)(2,1)S(1)} %add_convert_fusion.36), channel_id=1, source_target_pairs={{0,8},{8,16},{16,24},{24,28},{28,20},{20,12},{12,4},{4,0},{2,6},{1... | collective-permute-start | bytes 786440 | tf_op jit(solution)/shard_map/ppermute | solution.py:62
  775.5 180.9 %collective-permute-start.173 = (bf16[128,2048]{1,0:T(8,128)(2,1)}, bf16[128,2048]{1,0:T(8,128)(2,1)}, u32[]{:S(2)}, u32[]{:S(2)}) collective-permute-start(bf16[128,2048]{1,0:T(8,128)(2,1)} %slice.641), channel_id=1, source_target_pairs={{0,8},{8,16},{16,24},{24,28},{28,20},{20,12},{12,4},{4,0},{2,6},{1... | collective-permute-start | bytes 1572872 | tf_op jit(solution)/shard_map/ppermute | solution.py:62
  830.4 133.5 %collective-permute-start.165 = (bf16[128,2048]{1,0:T(8,128)(2,1)}, bf16[128,2048]{1,0:T(8,128)(2,1)S(1)}, u32[]{:S(2)}, u32[]{:S(2)}) collective-permute-start(bf16[128,2048]{1,0:T(8,128)(2,1)} %slice.632), channel_id=1, source_target_pairs={{0,8},{8,16},{16,24},{24,28},{28,20},{20,12},{12,4},{4,0},{2,6},{1... | collective-permute-start | bytes 1572872 | tf_op jit(solution)/shard_map/ppermute | solution.py:62
  904.1 151.1 %collective-permute-start.144 = (bf16[1536,1024]{1,0:T(8,128)(2,1)}, bf16[1536,1024]{1,0:T(8,128)(2,1)S(1)}, u32[]{:S(2)}, u32[]{:S(2)}) collective-permute-start(bf16[1536,1024]{1,0:T(8,128)(2,1)} %get-tuple-element.57), channel_id=1, source_target_pairs={{0,2},{2,0},{4,6},{6,4},{1,3},{3,1},{5,7},{7,5},{8,10},{10,8},{12,... | collective-permute-start | bytes 9437192 | tf_op jit(solution)/shard_map/ppermute | solution.py:65
  955.3 57.0 %collective-permute-start.189 = (bf16[1024,1024]{1,0:T(8,128)(2,1)}, bf16[1024,1024]{1,0:T(8,128)(2,1)}, u32[]{:S(2)}, u32[]{:S(2)}) collective-permute-start(bf16[1024,1024]{1,0:T(8,128)(2,1)} %convolution_convert_fusion.6), channel_id=1, source_target_pairs={{0,2},{2,0},{4,6},{6,4},{1,3},{3,1},{5,7},{7,5},{8,10},{10,8},{12,... | collective-permute-start | bytes 6291464 | tf_op jit(solution)/shard_map/ppermute | solution.py:65
  1054.5 56.0 %collective-permute-start.179 = (bf16[128,2048]{1,0:T(8,128)(2,1)S(1)}, bf16[128,2048]{1,0:T(8,128)(2,1)S(1)}, u32[]{:S(2)}, u32[]{:S(2)}) collective-permute-start(bf16[128,2048]{1,0:T(8,128)(2,1)S(1)} %add_convert_fusion.15), channel_id=1, source_target_pairs={{0,8},{8,16},{16,24},{24,28},{28,20},{20,12},{12,4},{4,0},{2,6},{1... | collective-permute-start | bytes 1572872 | tf_op jit(solution)/shard_map/ppermute | solution.py:62
  1054.7 57.0 %collective-permute-start.171 = (bf16[128,2048]{1,0:T(8,128)(2,1)S(1)}, bf16[128,2048]{1,0:T(8,128)(2,1)S(1)}, u32[]{:S(2)}, u32[]{:S(2)}) collective-permute-start(bf16[128,2048]{1,0:T(8,128)(2,1)S(1)} %add_convert_fusion.21), channel_id=1, source_target_pairs={{0,8},{8,16},{16,24},{24,28},{28,20},{20,12},{12,4},{4,0},{2,6},{1... | collective-permute-start | bytes 1572872 | tf_op jit(solution)/shard_map/ppermute | solution.py:62
  1057.1 77.5 %collective-permute-start.145 = (bf16[768,1024]{1,0:T(8,128)(2,1)}, bf16[768,1024]{1,0:T(8,128)(2,1)}, u32[]{:S(2)}, u32[]{:S(2)}) collective-permute-start(bf16[768,1024]{1,0:T(8,128)(2,1)} %add_convert_fusion.8), channel_id=1, source_target_pairs={{0,4},{2,6},{4,0},{6,2},{1,5},{3,7},{5,1},{7,3},{8,12},{10,14},{12... | collective-permute-start | bytes 4718600 | tf_op jit(solution)/shard_map/ppermute | solution.py:742
  1066.5 49.5 %collective-permute-start.185 = (bf16[128,2048]{1,0:T(8,128)(2,1)S(1)}, bf16[128,2048]{1,0:T(8,128)(2,1)S(1)}, u32[]{:S(2)}, u32[]{:S(2)}) collective-permute-start(bf16[128,2048]{1,0:T(8,128)(2,1)S(1)} %add_convert_fusion.11), channel_id=1, source_target_pairs={{0,8},{8,16},{16,24},{24,28},{28,20},{20,12},{12,4},{4,0},{2,6},{1... | collective-permute-start | bytes 1572872 | tf_op jit(solution)/shard_map/ppermute | solution.py:62
  (326 other events, 5891.8 us)
where the time goes:
time: 1280 us; the launch traced here: 1270 us
  waiting for transfers between devices  552 us (43%)
  matrix products  236 us (18%)
  local copies, waits for them, and re-layouts  161 us (13%)
  starting transfers between devices  133 us (10%)
  Pallas kernels  122 us (10%)
  other arithmetic  59.1 us (5%)
    ppermute x126, waiting for transfers between devices, hop(): return lax.ppermute(value, RING_AXES, self.hops)  433 us
    dot_general x36, matrix products, matmul(): return lax.dot_general(a, b, (dims, ((), ())), preferred_element_type=F32)  236 us
    unnamed x416, local copies, waits for them, and re-layouts  120 us
    ppermute x4, waiting for transfers between devices, tp_gather(): lax.ppermute(block, 'tp', [(i, (i - j) % n_tp) for i in range(n_tp)])  82.2 us
    ppermute x126, starting transfers between devices, hop(): return lax.ppermute(value, RING_AXES, self.hops)  73.5 us
    pallas_call x1, Pallas kernels, attend_back(): pl.pallas_call(functools.partial(attend_back_kernel, q_heads, k_heads, bl...  59.2 us
    ppermute x82, starting transfers between devices, swap(): return lax.ppermute(value, 'ctx', self.swaps)  44.3 us
    ppermute x4, waiting for transfers between devices, tp_scatter(): lax.ppermute(sent, 'tp', [(i, (i + j) % n_tp) for i in range(n_tp)])  31.3 us
  transfers between devices with their start and end apart: 221, of which 96 were waited for; matrix products, arithmetic and copies ran while one was open for 35% of the time, Pallas kernels for 10%

commit v1 on v0

v1 whole, which is shorter than its diff:
```python
import functools

import jax
import jax.numpy as jnp
import numpy as np
from jax import lax
from jax.experimental import pallas as pl
from jax.experimental.pallas import tpu as pltpu
from jax.sharding import PartitionSpec as P

HEAD = 128
LANES = 128
EPS = 1e-06
THETA = 1000000.0
MASKED = -1e30
LOG2E = 1.4426950408889634
SCALE = HEAD ** (-0.5)
KEY_TILE = 256
CHUNKS = 3
COLUMN_TILE = 256
ROW_TILE = 128
FORWARD_HEADS = 4
BACKWARD_HEADS = 2
GAINS = 64

F32 = jnp.float32
BF16 = jnp.bfloat16


def matmul(a, b, dims=((1,), (0,))):
    return lax.dot_general(a, b, (dims, ((), ())), preferred_element_type=F32)


def ring_tables(n_shard, n_ctx):
    path = []
    for x in range(n_ctx // 2):
        column = range(n_shard) if x % 2 == 0 else reversed(range(n_shard))
        path += [(z, x) for z in column]
    length = len(path)

    def device(place, core):
        z, x = path[place % length]
        return z * n_ctx + x * 2 + core

    hops = [(device(r, 0), device(r + 1, 0)) for r in range(length)]
    hops += [(device(r, 1), device(r - 1, 1)) for r in range(length)]
    order = np.zeros((n_shard * n_ctx, 2 * length), np.int32)
    for r in range(length):
        for core in (0, 1):
            back = -1 if core == 0 else 1
            order[device(r, core), 0::2] = [device(r + back * s, core) for s in range(length)]
            order[device(r, core), 1::2] = [device(r - back * s, 1 - core) for s in range(length)]
    return hops, order, length


def hold(value, *others):
    others = [other for other in others if other is not None]
    return lax.optimization_barrier((value, *others))[0] if others else value


class Ring:
    def __init__(self, n_shard, n_ctx):
        self.hops, self.order, self.length = ring_tables(n_shard, n_ctx)
        self.swaps = [(i, i ^ 1) for i in range(n_ctx)]

    def hop(self, value):
        return lax.ppermute(value, ("shard", "ctx"), self.hops)

    def swap(self, value):
        return lax.ppermute(value, "ctx", self.swaps)


class Gather:
    def __init__(self, ring, block):
        self.ring = ring
        self.last = block
        self.pieces = [block, ring.swap(block)]

    def step(self, *others):
        if len(self.pieces) < 2 * self.ring.length:
            self.last = self.ring.hop(hold(self.last, *others))
            self.pieces += [self.last, self.ring.swap(self.last)]
        return self.last


class Reduce:
    def __init__(self, ring, kept, sent):
        self.ring = ring
        self.rows = kept.shape[0] // ring.length
        self.kept = kept
        self.other = ring.swap(sent)
        self.place = 1
        self.total = self.own().astype(BF16)

    def own(self):
        first = (self.place % self.ring.length) * self.rows
        here = slice(first, first + self.rows)
        return self.kept[here].astype(F32) + self.other[here].astype(F32)

    def step(self, *others):
        if self.place < self.ring.length:
            self.place += 1
            total = self.ring.hop(hold(self.total, *others)).astype(F32) + self.own()
            self.total = total if self.place == self.ring.length else total.astype(BF16)
        return self.total

    def finish(self):
        while self.place < self.ring.length:
            self.step()
        return self.total


def tp_send(sent, rows, n_tp):
    return [
        lax.ppermute(
            sent[(j - 1) * rows : j * rows], "tp", [(i, (i + j) % n_tp) for i in range(n_tp)]
        )
        for j in range(1, n_tp)
    ]


def tp_gather(block, n_tp):
    blocks = [block]
    for j in range(1, n_tp):
        blocks.append(lax.ppermute(block, "tp", [(i, (i - j) % n_tp) for i in range(n_tp)]))
    return blocks


def tp_total(value, n_tp):
    total = value
    for j in range(1, n_tp):
        total = total + lax.ppermute(value, "tp", [(i, (i + j) % n_tp) for i in range(n_tp)])
    return total


def row_tile(rows):
    return next(tile for tile in (128, 96, 64, 48, 32, 16) if rows % tile == 0)


def params(mib=56):
    return pltpu.CompilerParams(vmem_limit_bytes=mib << 20)


def cost(flops, moved, transcendentals=0):
    return pl.CostEstimate(flops=flops, bytes_accessed=moved, transcendentals=transcendentals)


def fixed(shape):
    return pl.BlockSpec(shape, lambda *_: (0,) * len(shape), pipeline_mode=pl.Buffered(1))


def shaped(shape, dtype):
    return jax.ShapeDtypeStruct(shape, dtype)


def enter_kernel(order_ref, rows_ref, tok_ref, cot_ref, tok_out, cot_out, scale_out):
    value = tok_ref[...].astype(F32)
    scale = lax.rsqrt(jnp.mean(value * value, axis=-1, keepdims=True) + EPS)
    scale_out[...] = jnp.broadcast_to(scale, scale_out.shape)
    for j in range(tok_ref.shape[1] // LANES):
        source = pl.multiple_of(order_ref[j] * LANES, LANES)
        here = slice(j * LANES, (j + 1) * LANES)
        tok_out[:, here] = tok_ref[:, pl.ds(source, LANES)]
        cot_out[:, here] = cot_ref[:, pl.ds(source, LANES)]


def enter(order, tiles, tile, tokens, cotangent):
    rows, width = tokens.shape
    block = pl.BlockSpec((tile, width), lambda i, order, tiles: (tiles[i], 0))
    out = pl.BlockSpec((tile, width), lambda i, order, tiles: (i, 0))
    return pl.pallas_call(
        enter_kernel,
        grid_spec=pltpu.PrefetchScalarGridSpec(
            num_scalar_prefetch=2,
            grid=(rows // tile,),
            in_specs=[block, block],
            out_specs=[out, out, pl.BlockSpec((tile, LANES), lambda i, order, tiles: (i, 0))],
        ),
        out_shape=[
            shaped((rows, width), BF16),
            shaped((rows, width), BF16),
            shaped((rows, LANES), F32),
        ],
        compiler_params=params(),
        cost_estimate=cost(rows * width * 4, rows * width * 8),
        name="enter",
    )(order, tiles, tokens, cotangent)


def leave_kernel(parts, order_ref, tiles_ref, *refs):
    out_ref = refs[parts]
    per = pl.num_programs(0) // parts
    for k in range(parts):

        @pl.when(pl.program_id(0) // per == k)
        def _():
            for j in range(out_ref.shape[1] // LANES):
                target = pl.multiple_of(order_ref[j] * LANES, LANES)
                out_ref[:, pl.ds(target, LANES)] = refs[k][
                    :, j * LANES : (j + 1) * LANES
                ].astype(out_ref.dtype)


def leave(order, tiles, tile, parts, dtype, name):
    rows, width = parts[0].shape
    per = rows // tile
    total = rows * len(parts)

    def part(k):
        return pl.BlockSpec(
            (tile, width), lambda i, order, tiles: (jnp.clip(i - k * per, 0, per - 1), 0)
        )

    return pl.pallas_call(
        functools.partial(leave_kernel, len(parts)),
        grid_spec=pltpu.PrefetchScalarGridSpec(
            num_scalar_prefetch=2,
            grid=(total // tile,),
            in_specs=[part(k) for k in range(len(parts))],
            out_specs=pl.BlockSpec((tile, width), lambda i, order, tiles: (tiles[i], 0)),
        ),
        out_shape=shaped((total, width), dtype),
        compiler_params=params(),
        cost_estimate=cost(0, total * width * 6),
        name=name,
    )(order, tiles, *parts)


def gains_kernel(order_ref, *refs):
    pieces, (wide_out, head_out) = refs[:-2], refs[-2:]
    size = HEAD // len(pieces)
    total = jnp.zeros((8, HEAD), F32)
    for j, piece in enumerate(pieces):
        turned = jnp.transpose(piece[...].astype(F32))[GAINS : GAINS + 8]
        wide_out[:, j * LANES : (j + 1) * LANES] = turned
        total += pltpu.roll(turned, order_ref[j] * size, 1)
    head_out[...] = total


def gather_gains(order, pieces, q_width):
    count = len(pieces)
    block = pieces[0].shape[0]
    spec = pl.BlockSpec((block, LANES), lambda i, order: (0, q_width // LANES))
    return pl.pallas_call(
        gains_kernel,
        grid_spec=pltpu.PrefetchScalarGridSpec(
            num_scalar_prefetch=1,
            grid=(1,),
            in_specs=[spec] * count,
            out_specs=[
                pl.BlockSpec((8, block * count), lambda i, order: (0, 0)),
                pl.BlockSpec((8, HEAD), lambda i, order: (0, 0)),
            ],
        ),
        out_shape=[shaped((8, block * count), F32), shaped((8, HEAD), F32)],
        compiler_params=params(),
        cost_estimate=cost(0, block * count * LANES * 2),
        name="gather_gains",
    )(order, *pieces)


def turn(value, cos, sin):
    return value * cos + pltpu.roll(value, HEAD // 2, 1) * sin


def project_kernel(q_heads, k_heads, count, tiles_ref, *refs):
    tok_ref, scale_ref, wide_ref, head_ref, cos_ref, sin_ref = refs[:6]
    a_refs, b_refs = refs[6 : 6 + count], refs[6 + count : 6 + 2 * count]
    normed_out, a_out, b_out, q_out, kv_out, sg_out = refs[6 + 2 * count :]
    cos, sin = cos_ref[...], sin_ref[...]
    normed = (tok_ref[...].astype(F32) * scale_ref[:, :1] * wide_ref[0:1, :]).astype(BF16)
    normed_out[...] = normed

    def rotated(value, gain):
        scale = lax.rsqrt(jnp.mean(value * value, axis=-1, keepdims=True) + EPS)
        return turn(value * scale * gain, cos, sin).astype(BF16)

    def product(refs, here):
        return matmul(normed_out[...], jnp.concatenate([ref[:, here] for ref in refs], axis=0))

    q_width, k_width = q_heads * HEAD, k_heads * HEAD
    q_tile, k_tile = min(COLUMN_TILE, q_width), min(COLUMN_TILE, k_width)

    @pl.loop(0, q_width // q_tile, unroll=True)
    def _(i):
        here = pl.ds(pl.multiple_of(i * q_tile, q_tile), q_tile)
        value = product(a_refs, here)
        a_out[:, here] = value
        q_out[:, here] = jnp.concatenate(
            [
                rotated(value[:, h * HEAD : (h + 1) * HEAD], head_ref[2:3, :])
                for h in range(q_tile // HEAD)
            ],
            axis=1,
        )

    tail = slice(q_width, q_width + LANES)
    value = product(a_refs, tail)
    a_out[:, tail] = value
    sg_out[...] = jax.nn.sigmoid(value)

    @pl.loop(0, k_width // k_tile, unroll=True)
    def _(i):
        here = pl.ds(pl.multiple_of(i * k_tile, k_tile), k_tile)
        value = product(b_refs, here)
        b_out[:, here] = value
        kv_out[:, here] = jnp.concatenate(
            [
                rotated(value[:, h * HEAD : (h + 1) * HEAD], head_ref[3:4, :])
                for h in range(k_tile // HEAD)
            ],
            axis=1,
        )

    @pl.loop(0, k_width // k_tile, unroll=True)
    def _(i):
        here = pl.ds(pl.multiple_of(k_width + i * k_tile, k_tile), k_tile)
        value = product(b_refs, here)
        b_out[:, here] = value
        kv_out[:, here] = value.astype(BF16)


def project(tiles, tile, tok, scale, wide, head, cos, sin, pieces_a, pieces_b, q_heads, k_heads):
    rows, width = tok.shape
    count = len(pieces_a)
    a_width, b_width = pieces_a[0].shape[1], pieces_b[0].shape[1]

    def at(width):
        return pl.BlockSpec((tile, width), lambda i, tiles: (i, 0))

    return pl.pallas_call(
        functools.partial(project_kernel, q_heads, k_heads, count),
        grid_spec=pltpu.PrefetchScalarGridSpec(
            num_scalar_prefetch=1,
            grid=(rows // tile,),
            in_specs=[at(width), at(LANES), fixed(wide.shape), fixed(head.shape), at(HEAD), at(HEAD)]
            + [fixed(piece.shape) for piece in pieces_a + pieces_b],
            out_specs=[
                at(width),
                at(a_width),
                at(b_width),
                at(q_heads * HEAD),
                pl.BlockSpec((tile, 2 * k_heads * HEAD), lambda i, tiles: (tiles[i], 0)),
                at(LANES),
            ],
        ),
        out_shape=[
            shaped((rows, width), BF16),
            shaped((rows, a_width), F32),
            shaped((rows, b_width), F32),
            shaped((rows, q_heads * HEAD), BF16),
            shaped((rows, 2 * k_heads * HEAD), BF16),
            shaped((rows, LANES), F32),
        ],
        compiler_params=params(),
        cost_estimate=cost(
            2 * rows * width * (a_width + b_width), width * (a_width + b_width) * 2 + rows * width * 16
        ),
        name="project",
    )(tiles, tok, scale, wide, head, cos, sin, *pieces_a, *pieces_b)


def spread_kernel(terms, count, rows, has_start, split, *refs):
    used = 0
    groups = []
    for width, _ in terms:
        groups.append((refs[used], refs[used + 1 : used + 1 + count]))
        used += 1 + count
    start_ref = None
    if has_start:
        start_ref = refs[used]
        used += 1
    outs = 2 if split else 1
    out_refs, scratch = refs[used : used + outs], refs[used + outs :]
    bufs, sem = scratch[:-1], scratch[-1]
    step = pl.program_id(0)
    block = groups[0][1][0].shape[0]

    def copies(s):
        slot = s % 2
        found = []
        for t, (width, offset) in enumerate(terms):
            for k in range(2):
                found.append(
                    pltpu.make_async_copy(
                        groups[t][1][2 * s + k].at[:, pl.ds(offset, width)],
                        bufs[t].at[slot, pl.ds(k * block, block)],
                        sem.at[slot, 2 * t + k],
                    )
                )
        return found

    for s in range(count // 2):

        @pl.when(step == s)
        def _():
            if s == 0:
                for copy in copies(0):
                    copy.start()
            if s + 1 < count // 2:
                for copy in copies(s + 1):
                    copy.start()
            for copy in copies(s):
                copy.wait()

    slot = lax.rem(step, 2)
    total = None
    for t in range(len(terms)):
        part = matmul(groups[t][0][...], bufs[t][slot], ((1,), (1,)))
        total = part if total is None else total + part
    if has_start:
        total = total + start_ref[...]
    if split:
        out_refs[0][...] = total[:rows]
        out_refs[1][...] = total[rows:].astype(BF16)
    else:
        out_refs[0][...] = total


def spread(terms, rows, name, start=None, split=True):
    count = len(terms[0][1])
    block = terms[0][1][0].shape[0]
    total = terms[0][0].shape[0]
    width = block * count
    sizes = [(x.shape[1], offset) for x, _, offset in terms]
    operands, specs = [], []
    for x, pieces, _ in terms:
        operands += [x, *pieces]
        specs += [fixed(x.shape)] + [pl.BlockSpec(memory_space=pl.ANY)] * count
    column = pl.BlockSpec((total, 2 * block), lambda s: (0, s))
    if start is not None:
        operands.append(start)
        specs.append(column)
    if split:
        out_specs = [
            pl.BlockSpec((rows, 2 * block), lambda s: (0, s)),
            pl.BlockSpec((total - rows, 2 * block), lambda s: (0, s)),
        ]
        out_shape = [shaped((rows, width), F32), shaped((total - rows, width), BF16)]
    else:
        out_specs, out_shape = [column], [shaped((total, width), F32)]
    depth = sum(size for size, _ in sizes)
    return pl.pallas_call(
        functools.partial(spread_kernel, sizes, count, rows, start is not None, split),
        grid=(count // 2,),
        in_specs=specs,
        out_specs=out_specs,
        out_shape=out_shape,
        scratch_shapes=[pltpu.VMEM((2, 2 * block, size), BF16) for size, _ in sizes]
        + [pltpu.SemaphoreType.DMA((2, 2 * len(sizes)))],
        compiler_params=params(),
        cost_estimate=cost(2 * total * depth * width, depth * width * 2 + total * width * 6),
        name=name,
    )(*operands)


def units_kernel(parts, count, *refs):
    n_refs, c_ref = refs[:parts], refs[parts]
    weights = refs[parts + 1 : parts + 1 + 3 * count]
    hid_out, dgate_out, dup_out = refs[parts + 1 + 3 * count :]

    def weight(k):
        return jnp.concatenate([ref[...] for ref in weights[k * count : (k + 1) * count]], axis=0)

    rows = n_refs[0].shape[0]
    w_gate, w_up, w_down = weight(0), weight(1), weight(2)
    for k in range(parts):
        here = slice(k * rows, (k + 1) * rows)
        gate = matmul(n_refs[k][...], w_gate)
        up = matmul(n_refs[k][...], w_up)
        dhid = matmul(c_ref[here], w_down)
        sig = jax.nn.sigmoid(gate)
        silu = gate * sig
        hid_out[here] = (silu * up).astype(BF16)
        dgate_out[here] = (dhid * up * sig * (1.0 + gate * (1.0 - sig))).astype(BF16)
        dup_out[here] = (dhid * silu).astype(BF16)


def ff_units(normed, cot, pieces, offset, chunk):
    rows, width = cot.shape
    count = len(pieces)
    block = pieces[0].shape[0]
    specs, operands = [], []
    for k in range(3):
        first = (offset + k * chunk) // COLUMN_TILE
        specs += [pl.BlockSpec((block, COLUMN_TILE), lambda i, first=first: (0, first + i))] * count
        operands += pieces
    out = pl.BlockSpec((rows, COLUMN_TILE), lambda i: (0, i))
    return pl.pallas_call(
        functools.partial(units_kernel, len(normed), count),
        grid=(chunk // COLUMN_TILE,),
        in_specs=[fixed(part.shape) for part in normed] + [fixed(cot.shape)] + specs,
        out_specs=[out] * 3,
        out_shape=[shaped((rows, chunk), BF16)] * 3,
        compiler_params=params(),
        cost_estimate=cost(
            6 * rows * width * chunk, 3 * width * chunk * 2 + rows * width * 4, rows * chunk
        ),
        name="ff_units",
    )(*normed, cot, *operands)


def attended_back_kernel(parts, count, *refs):
    weights = refs[parts : parts + count]
    att_ref, sg_ref = refs[parts + count : parts + count + 2]
    dout_out, delta_out, dlog_out, dgat = refs[parts + count + 2 :]
    step = pl.program_id(0)

    @pl.when(step == 0)
    def _():
        delta_out[...] = jnp.zeros_like(delta_out)
        dlog_out[...] = jnp.zeros_like(dlog_out)

    weight = jnp.concatenate([ref[...] for ref in weights], axis=0)
    rows = refs[0].shape[0]
    for k in range(parts):
        dgat[k * rows : (k + 1) * rows] = matmul(refs[k][...], weight)
    lane = lax.broadcasted_iota(jnp.int32, (ROW_TILE, LANES), 1)
    place = lax.broadcasted_iota(jnp.int32, (delta_out.shape[0], ROW_TILE), 0)
    for r in range(dgat.shape[0] // ROW_TILE):
        there = slice(r * ROW_TILE, (r + 1) * ROW_TILE)
        dlog = dlog_out[there].astype(F32)
        delta = delta_out[:, there]
        for j in range(COLUMN_TILE // HEAD):
            head = step * (COLUMN_TILE // HEAD) + j
            here = slice(j * HEAD, (j + 1) * HEAD)
            sg = jnp.sum(jnp.where(lane == head, sg_ref[there], 0.0), axis=1, keepdims=True)
            grad = dgat[there, here]
            att = att_ref[there, here]
            rounded = (grad * sg).astype(BF16)
            dout_out[there, here] = rounded
            turned = jnp.transpose(rounded.astype(F32) * att)
            delta = jnp.where(place == head, jnp.sum(turned, axis=0, keepdims=True), delta)
            dlog_h = jnp.sum(grad * att, axis=1, keepdims=True) * sg * (1.0 - sg)
            dlog = jnp.where(lane == head, dlog_h, dlog)
        dlog_out[there] = dlog.astype(BF16)
        delta_out[:, there] = delta


def attended_back(lefts, pieces, att, sg):
    count = len(pieces)
    block = pieces[0].shape[0]
    rows = lefts[0].shape[0] * len(lefts)
    width = att.shape[1]
    column = pl.BlockSpec((rows, COLUMN_TILE), lambda i: (0, i))
    delta_rows = max(8, width // HEAD)
    return pl.pallas_call(
        functools.partial(attended_back_kernel, len(lefts), count),
        grid=(width // COLUMN_TILE,),
        in_specs=[fixed(left.shape) for left in lefts]
        + [pl.BlockSpec((block, COLUMN_TILE), lambda i: (0, i))] * count
        + [column, fixed(sg.shape)],
        out_specs=[
            column,
            pl.BlockSpec((delta_rows, rows), lambda i: (0, 0)),
            pl.BlockSpec((rows, LANES), lambda i: (0, 0)),
        ],
        out_shape=[
            shaped((rows, width), BF16),
            shaped((delta_rows, rows), F32),
            shaped((rows, LANES), BF16),
        ],
        scratch_shapes=[pltpu.VMEM((rows, COLUMN_TILE), F32)],
        compiler_params=params(),
        cost_estimate=cost(2 * rows * block * count * width, block * count * width * 2 + rows * width * 10),
        name="attended_back",
    )(*lefts, *pieces, att, sg)


def flip_kernel(*refs):
    rows = refs[0].shape[0]
    for k, ref in enumerate(refs[:-1]):
        refs[-1][:, k * rows : (k + 1) * rows] = jnp.transpose(ref[...])


def flip(parts, name):
    rows, width = parts[0].shape
    return pl.pallas_call(
        flip_kernel,
        grid=(width // COLUMN_TILE,),
        in_specs=[pl.BlockSpec((rows, COLUMN_TILE), lambda i: (0, i))] * len(parts),
        out_specs=pl.BlockSpec((COLUMN_TILE, rows * len(parts)), lambda i: (i, 0)),
        out_shape=shaped((width, rows * len(parts)), BF16),
        compiler_params=params(),
        cost_estimate=cost(0, rows * width * len(parts) * 4),
        name=name,
    )(*parts)


def outer_kernel(which, steps, gained, *refs):
    used = 0
    order_ref = gain_ref = None
    if gained is not None:
        order_ref, gain_ref = refs[0], refs[1]
        used = 2
    n_left = max(which) + 1
    lefts = refs[used : used + n_left]
    rights = refs[used + n_left : used + n_left + len(which)]
    kept_out, sent_out = refs[used + n_left + len(which) :]
    step = pl.program_id(0)
    count = lefts[0].shape[0] // LANES
    for k, left in enumerate(which):

        @pl.when(step // steps == k)
        def _():
            for j in range(count // 2):
                there = slice(2 * j * LANES, (2 * j + 2) * LANES)
                total = matmul(lefts[left][there], rights[k][...]).astype(BF16)
                kept_out[j * LANES : (j + 1) * LANES] = total[:LANES]
                sent_out[j * LANES : (j + 1) * LANES] = total[LANES:]

    if gained is not None:
        size = HEAD // count
        lane = lax.broadcasted_iota(jnp.int32, (16, LANES), 1)
        row = lax.broadcasted_iota(jnp.int32, (16, LANES), 0)
        tile = kept_out.shape[1]

        @pl.when(step == gained // tile)
        def _():
            there = slice(gained % tile, gained % tile + LANES)
            for j in range(count):
                more = jnp.zeros((16, LANES), F32)
                for k in range(2):
                    sums = jnp.broadcast_to(gain_ref[k : k + 1, :], (16, LANES))
                    picked = (lane == order_ref[j] * size + row) & (row < size)
                    column = jnp.sum(jnp.where(picked, sums, 0.0), axis=1, keepdims=True)
                    more += jnp.where(lane == GAINS + 2 + k, column, 0.0)
                out = kept_out if j % 2 == 0 else sent_out
                here = slice((j // 2) * LANES, (j // 2) * LANES + 16)
                out[here, there] = (out[here, there].astype(F32) + more).astype(BF16)


def outer(lefts, rights, which, name, gains=None, gained=None):
    width, rows = lefts[0].shape
    size = rights[0].shape[1]
    tile = next(tile for tile in (384, 256, 128) if size % tile == 0)
    if len(rights) > 1:
        tile = COLUMN_TILE
    steps = size // tile
    specs, operands = [], []
    if gained is not None:
        operands += list(gains)
        specs += [pl.BlockSpec(memory_space=pltpu.SMEM), fixed(gains[1].shape)]
    operands += list(lefts) + list(rights)
    specs += [fixed(left.shape) for left in lefts]
    for k in range(len(rights)):
        specs.append(
            pl.BlockSpec((rows, tile), lambda i, k=k: (0, jnp.clip(i - k * steps, 0, steps - 1)))
        )
    total = size * len(rights)
    out = pl.BlockSpec((width // 2, tile), lambda i: (0, i))
    return pl.pallas_call(
        functools.partial(outer_kernel, which, steps, gained),
        grid=(steps * len(rights),),
        in_specs=specs,
        out_specs=[out, out],
        out_shape=[shaped((width // 2, total), BF16)] * 2,
        compiler_params=params(),
        cost_estimate=cost(2 * rows * width * total, width * total * 2 + rows * (width + total) * 2),
        name=name,
    )(*operands)


def arrived_sum(own_ref, refs):
    total = own_ref[...]
    for ref in refs:
        total = total + ref[...].astype(F32)
    return total


def mean_of(value):
    return jnp.mean(value, axis=-1, keepdims=True)


def middle_kernel(own_ref, tok_ref, wide_ref, *refs):
    middle_out, normed_out = refs[-2:]
    middle = tok_ref[...].astype(F32) + arrived_sum(own_ref, refs[:-2])
    middle_out[...] = middle
    scale = lax.rsqrt(mean_of(middle * middle) + EPS)
    normed_out[...] = (middle * scale * wide_ref[1:2, :]).astype(BF16)


def middle_back_kernel(own_ref, cot_ref, middle_ref, wide_ref, *refs):
    dmid_out, low_out = refs[-2:]
    middle = middle_ref[...]
    scale = lax.rsqrt(mean_of(middle * middle) + EPS)
    unit = middle * scale
    grad = arrived_sum(own_ref, refs[:-2]) * wide_ref[1:2, :]
    dmid = cot_ref[...].astype(F32) + scale * (grad - unit * mean_of(grad * unit))
    dmid_out[...] = dmid
    low_out[...] = dmid.astype(BF16)


def output_kernel(own_ref, middle_ref, *refs):
    refs[-1][...] = (middle_ref[...] + arrived_sum(own_ref, refs[:-1])).astype(BF16)


def input_back_kernel(own_ref, tok_ref, scale_ref, dmid_ref, wide_ref, *refs):
    scale = scale_ref[:, :1]
    unit = tok_ref[...].astype(F32) * scale
    grad = arrived_sum(own_ref, refs[:-1]) * wide_ref[0:1, :]
    refs[-1][...] = (dmid_ref[...] + scale * (grad - unit * mean_of(grad * unit))).astype(BF16)


def by_rows(kernel, rows, tile, operands, wide, arrived, dtypes, name):
    width = operands[0].shape[1]

    def at(operand):
        return pl.BlockSpec((tile, operand.shape[1]), lambda i: (i, 0))

    specs = [at(operand) for operand in operands]
    if wide is not None:
        specs.append(fixed(wide.shape))
        operands = operands + [wide]
    specs += [at(operand) for operand in arrived]
    out = pl.BlockSpec((tile, width), lambda i: (i, 0))
    return pl.pallas_call(
        kernel,
        grid=(rows // tile,),
        in_specs=specs,
        out_specs=[out] * len(dtypes),
        out_shape=[shaped((rows, width), dtype) for dtype in dtypes],
        compiler_params=params(),
        cost_estimate=cost(rows * width * 12, rows * width * 14),
        name=name,
    )(*operands, *arrived)


def heads_back_kernel(q_heads, k_heads, groups, tiles_ref, *refs):
    dq_refs = refs[:groups]
    dkv_refs = refs[groups : 4 * groups]
    dlog_refs = refs[4 * groups : 5 * groups]
    a_ref, b_ref, cos_ref, sin_ref, head_ref = refs[5 * groups : 5 * groups + 5]
    a_out, b_out, gain_out = refs[5 * groups + 5 :]

    @pl.when(pl.program_id(0) == 0)
    def _():
        gain_out[...] = jnp.zeros_like(gain_out)

    cos, sin = cos_ref[...], -sin_ref[...]

    def back(grad, value, gain):
        scale = lax.rsqrt(jnp.mean(value * value, axis=-1, keepdims=True) + EPS)
        unit = value * scale
        turned = turn(grad, cos, sin)
        scaled = turned * gain
        result = scale * (scaled - unit * jnp.mean(scaled * unit, axis=-1, keepdims=True))
        return result.astype(BF16), jnp.sum(turned * unit, axis=0, keepdims=True)

    def columns(h):
        return slice(h * HEAD, (h + 1) * HEAD)

    q_total = jnp.zeros((1, HEAD), F32)
    k_total = jnp.zeros((1, HEAD), F32)
    per = q_heads // groups
    for h in range(q_heads):
        grad = dq_refs[h // per][:, columns(h % per)]
        a_out[:, columns(h)], more = back(grad, a_ref[:, columns(h)], head_ref[2:3, :])
        q_total += more
    tail = dlog_refs[0][...]
    for ref in dlog_refs[1:]:
        tail = tail + ref[...]
    a_out[:, q_heads * HEAD :] = tail
    per = k_heads // groups

    def total(h, first):
        found = dkv_refs[3 * (h // per) : 3 * (h // per) + 3]
        return sum(ref[:, columns(first + h % per)].astype(F32) for ref in found)

    for h in range(k_heads):
        b_out[:, columns(h)], more = back(total(h, 0), b_ref[:, columns(h)], head_ref[3:4, :])
        k_total += more
        b_out[:, columns(k_heads + h)] = total(h, per).astype(BF16)
    gain_out[0:1, :] += q_total
    gain_out[1:2, :] += k_total


def heads_back(tiles, tile, dqs, dkvs, dlogs, raw_a, raw_b, cos, sin, head, q_heads, k_heads):
    rows = raw_a.shape[0]
    groups = len(dqs)

    def at(width):
        return pl.BlockSpec((tile, width), lambda i, tiles: (i, 0))

    moved = pl.BlockSpec((tile, 2 * k_heads * HEAD // groups), lambda i, tiles: (tiles[i], 0))
    return pl.pallas_call(
        functools.partial(heads_back_kernel, q_heads, k_heads, groups),
        grid_spec=pltpu.PrefetchScalarGridSpec(
            num_scalar_prefetch=1,
            grid=(rows // tile,),
            in_specs=[at(q_heads * HEAD // groups)] * groups
            + [moved] * (3 * groups)
            + [at(LANES)] * groups
            + [at(raw_a.shape[1]), at(raw_b.shape[1]), at(HEAD), at(HEAD), fixed(head.shape)],
            out_specs=[
                at(raw_a.shape[1]),
                at(raw_b.shape[1]),
                pl.BlockSpec((8, HEAD), lambda i, tiles: (0, 0)),
            ],
        ),
        out_shape=[
            shaped(raw_a.shape, BF16),
            shaped(raw_b.shape, BF16),
            shaped((8, HEAD), F32),
        ],
        compiler_params=params(),
        cost_estimate=cost(rows * (q_heads + k_heads) * HEAD * 30, rows * 2000 * 16),
        name="heads_back",
    )(tiles, *dqs, *[x for group in dkvs for x in group], *dlogs, raw_a, raw_b, cos, sin, head)


def load_keys(kv_refs, kv_all, sem, block_rows, columns):
    copies = [
        pltpu.make_async_copy(
            ref.at[:, pl.ds(source, width)],
            kv_all.at[pl.ds(m * block_rows, block_rows), pl.ds(target, width)],
            sem.at[m, k],
        )
        for m, ref in enumerate(kv_refs)
        for k, (source, target, width) in enumerate(columns)
    ]
    for copy in copies:
        copy.start()
    for copy in copies:
        copy.wait()


def key_columns(k_heads, k_first, mine):
    return [
        (k_first * HEAD, 0, mine * HEAD),
        ((k_heads + k_first) * HEAD, mine * HEAD, mine * HEAD),
    ]


def turn_blocks(kv_all, turned, first, mine):
    @pl.loop(0, kv_all.shape[0] // KEY_TILE)
    def _(t):
        rows = pl.ds(pl.multiple_of(t * KEY_TILE, KEY_TILE), KEY_TILE)
        for g in range(mine):
            here = slice((first + g) * HEAD, (first + g + 1) * HEAD)
            turned[g, :, rows] = jnp.transpose(kv_all[rows, here])


def attend_kernel(k_heads, k_first, blocks, flags_ref, *refs):
    q_ref, bias_ref, sg_ref = refs[:3]
    kv_refs = refs[3 : 3 + blocks]
    att_out, gated_out, lse_out = refs[3 + blocks : 6 + blocks]
    kv_all, v_turned, q_turned, acc, norm, sem = refs[6 + blocks :]
    mine = kv_all.shape[1] // (2 * HEAD)
    share = q_ref.shape[1] // (mine * HEAD)
    tile = q_ref.shape[0]
    step = pl.program_id(0)
    key_tiles = kv_all.shape[0] // KEY_TILE

    @pl.when(step == 0)
    def _():
        block_rows = kv_all.shape[0] // blocks
        load_keys(kv_refs, kv_all, sem, block_rows, key_columns(k_heads, k_first, mine))
        turn_blocks(kv_all, v_turned, mine, mine)
        lse_out[...] = jnp.zeros_like(lse_out)

    for h in range(mine * share):
        g, j = h // share, h % share
        q_turned[g, :, j * tile : (j + 1) * tile] = jnp.transpose(
            q_ref[:, h * HEAD : (h + 1) * HEAD]
        )
    acc[...] = jnp.zeros_like(acc)
    norm[...] = jnp.zeros_like(norm)

    @pl.loop(0, key_tiles)
    def _(t):
        @pl.when(flags_ref[step * key_tiles + t] > 0)
        def _():
            rows = pl.ds(pl.multiple_of(t * KEY_TILE, KEY_TILE), KEY_TILE)
            bias = bias_ref[rows, :]
            bias = jnp.concatenate([bias] * share, axis=1)
            for first in range(0, mine, FORWARD_HEADS):
                found = range(first, min(first + FORWARD_HEADS, mine))
                scores = [
                    matmul(kv_all[rows, g * HEAD : (g + 1) * HEAD], q_turned[g]) for g in found
                ]
                weights = [jnp.exp2(score * (SCALE * LOG2E) + bias) for score in scores]
                parts = [
                    matmul(v_turned[g, :, rows], weight.astype(BF16))
                    for g, weight in zip(found, weights)
                ]
                sums = [
                    jnp.sum(weight.reshape(KEY_TILE // 8, 8, share * tile), axis=0)
                    for weight in weights
                ]
                for g, part, more in zip(found, parts, sums):
                    acc[g] += part
                    norm[g] += more

    for g in range(mine):
        total = jnp.sum(norm[g], axis=0, keepdims=True)
        attended = acc[g] / total
        log_total = jnp.log2(total)
        for j in range(share):
            h = g * share + j
            here = slice(h * HEAD, (h + 1) * HEAD)
            there = slice(j * tile, (j + 1) * tile)
            part = jnp.transpose(attended[:, there])
            att_out[:, here] = part
            q_head = k_first * share + h
            gated_out[:, here] = (part * sg_ref[:, q_head : q_head + 1]).astype(BF16)
            lse_out[h : h + 1, pl.ds(pl.multiple_of(step * tile, tile), tile)] = log_total[:, there]


def attend(flags, tile, queries, bias, sg, kvs, q_heads, k_heads, k_first, k_count):
    rows = queries.shape[0]
    blocks = len(kvs)
    keys = sum(kv.shape[0] for kv in kvs)
    share = q_heads // k_heads
    q_width, kv_width = k_count * share * HEAD, 2 * k_count * HEAD
    lse_rows = max(8, k_count * share)

    def at(width, column=0):
        return pl.BlockSpec((tile, width), lambda i, flags: (i, column))

    return pl.pallas_call(
        functools.partial(attend_kernel, k_heads, k_first, blocks),
        grid_spec=pltpu.PrefetchScalarGridSpec(
            num_scalar_prefetch=1,
            grid=(rows // tile,),
            in_specs=[
                at(q_width, k_first // k_count),
                pl.BlockSpec((None, keys, tile), lambda i, flags: (i, 0, 0)),
                at(LANES),
            ]
            + [pl.BlockSpec(memory_space=pl.ANY)] * blocks,
            out_specs=[
                at(q_width),
                at(q_width),
                pl.BlockSpec((lse_rows, rows), lambda i, flags: (0, 0)),
            ],
            scratch_shapes=[
                pltpu.VMEM((keys, kv_width), BF16),
                pltpu.VMEM((k_count, HEAD, keys), BF16),
                pltpu.VMEM((k_count, HEAD, share * tile), BF16),
                pltpu.VMEM((k_count, HEAD, share * tile), F32),
                pltpu.VMEM((k_count, 8, share * tile), F32),
                pltpu.SemaphoreType.DMA((blocks, 2)),
            ],
        ),
        out_shape=[
            shaped((rows, q_width), F32),
            shaped((rows, q_width), BF16),
            shaped((lse_rows, rows), F32),
        ],
        compiler_params=params(),
        cost_estimate=cost(
            2 * rows * keys * q_width * 2, rows * keys * 4, rows * keys * q_width // HEAD
        ),
        name="attend",
    )(flags, queries, bias, sg, *kvs)


def attend_back_kernel(k_heads, k_first, blocks, flags_ref, *refs):
    q_ref, dout_ref, bias_ref, lse_ref, delta_ref = refs[:5]
    kv_refs = refs[5 : 5 + blocks]
    dq_out, keep_out, send_out = refs[5 + blocks : 8 + blocks]
    kv_all, k_turned, dkv, q_rows, q_turned, d_rows, d_turned, dq, sem = refs[8 + blocks :]
    mine = kv_all.shape[1] // (2 * HEAD)
    share = q_ref.shape[1] // (mine * HEAD)
    tile = q_ref.shape[0]
    step = pl.program_id(0)
    key_tiles = kv_all.shape[0] // KEY_TILE

    @pl.when(step == 0)
    def _():
        block_rows = kv_all.shape[0] // blocks
        load_keys(kv_refs, kv_all, sem, block_rows, key_columns(k_heads, k_first, mine))
        turn_blocks(kv_all, k_turned, 0, mine)
        dkv[...] = jnp.zeros_like(dkv)

    dq[...] = jnp.zeros_like(dq)
    for h in range(mine * share):
        g, j = h // share, h % share
        here = slice(h * HEAD, (h + 1) * HEAD)
        there = slice(j * tile, (j + 1) * tile)
        q_rows[g, there] = q_ref[:, here]
        q_turned[g, :, there] = jnp.transpose(q_ref[:, here])
        d_rows[g, there] = dout_ref[:, here]
        d_turned[g, :, there] = jnp.transpose(dout_ref[:, here])

    q_first = k_first * share

    def row_of(ref, g, first):
        cut = first + g * share
        return jnp.concatenate([ref[cut + j : cut + j + 1, :] for j in range(share)], axis=1)

    @pl.loop(0, key_tiles)
    def _(t):
        @pl.when(flags_ref[step * key_tiles + t] > 0)
        def _():
            rows = pl.ds(pl.multiple_of(t * KEY_TILE, KEY_TILE), KEY_TILE)
            bias = bias_ref[rows, :]
            bias = jnp.concatenate([bias] * share, axis=1)
            for first in range(0, mine, BACKWARD_HEADS):
                found = range(first, min(first + BACKWARD_HEADS, mine))
                scores = [
                    matmul(kv_all[rows, g * HEAD : (g + 1) * HEAD], q_turned[g]) for g in found
                ]
                dprobs = [
                    matmul(kv_all[rows, (mine + g) * HEAD : (mine + g + 1) * HEAD], d_turned[g])
                    for g in found
                ]
                probs = [
                    jnp.exp2(score * (SCALE * LOG2E) + bias - row_of(lse_ref, g, q_first))
                    for g, score in zip(found, scores)
                ]
                dscores = [
                    (prob * (dprob - row_of(delta_ref, g, q_first))).astype(BF16)
                    for g, prob, dprob in zip(found, probs, dprobs)
                ]
                dvs = [matmul(prob.astype(BF16), d_rows[g]) for g, prob in zip(found, probs)]
                dks = [matmul(dscore, q_rows[g]) for g, dscore in zip(found, dscores)]
                dqs = [
                    matmul(k_turned[g, :, rows], dscore) for g, dscore in zip(found, dscores)
                ]
                for k, g in enumerate(found):
                    dkv[rows, (mine + g) * HEAD : (mine + g + 1) * HEAD] += dvs[k]
                    dkv[rows, g * HEAD : (g + 1) * HEAD] += dks[k]
                    dq[g] += dqs[k]

    for h in range(mine * share):
        g, j = h // share, h % share
        dq_out[:, h * HEAD : (h + 1) * HEAD] = jnp.transpose(
            dq[g, :, j * tile : (j + 1) * tile] * SCALE
        )

    @pl.when(step == pl.num_programs(0) - 1)
    def _():
        half = kv_all.shape[0] // 2
        k_all = slice(0, mine * HEAD)
        v_all = slice(mine * HEAD, 2 * mine * HEAD)
        for out, first in ((keep_out, 0), (send_out, half)):
            out[:, k_all] = (dkv[first : first + half, k_all] * SCALE).astype(BF16)
            out[:, v_all] = dkv[first : first + half, v_all].astype(BF16)


def attend_back(
    flags, tile, queries, dout, bias, lse, delta, kvs, q_heads, k_heads, k_first, k_count
):
    rows = queries.shape[0]
    blocks = len(kvs)
    keys = sum(kv.shape[0] for kv in kvs)
    share = q_heads // k_heads
    q_width, kv_width = k_count * share * HEAD, 2 * k_count * HEAD
    column = k_first // k_count

    def at(width, column=0):
        return pl.BlockSpec((tile, width), lambda i, flags: (i, column))

    whole = pl.BlockSpec((keys // 2, kv_width), lambda i, flags: (0, 0))

    def by_lane(array):
        return pl.BlockSpec((array.shape[0], tile), lambda i, flags: (0, i))

    return pl.pallas_call(
        functools.partial(attend_back_kernel, k_heads, k_first, blocks),
        grid_spec=pltpu.PrefetchScalarGridSpec(
            num_scalar_prefetch=1,
            grid=(rows // tile,),
            in_specs=[
                at(q_width, column),
                at(q_width, column),
                pl.BlockSpec((None, keys, tile), lambda i, flags: (i, 0, 0)),
                by_lane(lse),
                by_lane(delta),
            ]
            + [pl.BlockSpec(memory_space=pl.ANY)] * blocks,
            out_specs=[at(q_width), whole, whole],
            scratch_shapes=[
                pltpu.VMEM((keys, kv_width), BF16),
                pltpu.VMEM((k_count, HEAD, keys), BF16),
                pltpu.VMEM((keys, kv_width), F32),
                pltpu.VMEM((k_count, share * tile, HEAD), BF16),
                pltpu.VMEM((k_count, HEAD, share * tile), BF16),
                pltpu.VMEM((k_count, share * tile, HEAD), BF16),
                pltpu.VMEM((k_count, HEAD, share * tile), BF16),
                pltpu.VMEM((k_count, HEAD, share * tile), F32),
                pltpu.SemaphoreType.DMA((blocks, 2)),
            ],
        ),
        out_shape=[
            shaped((rows, q_width), F32),
            shaped((keys // 2, kv_width), BF16),
            shaped((keys // 2, kv_width), BF16),
        ],
        compiler_params=params(),
        cost_estimate=cost(
            2 * rows * keys * q_width * 5, rows * keys * 4, rows * keys * q_width // HEAD
        ),
        name="attend_back",
    )(flags, queries, dout, bias, lse, delta, *kvs)


def per_device(
    sizes,
    tokens,
    seg_ids,
    positions,
    cotangent,
    norm_in,
    norm_mid,
    query_gain,
    key_gain,
    query_weight,
    key_matrix,
    value_matrix,
    head_weight,
    out_weight,
    gate_weight,
    up_weight,
    down_weight,
):
    n_shard, n_ctx, n_tp = sizes
    ring = Ring(n_shard, n_ctx)
    row_count, width = tokens.shape
    block = query_weight.shape[0]
    q_width = query_weight.shape[1]
    k_width = key_matrix.shape[1]
    q_heads, k_heads = q_width // HEAD, k_width // HEAD
    chunk = gate_weight.shape[1] // CHUNKS
    rows = row_count // n_tp
    tile = row_tile(rows)
    n_head = head_weight.shape[1]
    gain_size = query_gain.shape[0]

    here_ctx = lax.axis_index("ctx")
    here_tp = lax.axis_index("tp")
    here = lax.axis_index("shard") * n_ctx + here_ctx
    order = lax.dynamic_index_in_dim(jnp.asarray(ring.order), here, keepdims=False)

    def row_tiles(size):
        ids = np.arange(row_count // size)
        per = rows // size
        return (((here_tp + ids // per) % n_tp) * per + ids % per).astype(jnp.int32)

    tiles = row_tiles(tile)

    def padded(gain):
        return jnp.pad(gain, (0, block - gain_size))[:, None]

    send_a = jnp.concatenate(
        [
            query_weight,
            head_weight,
            jnp.zeros((block, GAINS - n_head), BF16),
            norm_in[:, None],
            norm_mid[:, None],
            padded(query_gain),
            padded(key_gain),
            jnp.zeros((block, LANES - GAINS - 4), BF16),
        ],
        axis=1,
    )

    def chunk_block(j, *others):
        cut = slice(j * chunk, (j + 1) * chunk)
        gate, up, down = gate_weight[:, cut], up_weight[:, cut], down_weight[cut]
        gate, up, down = lax.optimization_barrier((gate, up, down, *others))[:3]
        return jnp.concatenate([gate, up, down.T], axis=1)

    ring_a = Gather(ring, send_a)
    ring_b = Gather(ring, jnp.concatenate([key_matrix, value_matrix], axis=1))

    def tick(others, *rings):
        for one in rings:
            one.step(*others)

    tick([], ring_a, ring_b)
    tok, cot, scale_in = enter(order, tiles, tile, tokens, cotangent)
    offset = here_ctx * row_count

    def own_rows(values):
        parts = [
            lax.dynamic_slice_in_dim(values, offset + ((here_tp + j) % n_tp) * rows, rows)
            for j in range(n_tp)
        ]
        return jnp.concatenate(parts)

    own_seg, own_pos = own_rows(seg_ids), own_rows(positions)
    block_order = sorted(range(n_ctx), key=lambda m: (m & 1, m))

    def key_rows(values):
        return jnp.concatenate(
            [
                lax.dynamic_slice_in_dim(values, (here_ctx ^ m) * row_count, row_count)
                for m in block_order
            ]
        )

    key_seg, key_pos = key_rows(seg_ids), key_rows(positions)
    tick([tok], ring_a, ring_b)
    half = HEAD // 2
    frequency = THETA ** (-(jnp.arange(half, dtype=F32) * 2.0) / HEAD)
    angles = own_pos.astype(F32)[:, None] * frequency[None, :]
    cos, sin = jnp.cos(angles), jnp.sin(angles)
    cos = jnp.concatenate([cos, cos], axis=1)
    sin = jnp.concatenate([-sin, sin], axis=1)
    tick([cos, sin], ring_a, ring_b)
    key_pos = hold(key_pos, cos)
    q_tiles, key_tiles = row_count // ROW_TILE, key_seg.shape[0] // KEY_TILE
    q_seg, q_pos = (v.reshape(q_tiles, 1, ROW_TILE) for v in (own_seg, own_pos))
    k_seg, k_pos = key_seg[None, :, None], key_pos[None, :, None]
    allowed = ((k_seg == 0) | (k_seg == q_seg)) & (k_pos <= q_pos)
    bias = jnp.where(allowed, 0.0, MASKED).astype(F32)
    tick([bias], ring_a, ring_b)
    flags = jnp.max(
        allowed.astype(jnp.int32).reshape(q_tiles, key_tiles, KEY_TILE, ROW_TILE), axis=(2, 3)
    ).reshape(-1)
    ring_o = Gather(ring, hold(out_weight.T, bias))
    tick([flags], ring_a, ring_b, ring_o)
    tick([], ring_a, ring_b, ring_o)
    ring_c = [Gather(ring, chunk_block(0, ring_o.last))]
    tick([], ring_a, ring_b, ring_o)
    ring_c.append(Gather(ring, chunk_block(1, ring_o.last)))
    tick([ring_a.last], ring_o, ring_c[0], ring_c[1])

    wide, head = gather_gains(order, ring_a.pieces, q_width)
    normed, raw_a, raw_b, queries, kv, sg = project(
        row_tiles(rows),
        rows,
        tok,
        scale_in,
        wide,
        head,
        cos,
        sin,
        ring_a.pieces,
        ring_b.pieces,
        q_heads,
        k_heads,
    )
    kvs = {0: kv}
    bit = n_ctx // 2
    while bit:
        for m in list(kvs):
            kvs[m | bit] = lax.ppermute(kvs[m], "ctx", [(i, i ^ bit) for i in range(n_ctx)])
        bit //= 2
    kvs = [kvs[m] for m in block_order]
    tick([queries], ring_o)
    cot_turned = flip([hold(cot, queries)], "flip_cot")
    ring_c.append(Gather(ring, chunk_block(2, cot_turned)))
    queries = hold(queries, cot_turned, ring_o.last)
    tick([kvs[-1]], ring_o, *ring_c)
    att, gated, lse = attend(
        flags, ROW_TILE, queries, bias, sg, kvs, q_heads, k_heads, 0, k_heads
    )
    while len(ring_o.pieces) < 2 * ring.length:
        tick([gated], ring_o)
    tick([gated], ring_c[0])
    own, sent = spread([(gated, ring_o.pieces, 0)], rows, "out_rows")
    arrived = tp_send(sent, rows, n_tp)
    tick([sent], *ring_c)
    reached = ring_c[0].last
    tick([], ring_c[0])
    own = hold(own, reached)
    middle, low = by_rows(
        middle_kernel, rows, tile, [own, tok], wide, arrived, [F32, BF16], "middle"
    )
    normed_mid = tp_gather(low, n_tp)
    tick([low], *ring_c)
    reached = ring_c[0].last
    tick([], *ring_c)
    normed_mid[0] = hold(normed_mid[0], reached)

    def units(j, *others):
        normed = [hold(normed_mid[0], *others)] + normed_mid[1:]
        return ff_units(normed, cot, ring_c[j].pieces, 0, chunk)

    def weight_grads(j, *others):
        hidden, dgate, dup = made[j]
        kept, sent = outer(
            [normed_turned, cot_turned],
            [hold(dgate, *others), dup, hidden],
            [0, 0, 1],
            "unit_grads",
        )
        return Reduce(ring, kept, sent)

    def mid_terms(j):
        return [
            (made[j][1], ring_c[j].pieces, 0),
            (made[j][2], ring_c[j].pieces, chunk),
        ]

    for _ in range(2 * ring.length):
        if len(ring_c[0].pieces) < 2 * ring.length:
            ring_c[0].step()
    made = [units(0)]
    tick([made[0][0]], ring_c[1], ring_c[2])
    normed_turned = flip([hold(normed_mid[0], made[0][0])] + normed_mid[1:], "flip_mid")
    sums_c = [weight_grads(0)]
    tick([sums_c[0].kept], ring_c[1], ring_c[2])
    while len(ring_c[1].pieces) < 2 * ring.length:
        tick([], ring_c[1], ring_c[2])
    made.append(units(1, sums_c[0].kept))
    tick([made[1][0]], ring_c[2], sums_c[0])
    start = spread(mid_terms(0) + mid_terms(1), rows, "mid_start", split=False)[0]
    tick([start], ring_c[2], sums_c[0])
    while len(ring_c[2].pieces) < 2 * ring.length:
        tick([], ring_c[2])
    made.append(units(2, start))
    tick([made[2][0]], sums_c[0])
    own, sent = spread(mid_terms(2), rows, "mid_rows", start=start)
    arrived = tp_send(sent, rows, n_tp)
    tick([sent], sums_c[0])
    sums_c.append(weight_grads(1, sent))
    tick([sums_c[1].kept], sums_c[0])
    sums_c.append(weight_grads(2, sums_c[1].kept))
    tick([sums_c[2].kept], *sums_c[:2])
    own = hold(own, sums_c[2].kept)
    dmid, low = by_rows(
        middle_back_kernel,
        rows,
        tile,
        [own, cot, middle],
        wide,
        arrived,
        [F32, BF16],
        "middle_back",
    )
    dmid_low = tp_gather(low, n_tp)
    tick([low], *sums_c)
    terms = [(hold(made[j][0], low), ring_c[j].pieces, 2 * chunk) for j in range(CHUNKS)]
    mixed_own, mixed_sent = spread(terms, rows, "mixed_rows")
    tick([mixed_own], *sums_c)
    mixed_sent = hold(mixed_sent, dmid_low[-1])
    mixed_arrived = tp_send(mixed_sent, rows, n_tp)
    dmid_low[0] = hold(dmid_low[0], mixed_own)

    dout, delta, dlog = attended_back(dmid_low, ring_o.pieces, att, sg)
    tick([dout], *sums_c)
    dq, keep, sent = attend_back(
        flags, ROW_TILE, queries, dout, bias, lse, delta, kvs, q_heads, k_heads, 0, k_heads
    )
    other = ring.swap(sent)
    extra = None
    for k in range(1, n_ctx // 2):
        piece = slice(k * row_count, (k + 1) * row_count)
        away = (keep[piece].astype(F32) + other[piece].astype(F32)).astype(BF16)
        m = block_order[k]
        came = lax.ppermute(away, "ctx", [(i, i ^ m) for i in range(n_ctx)])
        extra = came if extra is None else (extra.astype(F32) + came.astype(F32)).astype(BF16)
    tick([dq], *sums_c)
    dmid_low[0] = hold(dmid_low[0], dq)
    dmid_turned = flip(dmid_low, "flip_dmid")
    sum_o = Reduce(ring, *outer([dmid_turned], [hold(gated, dmid_turned)], [0], "out_grad"))
    normed_in_turned = flip([hold(normed, sum_o.kept)], "flip_in")
    output = by_rows(
        output_kernel,
        rows,
        tile,
        [hold(mixed_own, normed_in_turned), middle],
        None,
        mixed_arrived,
        [BF16],
        "output",
    )[0]
    output_parts = tp_gather(output, n_tp)
    tick([output], sum_o, *sums_c)
    dq = hold(dq, output)
    d_a, d_b, gain_sums = heads_back(
        tiles, tile, [dq], [[keep, other, extra]], [dlog], raw_a, raw_b, cos, sin, head, q_heads, k_heads
    )
    tick([d_a], sum_o, *sums_c)
    sum_a = Reduce(
        ring,
        *outer(
            [normed_in_turned],
            [d_a],
            [0],
            "query_grad",
            gains=(order, gain_sums),
            gained=q_width,
        ),
    )
    tick([sum_a.kept], sum_o)
    sum_b = Reduce(ring, *outer([normed_in_turned], [hold(d_b, sum_a.kept)], [0], "key_grad"))
    tick([sum_b.kept], sum_a, sum_o, *sums_c)
    own, sent = spread(
        [(hold(d_a, sum_b.kept), ring_a.pieces, 0), (d_b, ring_b.pieces, 0)], rows, "in_rows"
    )
    arrived = tp_send(sent, rows, n_tp)
    tick([sent], sum_a, sum_b, sum_o, *sums_c)
    tick([], sum_a, sum_b, sum_o)
    own = hold(own, sum_a.total, sum_b.total)
    tick([], sum_a, sum_b, sum_o)
    low = by_rows(
        input_back_kernel,
        rows,
        tile,
        [own, tok, scale_in, dmid],
        wide,
        arrived,
        [BF16],
        "input_back",
    )[0]
    parts = tp_gather(low, n_tp)
    tick([low], sum_a, sum_b, sum_o, *sums_c)
    output = leave(
        order, tiles, tile, [hold(output_parts[0], low)] + output_parts[1:], BF16, "leave_output"
    )
    for _ in range(2):
        tick([], sum_a, sum_b, sum_o)
    parts[0] = hold(parts[0], output, sum_a.total, sum_b.total)
    input_grad = leave(order, tiles, tile, parts, F32, "leave_grad")

    sums_c = [part.finish() for part in sums_c]
    sum_a, sum_b, sum_o = sum_a.finish(), sum_b.finish(), sum_o.finish()
    sum_gate = jnp.concatenate([part[:, :chunk] for part in sums_c], axis=1)
    sum_up = jnp.concatenate([part[:, chunk : 2 * chunk] for part in sums_c], axis=1)
    sum_down = jnp.concatenate([part[:, 2 * chunk :].T for part in sums_c], axis=0)
    mid_share = jnp.sum(sum_gate * gate_weight.astype(F32), axis=1) + jnp.sum(
        sum_up * up_weight.astype(F32), axis=1
    )
    in_share = (
        jnp.sum(sum_a[:, :q_width] * query_weight.astype(F32), axis=1)
        + jnp.sum(sum_b[:, :k_width] * key_matrix.astype(F32), axis=1)
        + jnp.sum(sum_b[:, k_width:] * value_matrix.astype(F32), axis=1)
        + jnp.sum(sum_a[:, q_width : q_width + n_head] * head_weight.astype(F32), axis=1)
    )
    small = jnp.stack(
        [
            in_share / norm_in.astype(F32),
            mid_share / norm_mid.astype(F32),
            sum_a[:, q_width + GAINS + 2],
            sum_a[:, q_width + GAINS + 3],
        ]
    )
    small = tp_total(small, n_tp)
    return (
        output,
        input_grad,
        small[0],
        small[1],
        small[2, :gain_size],
        small[3, :gain_size],
        sum_a[:, :q_width],
        sum_b[:, :k_width],
        sum_b[:, k_width:],
        sum_a[:, q_width : q_width + n_head],
        sum_o.T,
        sum_gate,
        sum_up,
        sum_down,
    )


def solution(mesh):
    sizes = (mesh.shape["shard"], mesh.shape["ctx"], mesh.shape["tp"])
    split = ("shard", "ctx")
    rows = P(split, None)
    vector = P(split)
    weight = P(split, "tp")
    turned = P("tp", split)
    return jax.shard_map(
        functools.partial(per_device, sizes),
        mesh=mesh,
        in_specs=(rows, P("shard"), P("shard"), rows)
        + (vector,) * 4
        + (weight,) * 4
        + (turned, weight, weight, turned),
        out_specs=(rows, rows) + (vector,) * 4 + (weight,) * 4 + (turned, weight, weight, turned),
        check_vma=False,
    )
```

time: 1280 us -> 995 us (0.78)
  Pallas kernels: 122 us -> 375 us
  matrix products: 236 us -> 0 us
  waiting for transfers between devices: 552 us -> 362 us
  local copies, waits for them, and re-layouts: 161 us -> 31.7 us
  other arithmetic: 59.1 us -> 101 us
  starting transfers between devices: 133 us -> 109 us
    pallas_call x6 -> x30, Pallas kernels: 114 us -> 367 us  [the longest x6 78.4 us: outer(): pl.pallas_call(functools.partial(outer_kernel, which, steps, gained), gri...]
    dot_general x36 -> x0, matrix products: 236 us -> none  [matmul(): return lax.dot_general(a, b, (dims, ((), ())), preferred_element_type=F32)]
    ppermute x131 -> x89, waiting for transfers between devices: 464 us -> 308 us  [the longest x84 305 us: hop(): return lax.ppermute(value, ('shard', 'ctx'), self.hops)]
    unnamed x416 -> x236, local copies, waits for them, and re-layouts: 120 us -> 17.2 us
    ppermute x4, waiting for transfers between devices: 82.2 us -> 15.5 us  [tp_gather(): lax.ppermute(block, 'tp', [(i, (i - j) % n_tp) for i in range(n_tp)])]
    convert_element_type x60 -> x43, other arithmetic: 21.1 us -> 69.3 us  [the longest x36 60.2 us: step(): self.total = total if self.place == self.ring.length else total.astype(BF16)]
    ppermute x3, waiting for transfers between devices: 0.01 us -> 34.7 us  [per_device(): lax.ppermute(kvs[m], 'ctx', [(i, i ^ bit) for i in range(n_ctx)])]
    ppermute x82 -> x55, starting transfers between devices: 44.3 us -> 31.1 us  [swap(): return lax.ppermute(value, 'ctx', self.swaps)]
  transfers between devices with their start and end apart: 221 -> 152, of which waited for: 96 -> 52; matrix products, arithmetic and copies ran while one was open for 35% -> 12% of each run, Pallas kernels for 10% -> 36%
where the time goes in v1:
time: 995 us; the launch traced here: 982 us
  Pallas kernels  375 us (38%)
  waiting for transfers between devices  362 us (36%)
  starting transfers between devices  109 us (11%)
  other arithmetic  101 us (10%)
  local copies, waits for them, and re-layouts  31.7 us (3%)
    ppermute x84, waiting for transfers between devices, hop(): return lax.ppermute(value, ('shard', 'ctx'), self.hops)  305 us
    pallas_call x6, Pallas kernels, outer(): pl.pallas_call(functools.partial(outer_kernel, which, steps, gained), gri...  78.4 us
    pallas_call x5, Pallas kernels, spread(): pl.pallas_call(functools.partial(spread_kernel, sizes, count, rows, start...  76.2 us
    ppermute x84, starting transfers between devices, hop(): return lax.ppermute(value, ('shard', 'ctx'), self.hops)  66.3 us
    convert_element_type x36, other arithmetic, step(): self.total = total if self.place == self.ring.length else total.astype(BF16)  60.2 us
    pallas_call x3, Pallas kernels, ff_units(): pl.pallas_call(functools.partial(units_kernel, len(normed), count), grid=...  49.3 us
    ppermute x3, waiting for transfers between devices, per_device(): lax.ppermute(kvs[m], 'ctx', [(i, i ^ bit) for i in range(n_ctx)])  34.7 us
    pallas_call x1, Pallas kernels, attend_back(): pl.pallas_call(functools.partial(attend_back_kernel, k_heads, k_first, bl...  33.9 us
  transfers between devices with their start and end apart: 152, of which 52 were waited for; matrix products, arithmetic and copies ran while one was open for 12% of the time, Pallas kernels for 36%

profile of v1, /device:TPU:0, one launch (start us, length us, event | category | flops | bytes accessed | tf_op | source)
XLA Modules:
  0.0 981.6 jit_solution(10045055003968250277)
XLA Ops:
  83.8 14.9 %project.1 = (bf16[768,2048]{1,0:T(8,128)(2,1)}, f32[768,1152]{1,0:T(8,128)}, f32[768,1024]{1,0:T(8,128)}, bf16[768,1024]{1,0:T(8,128)(2,1)}, bf16[768,1024]{1,0:T(8,128)(2,1)}, /*index=5*/f32[768,128]{1,0:T(8,128)}) custom-call(s32[2]{0:T(128)} %and_select_fusion.1.tiles_ref, bf16[768,2048]{1,0:T(8,128)(2,1)} %get-tuple-element.168.refs_0_.tok_ref, ...), custom_call_target="tpu_custom_call" | custom-call | flops 6845104128 | bytes 34078720 | tf_op jit(solution)/shard_map/project/pallas_call | solution.py:331
  101.2 34.7 %collective-permute-done.35.refs_4_.refs_6_ = bf16[768,1024]{1,0:T(8,128)(2,1)} collective-permute-done((bf16[768,1024]{1,0:T(8,128)(2,1)}, bf16[768,1024]{1,0:T(8,128)(2,1)}, u32[]{:S(2)}, u32[]{:S(2)}) %collective-permute-start.35) | collective-permute-done | bytes 1572896 | tf_op jit(solution)/shard_map/ppermute | solution.py:1242
  152.1 11.2 %collective-permute-done.33.refs_9_.refs_10_ = bf16[128,1024]{1,0:T(8,128)(2,1)} collective-permute-done((bf16[128,1024]{1,0:T(8,128)(2,1)}, bf16[128,1024]{1,0:T(8,128)(2,1)}, u32[]{:S(2)}, u32[]{:S(2)}) %collective-permute-start.33) | collective-permute-done | bytes 262176 | tf_op jit(solution)/shard_map/ppermute | solution.py:67
  172.4 23.5 %attend.1 = (f32[768,1024]{1,0:T(8,128)}, bf16[768,1024]{1,0:T(8,128)(2,1)}, f32[8,768]{1,0:T(8,128)}) custom-call(s32[72]{0:T(128)} %reshape.105.flags_ref, bf16[768,1024]{1,0:T(8,128)(2,1)} %get-tuple-element.187.refs_0_, f32[6,3072,128]{2,1,0:T(8,128)} %and_select_fusion.refs_1_.refs_2_, f32[768,128]{1,0:T(8,128)} %get-tuple-element.188.refs_2_.refs_19_, ...), custom_call_target="tpu_custom_call" | custom-call | flops 9663676416 | bytes 9437184 | tf_op jit(solution)/shard_map/attend/pallas_call | solution.py:921
  218.0 9.9 %out_rows.1 = (f32[384,2048]{1,0:T(8,128)}, bf16[384,2048]{1,0:T(8,128)(2,1)}) custom-call(bf16[768,1024]{1,0:T(8,128)(2,1)} %get-tuple-element.258.refs_0_.refs_1_, bf16[128,1024]{1,0:T(8,128)(2,1)} %bitcast.50, bf16[128,1024]{1,0:T(8,128)(2,1)} %copy-done.103, bf16[128,1024]{1,0:T(8,128)(2,1)} %collective-permute-done.30.refs_3_.refs_4_, ...), custom_call_target="tpu_custom_call" | custom-call | flops 3221225472 | bytes 13631488 | tf_op jit(solution)/shard_map/out_rows/pallas_call | solution.py:443
  235.5 9.4 collective-permute-done.51.refs_11_.refs_27_.refs_43_.refs_9_.refs_26_
  244.9 8.4 collective-permute-done.68.refs_7_.refs_23_.refs_39_.refs_56_.refs_22_
  303.8 8.4 collective-permute-done.63.refs_17_.refs_33_.refs_49_.refs_15_.refs_32_
  312.2 8.5 collective-permute-done.85.refs_9_.refs_25_.refs_41_.refs_7_.refs_24_
  323.4 16.5 %ff_units.3 = (bf16[768,1024]{1,0:T(8,128)(2,1)}, bf16[768,1024]{1,0:T(8,128)(2,1)}, bf16[768,1024]{1,0:T(8,128)(2,1)}) custom-call(bf16[384,2048]{1,0:T(8,128)(2,1)} %get-tuple-element.223.refs_0_, bf16[384,2048]{1,0:T(8,128)(2,1)} %copy-done.33, bf16[768,2048]{1,0:T(8,128)(2,1)} %get-tuple-element.182.refs_0_.refs_2_.cot_ref, bf16[128,3072]{1,0:T(8,128)(2,1)} %copy-done, ...), custom_call_target="tpu_custom_call" | custom-call | flops 9663676416 | bytes 18874368 | tf_op jit(solution)/shard_map/ff_units/pallas_call | solution.py:489
  346.7 18.1 %unit_grads.3 = (bf16[1024,3072]{1,0:T(8,128)(2,1)}, bf16[1024,3072]{1,0:T(8,128)(2,1)}) custom-call(bf16[2048,768]{1,0:T(8,128)(2,1)} %flip_mid.1.refs_0_, bf16[2048,768]{1,0:T(8,128)(2,1)} %flip_cot.1.refs_1_, bf16[768,1024]{1,0:T(8,128)(2,1)} %get-tuple-element.207.refs_2_.refs_0_, bf16[768,1024]{1,0:T(8,128)(2,1)} %get-tuple-element.208.refs_3_.refs_17_, ...), custom_call_target="tpu_custom_call" | custom-call | flops 9663676416 | bytes 20447232 | tf_op jit(solution)/shard_map/unit_grads/pallas_call | solution.py:652
  370.6 9.2 collective-permute-done.89.refs_13_.refs_29_.refs_45_.refs_11_.refs_28_
  379.8 8.3 collective-permute-done.78.refs_17_.refs_33_.refs_49_.refs_66_.refs_32_
  392.2 16.5 %ff_units.4 = (bf16[768,1024]{1,0:T(8,128)(2,1)}, bf16[768,1024]{1,0:T(8,128)(2,1)}, bf16[768,1024]{1,0:T(8,128)(2,1)}) custom-call(bf16[384,2048]{1,0:T(8,128)(2,1)} %get-tuple-element.223.refs_0_, bf16[384,2048]{1,0:T(8,128)(2,1)} %copy-done.33, bf16[768,2048]{1,0:T(8,128)(2,1)} %get-tuple-element.182.refs_0_.refs_2_.cot_ref, bf16[128,3072]{1,0:T(8,128)(2,1)} %copy-done.1, ...), custom_call_target="tpu_custom_call" | custom-call | flops 9663676416 | bytes 18874368 | tf_op jit(solution)/shard_map/ff_units/pallas_call | solution.py:489
  411.4 9.7 collective-permute-done.93.refs_17_.refs_33_.refs_49_.refs_15_.refs_32_
  421.0 21.4 %mid_start.1.refs_34_ = f32[768,2048]{1,0:T(8,128)} custom-call(bf16[768,1024]{1,0:T(8,128)(2,1)} %get-tuple-element.207.refs_2_.refs_0_, bf16[128,3072]{1,0:T(8,128)(2,1)} %copy-done, bf16[128,3072]{1,0:T(8,128)(2,1)} %copy-done.7, bf16[128,3072]{1,0:T(8,128)(2,1)} %copy-done.3, bf16[128,3072]{1,0:T(8,128)(2,1)} %copy-done.8, bf16[128,3072]{1,0:T(8,128)(2,1)} %copy-done.4, ...), custom_call_target="tpu_custom_call" | custom-call | flops 12884901888 | bytes 26214400 | tf_op jit(solution)/shard_map/mid_start/pallas_call | solution.py:443
  444.9 16.4 %ff_units.5 = (bf16[768,1024]{1,0:T(8,128)(2,1)}, bf16[768,1024]{1,0:T(8,128)(2,1)}, bf16[768,1024]{1,0:T(8,128)(2,1)}) custom-call(bf16[384,2048]{1,0:T(8,128)(2,1)} %get-tuple-element.223.refs_0_, bf16[384,2048]{1,0:T(8,128)(2,1)} %copy-done.33, bf16[768,2048]{1,0:T(8,128)(2,1)} %get-tuple-element.182.refs_0_.refs_2_.cot_ref, bf16[128,3072]{1,0:T(8,128)(2,1)} %copy-done.2, ...), custom_call_target="tpu_custom_call" | custom-call | flops 9663676416 | bytes 18874368 | tf_op jit(solution)/shard_map/ff_units/pallas_call | solution.py:489
  461.3 14.4 %mid_rows.1 = (f32[384,2048]{1,0:T(8,128)}, bf16[384,2048]{1,0:T(8,128)(2,1)}) custom-call(bf16[768,1024]{1,0:T(8,128)(2,1)} %get-tuple-element.240.refs_0_.refs_2_, bf16[128,3072]{1,0:T(8,128)(2,1)} %copy-done.2, bf16[128,3072]{1,0:T(8,128)(2,1)} %copy-done.25, bf16[128,3072]{1,0:T(8,128)(2,1)} %collective-permute-done.81.refs_5_.refs_21_.refs_37_.refs_3_.refs_20_, ...), custom_call_target="tpu_custom_call" | custom-call | flops 6442450944 | bytes 17825792 | tf_op jit(solution)/shard_map/mid_rows/pallas_call | solution.py:443
  477.3 18.3 %unit_grads.4 = (bf16[1024,3072]{1,0:T(8,128)(2,1)}, bf16[1024,3072]{1,0:T(8,128)(2,1)}) custom-call(bf16[2048,768]{1,0:T(8,128)(2,1)} %flip_mid.1.refs_0_, bf16[2048,768]{1,0:T(8,128)(2,1)} %flip_cot.1.refs_1_, bf16[768,1024]{1,0:T(8,128)(2,1)} %get-tuple-element.238.refs_34_.refs_2_, bf16[768,1024]{1,0:T(8,128)(2,1)} %get-tuple-element.222.refs_51_.refs_3_, ...), custom_call_target="tpu_custom_call" | custom-call | flops 9663676416 | bytes 20447232 | tf_op jit(solution)/shard_map/unit_grads/pallas_call | solution.py:652
  498.8 18.1 %unit_grads.5 = (bf16[1024,3072]{1,0:T(8,128)(2,1)}, bf16[1024,3072]{1,0:T(8,128)(2,1)}) custom-call(bf16[2048,768]{1,0:T(8,128)(2,1)} %flip_mid.1.refs_0_, bf16[2048,768]{1,0:T(8,128)(2,1)} %flip_cot.1.refs_1_, bf16[768,1024]{1,0:T(8,128)(2,1)} %get-tuple-element.240.refs_0_.refs_2_, bf16[768,1024]{1,0:T(8,128)(2,1)} %get-tuple-element.235.refs_17_.refs_3_, ...), custom_call_target="tpu_custom_call" | custom-call | flops 9663676416 | bytes 20447232 | tf_op jit(solution)/shard_map/unit_grads/pallas_call | solution.py:652
  530.5 16.9 %mixed_rows.1 = (f32[384,2048]{1,0:T(8,128)}, bf16[384,2048]{1,0:T(8,128)(2,1)}) custom-call(bf16[768,1024]{1,0:T(8,128)(2,1)} %get-tuple-element.246.refs_4_.refs_0_, bf16[128,3072]{1,0:T(8,128)(2,1)} %copy-done, bf16[128,3072]{1,0:T(8,128)(2,1)} %copy-done.7, bf16[128,3072]{1,0:T(8,128)(2,1)} %copy-done.3, bf16[128,3072]{1,0:T(8,128)(2,1)} %copy-done.8, ...), custom_call_target="tpu_custom_call" | custom-call | flops 9663676416 | bytes 22020096 | tf_op jit(solution)/shard_map/mixed_rows/pallas_call | solution.py:443
  547.5 15.5 %collective-permute-done.96.refs_1_ = bf16[384,2048]{1,0:T(8,128)(2,1)S(1)} collective-permute-done((bf16[384,2048]{1,0:T(8,128)(2,1)}, bf16[384,2048]{1,0:T(8,128)(2,1)S(1)}, u32[]{:S(2)}, u32[]{:S(2)}) %collective-permute-start.96) | collective-permute-done | bytes 1572896 | tf_op jit(solution)/shard_map/ppermute | solution.py:125
  564.1 9.8 %attended_back.1 = (bf16[768,1024]{1,0:T(8,128)(2,1)}, f32[8,768]{1,0:T(8,128)}, bf16[768,128]{1,0:T(8,128)(2,1)}) custom-call(bf16[384,2048]{1,0:T(8,128)(2,1)} %get-tuple-element.257.refs_0_, bf16[384,2048]{1,0:T(8,128)(2,1)} %copy-done.49, bf16[128,1024]{1,0:T(8,128)(2,1)} %bitcast.51, bf16[128,1024]{1,0:T(8,128)(2,1)} %copy-done.103, ...), custom_call_target="tpu_custom_call" | custom-call | flops 3221225472 | bytes 12058624 | tf_op jit(solution)/shard_map/attended_back/pallas_call | solution.py:547
  576.8 33.9 %attend_back.1 = (f32[768,1024]{1,0:T(8,128)}, bf16[1536,1024]{1,0:T(8,128)(2,1)}, bf16[1536,1024]{1,0:T(8,128)(2,1)}) custom-call(s32[72]{0:T(128)} %reshape.105.flags_ref, bf16[768,1024]{1,0:T(8,128)(2,1)} %get-tuple-element.187.refs_0_, bf16[768,1024]{1,0:T(8,128)(2,1)} %get-tuple-element.253.refs_1_, f32[6,3072,128]{2,1,0:T(8,128)} %and_select_fusion.refs_1_.refs_2_, ...), custom_call_target="tpu_custom_call" | custom-call | flops 24159191040 | bytes 9437184 | tf_op jit(solution)/shard_map/attend_back/pallas_call | solution.py:1061
  633.8 26.0 %collective-permute-done.123 = bf16[128,3072]{1,0:T(8,128)(2,1)S(1)} collective-permute-done((bf16[128,3072]{1,0:T(8,128)(2,1)S(1)}, bf16[128,3072]{1,0:T(8,128)(2,1)S(1)}, u32[]{:S(2)}, u32[]{:S(2)}) %collective-permute-start.123) | collective-permute-done | bytes 786464 | tf_op jit(solution)/shard_map/ppermute | solution.py:67
  693.5 24.8 %collective-permute-done.128 = bf16[128,3072]{1,0:T(8,128)(2,1)S(1)} collective-permute-done((bf16[128,3072]{1,0:T(8,128)(2,1)S(1)}, bf16[128,3072]{1,0:T(8,128)(2,1)S(1)}, u32[]{:S(2)}, u32[]{:S(2)}) %collective-permute-start.128) | collective-permute-done | bytes 786464 | tf_op jit(solution)/shard_map/ppermute | solution.py:67
  720.1 11.9 %collective-permute-done.136 = bf16[128,3072]{1,0:T(8,128)(2,1)S(1)} collective-permute-done((bf16[128,3072]{1,0:T(8,128)(2,1)S(1)}, bf16[128,3072]{1,0:T(8,128)(2,1)S(1)}, u32[]{:S(2)}, u32[]{:S(2)}) %collective-permute-start.136) | collective-permute-done | bytes 786464 | tf_op jit(solution)/shard_map/ppermute | solution.py:67
  735.7 21.7 %collective-permute-done.129 = bf16[128,3072]{1,0:T(8,128)(2,1)S(1)} collective-permute-done((bf16[128,3072]{1,0:T(8,128)(2,1)S(1)}, bf16[128,3072]{1,0:T(8,128)(2,1)S(1)}, u32[]{:S(2)}, u32[]{:S(2)}) %collective-permute-start.129) | collective-permute-done | bytes 786464 | tf_op jit(solution)/shard_map/ppermute | solution.py:67
  778.0 12.8 %heads_back.1 = (bf16[768,1152]{1,0:T(8,128)(2,1)}, bf16[768,1024]{1,0:T(8,128)(2,1)}, f32[8,128]{1,0:T(8,128)}) custom-call(s32[6]{0:T(128)} %fusion.3.rows_ref.tiles_ref, f32[768,1024]{1,0:T(8,128)} %get-tuple-element.264.refs_0_, bf16[1536,1024]{1,0:T(8,128)(2,1)} %get-tuple-element.265.refs_1_, bf16[1536,1024]{1,0:T(8,128)(2,1)} %copy-done.35, ...), custom_call_target="tpu_custom_call" | custom-call | flops 35389440 | bytes 24576000 | tf_op jit(solution)/shard_map/heads_back/pallas_call | solution.py:786
  790.9 9.1 query_grad.1
  811.7 13.7 %in_rows.1 = (f32[384,2048]{1,0:T(8,128)}, bf16[384,2048]{1,0:T(8,128)(2,1)}) custom-call(bf16[768,1152]{1,0:T(8,128)(2,1)} %get-tuple-element.276.refs_3_.refs_0_, bf16[128,1152]{1,0:T(8,128)(2,1)} %copy-done.51, bf16[128,1152]{1,0:T(8,128)(2,1)} %copy-done.64, bf16[128,1152]{1,0:T(8,128)(2,1)} %copy-done.59, bf16[128,1152]{1,0:T(8,128)(2,1)} %copy-done.66, ...), custom_call_target="tpu_custom_call" | custom-call | flops 6845104128 | bytes 18350080 | tf_op jit(solution)/shard_map/in_rows/pallas_call | solution.py:443
  837.6 10.5 %collective-permute-done.150 = bf16[128,1024]{1,0:T(8,128)(2,1)S(1)} collective-permute-done((bf16[128,1024]{1,0:T(8,128)(2,1)S(1)}, bf16[128,1024]{1,0:T(8,128)(2,1)S(1)}, u32[]{:S(2)}, u32[]{:S(2)}) %collective-permute-start.150) | collective-permute-done | bytes 262176 | tf_op jit(solution)/shard_map/ppermute | solution.py:67
  (653 shorter events, 476.2 us)
Async XLA Ops:
  98.8 37.1 %collective-permute-start.35 = (bf16[768,1024]{1,0:T(8,128)(2,1)}, bf16[768,1024]{1,0:T(8,128)(2,1)}, u32[]{:S(2)}, u32[]{:S(2)}) collective-permute-start(bf16[768,1024]{1,0:T(8,128)(2,1)} %get-tuple-element.189.refs_3_.refs_5_), channel_id=1, source_target_pairs={{0,4},{2,6},{4,0},{6,2},{1,5},{3,7},{5,1},{7,3},{8,12},{10,14},{12... | collective-permute-start | bytes 4718600 | tf_op jit(solution)/shard_map/ppermute | solution.py:1242
  99.5 39.2 %collective-permute-start.30 = (bf16[128,1024]{1,0:T(8,128)(2,1)S(1)}, bf16[128,1024]{1,0:T(8,128)(2,1)}, u32[]{:S(2)}, u32[]{:S(2)}) collective-permute-start(bf16[128,1024]{1,0:T(8,128)(2,1)S(1)} %bitcast.49), channel_id=1, source_target_pairs={{0,8},{8,16},{16,24},{24,28},{28,20},{20,12},{12,4},{4,0},{2,6},{1... | collective-permute-start | bytes 786440 | tf_op jit(solution)/shard_map/ppermute | solution.py:67
  100.8 70.8 %collective-permute-start.36 = (bf16[768,1024]{1,0:T(8,128)(2,1)}, bf16[768,1024]{1,0:T(8,128)(2,1)}, u32[]{:S(2)}, u32[]{:S(2)}) collective-permute-start(bf16[768,1024]{1,0:T(8,128)(2,1)} %get-tuple-element.189.refs_3_.refs_5_), channel_id=1, source_target_pairs={{0,2},{2,0},{4,6},{6,4},{1,3},{3,1},{5,7},{7,5},{8,10},{10,8},{12,... | collective-permute-start | bytes 4718600 | tf_op jit(solution)/shard_map/ppermute | solution.py:1242
  135.9 35.5 %collective-permute-start.37 = (bf16[768,1024]{1,0:T(8,128)(2,1)}, bf16[768,1024]{1,0:T(8,128)(2,1)}, u32[]{:S(2)}, u32[]{:S(2)}) collective-permute-start(bf16[768,1024]{1,0:T(8,128)(2,1)} %collective-permute-done.35.refs_4_.refs_6_), channel_id=1, source_target_pairs={{0,2},{2,0},{4,6},{6,4},{1,3},{3,1},{5,7},{7,5},{8,10},{10,8},{12,... | collective-permute-start | bytes 4718600 | tf_op jit(solution)/shard_map/ppermute | solution.py:1242
  163.3 38.1 %collective-permute-start.38 = (bf16[128,1024]{1,0:T(8,128)(2,1)S(1)}, bf16[128,1024]{1,0:T(8,128)(2,1)S(1)}, u32[]{:S(2)}, u32[]{:S(2)}) collective-permute-start(bf16[128,1024]{1,0:T(8,128)(2,1)S(1)} %bitcast.52), channel_id=1, source_target_pairs={{0,2},{2,0},{4,6},{6,4},{1,3},{3,1},{5,7},{7,5},{8,10},{10,8},{12,... | collective-permute-start | bytes 786440 | tf_op jit(solution)/shard_map/ppermute | solution.py:70
  227.8 36.8 %collective-permute-start.52 = (bf16[384,2048]{1,0:T(8,128)(2,1)}, bf16[384,2048]{1,0:T(8,128)(2,1)}, u32[]{:S(2)}, u32[]{:S(2)}) collective-permute-start(bf16[384,2048]{1,0:T(8,128)(2,1)} %get-tuple-element.200), channel_id=1, source_target_pairs={{0,1},{1,0},{2,3},{3,2},{4,5},{5,4},{6,7},{7,6},{8,9},{9,8},{10,11... | collective-permute-start | bytes 4718600 | tf_op jit(solution)/shard_map/ppermute | solution.py:115
  279.0 41.8 %collective-permute-start.55 = (bf16[384,2048]{1,0:T(8,128)(2,1)}, bf16[384,2048]{1,0:T(8,128)(2,1)S(1)}, u32[]{:S(2)}, u32[]{:S(2)}) collective-permute-start(bf16[384,2048]{1,0:T(8,128)(2,1)} %get-tuple-element.223.refs_0_), channel_id=1, source_target_pairs={{0,1},{1,0},{2,3},{3,2},{4,5},{5,4},{6,7},{7,6},{8,9},{9,8},{10,11... | collective-permute-start | bytes 4718600 | tf_op jit(solution)/shard_map/ppermute | solution.py:125
  320.7 48.5 %collective-permute-start.65 = (bf16[128,3072]{1,0:T(8,128)(2,1)S(1)}, bf16[128,3072]{1,0:T(8,128)(2,1)}, u32[]{:S(2)}, u32[]{:S(2)}) collective-permute-start(bf16[128,3072]{1,0:T(8,128)(2,1)S(1)} %pad_maximum_fusion.4.refs_3_.refs_19_.refs_35_.refs_52_.refs_18_), channel_id=1, source_target_pairs={{0,2},{2,0},{4,6},{6,4},{1,3},{3,1},{5,7},{7,5},{8,10},{10,8},{12,... | collective-permute-start | bytes 2359304 | tf_op jit(solution)/shard_map/ppermute | solution.py:70
  320.8 49.2 %collective-permute-start.67 = (bf16[128,3072]{1,0:T(8,128)(2,1)}, bf16[128,3072]{1,0:T(8,128)(2,1)}, u32[]{:S(2)}, u32[]{:S(2)}) collective-permute-start(bf16[128,3072]{1,0:T(8,128)(2,1)} %collective-permute-done.66.refs_5_.refs_21_.refs_37_.refs_54_.refs_20_), channel_id=1, source_target_pairs={{0,2},{2,0},{4,6},{6,4},{1,3},{3,1},{5,7},{7,5},{8,10},{10,8},{12,... | collective-permute-start | bytes 2359304 | tf_op jit(solution)/shard_map/ppermute | solution.py:70
  321.3 48.7 %collective-permute-start.69 = (bf16[128,3072]{1,0:T(8,128)(2,1)}, bf16[128,3072]{1,0:T(8,128)(2,1)}, u32[]{:S(2)}, u32[]{:S(2)}) collective-permute-start(bf16[128,3072]{1,0:T(8,128)(2,1)} %collective-permute-done.68.refs_7_.refs_23_.refs_39_.refs_56_.refs_22_), channel_id=1, source_target_pairs={{0,2},{2,0},{4,6},{6,4},{1,3},{3,1},{5,7},{7,5},{8,10},{10,8},{12,... | collective-permute-start | bytes 2359304 | tf_op jit(solution)/shard_map/ppermute | solution.py:70
  323.3 41.5 %collective-permute-start.87 = (bf16[128,3072]{1,0:T(8,128)(2,1)}, bf16[128,3072]{1,0:T(8,128)(2,1)}, u32[]{:S(2)}, u32[]{:S(2)}) collective-permute-start(bf16[128,3072]{1,0:T(8,128)(2,1)} %collective-permute-done.85.refs_9_.refs_25_.refs_41_.refs_7_.refs_24_), channel_id=1, source_target_pairs={{0,8},{8,16},{16,24},{24,28},{28,20},{20,12},{12,4},{4,0},{2,6},{1... | collective-permute-start | bytes 2359304 | tf_op jit(solution)/shard_map/ppermute | solution.py:67
  370.0 125.7 %collective-permute-start.119 = (bf16[1024,3072]{1,0:T(8,128)(2,1)}, bf16[1024,3072]{1,0:T(8,128)(2,1)}, u32[]{:S(2)}, u32[]{:S(2)}) collective-permute-start(bf16[1024,3072]{1,0:T(8,128)(2,1)} %get-tuple-element.290), channel_id=1, source_target_pairs={{0,2},{2,0},{4,6},{6,4},{1,3},{3,1},{5,7},{7,5},{8,10},{10,8},{12,... | collective-permute-start | bytes 18874376 | tf_op jit(solution)/shard_map/ppermute | solution.py:70
  475.7 41.7 %collective-permute-start.95 = (bf16[384,2048]{1,0:T(8,128)(2,1)}, bf16[384,2048]{1,0:T(8,128)(2,1)S(1)}, u32[]{:S(2)}, u32[]{:S(2)}) collective-permute-start(bf16[384,2048]{1,0:T(8,128)(2,1)} %get-tuple-element.237), channel_id=1, source_target_pairs={{0,1},{1,0},{2,3},{3,2},{4,5},{5,4},{6,7},{7,6},{8,9},{9,8},{10,11... | collective-permute-start | bytes 4718600 | tf_op jit(solution)/shard_map/ppermute | solution.py:115
  516.9 169.5 %collective-permute-start.127 = (bf16[1024,3072]{1,0:T(8,128)(2,1)}, bf16[1024,3072]{1,0:T(8,128)(2,1)}, u32[]{:S(2)}, u32[]{:S(2)}) collective-permute-start(bf16[1024,3072]{1,0:T(8,128)(2,1)} %get-tuple-element.298), channel_id=1, source_target_pairs={{0,2},{2,0},{4,6},{6,4},{1,3},{3,1},{5,7},{7,5},{8,10},{10,8},{12,... | collective-permute-start | bytes 18874376 | tf_op jit(solution)/shard_map/ppermute | solution.py:70
  516.9 171.3 %collective-permute-start.135 = (bf16[1024,3072]{1,0:T(8,128)(2,1)}, bf16[1024,3072]{1,0:T(8,128)(2,1)}, u32[]{:S(2)}, u32[]{:S(2)}) collective-permute-start(bf16[1024,3072]{1,0:T(8,128)(2,1)} %get-tuple-element.306), channel_id=1, source_target_pairs={{0,2},{2,0},{4,6},{6,4},{1,3},{3,1},{5,7},{7,5},{8,10},{10,8},{12,... | collective-permute-start | bytes 18874376 | tf_op jit(solution)/shard_map/ppermute | solution.py:70
  526.4 36.6 %collective-permute-start.96 = (bf16[384,2048]{1,0:T(8,128)(2,1)}, bf16[384,2048]{1,0:T(8,128)(2,1)S(1)}, u32[]{:S(2)}, u32[]{:S(2)}) collective-permute-start(bf16[384,2048]{1,0:T(8,128)(2,1)} %get-tuple-element.257.refs_0_), channel_id=1, source_target_pairs={{0,1},{1,0},{2,3},{3,2},{4,5},{5,4},{6,7},{7,6},{8,9},{9,8},{10,11... | collective-permute-start | bytes 4718600 | tf_op jit(solution)/shard_map/ppermute | solution.py:125
  529.5 44.4 %collective-permute-start.121 = (bf16[128,3072]{1,0:T(8,128)(2,1)}, bf16[128,3072]{1,0:T(8,128)(2,1)}, u32[]{:S(2)}, u32[]{:S(2)}) collective-permute-start(bf16[128,3072]{1,0:T(8,128)(2,1)} %add_convert_fusion.20), channel_id=1, source_target_pairs={{0,8},{8,16},{16,24},{24,28},{28,20},{20,12},{12,4},{4,0},{2,6},{1... | collective-permute-start | bytes 2359304 | tf_op jit(solution)/shard_map/ppermute | solution.py:67
  562.9 99.4 %collective-permute-start.97 = (bf16[384,2048]{1,0:T(8,128)(2,1)}, bf16[384,2048]{1,0:T(8,128)(2,1)}, u32[]{:S(2)}, u32[]{:S(2)}) collective-permute-start(bf16[384,2048]{1,0:T(8,128)(2,1)} %get-tuple-element.263), channel_id=1, source_target_pairs={{0,1},{1,0},{2,3},{3,2},{4,5},{5,4},{6,7},{7,6},{8,9},{9,8},{10,11... | collective-permute-start | bytes 4718600 | tf_op jit(solution)/shard_map/ppermute | solution.py:115
  575.7 55.8 %collective-permute-start.122 = (bf16[128,3072]{1,0:T(8,128)(2,1)S(1)}, bf16[128,3072]{1,0:T(8,128)(2,1)S(1)}, u32[]{:S(2)}, u32[]{:S(2)}) collective-permute-start(bf16[128,3072]{1,0:T(8,128)(2,1)S(1)} %add_convert_fusion.19), channel_id=1, source_target_pairs={{0,8},{8,16},{16,24},{24,28},{28,20},{20,12},{12,4},{4,0},{2,6},{1... | collective-permute-start | bytes 2359304 | tf_op jit(solution)/shard_map/ppermute | solution.py:67
  624.9 49.0 %collective-permute-start.144 = (bf16[1024,1024]{1,0:T(8,128)(2,1)}, bf16[1024,1024]{1,0:T(8,128)(2,1)}, u32[]{:S(2)}, u32[]{:S(2)}) collective-permute-start(bf16[1024,1024]{1,0:T(8,128)(2,1)} %get-tuple-element.314), channel_id=1, source_target_pairs={{0,2},{2,0},{4,6},{6,4},{1,3},{3,1},{5,7},{7,5},{8,10},{10,8},{12,... | collective-permute-start | bytes 6291464 | tf_op jit(solution)/shard_map/ppermute | solution.py:70
  681.8 254.3 %collective-permute-start.108 = (bf16[384,2048]{1,0:T(8,128)(2,1)}, bf16[384,2048]{1,0:T(8,128)(2,1)}, u32[]{:S(2)}, u32[]{:S(2)}) collective-permute-start(bf16[384,2048]{1,0:T(8,128)(2,1)} %output.1.refs_0_), channel_id=1, source_target_pairs={{0,1},{1,0},{2,3},{3,2},{4,5},{5,4},{6,7},{7,6},{8,9},{9,8},{10,11... | collective-permute-start | bytes 4718600 | tf_op jit(solution)/shard_map/ppermute | solution.py:125
  686.3 47.5 %collective-permute-start.125 = (bf16[128,3072]{1,0:T(8,128)(2,1)S(1)}, bf16[128,3072]{1,0:T(8,128)(2,1)S(1)}, u32[]{:S(2)}, u32[]{:S(2)}) collective-permute-start(bf16[128,3072]{1,0:T(8,128)(2,1)S(1)} %add_convert_fusion.16), channel_id=1, source_target_pairs={{0,8},{8,16},{16,24},{24,28},{28,20},{20,12},{12,4},{4,0},{2,6},{1... | collective-permute-start | bytes 2359304 | tf_op jit(solution)/shard_map/ppermute | solution.py:67
  689.8 42.3 %collective-permute-start.136 = (bf16[128,3072]{1,0:T(8,128)(2,1)S(1)}, bf16[128,3072]{1,0:T(8,128)(2,1)S(1)}, u32[]{:S(2)}, u32[]{:S(2)}) collective-permute-start(bf16[128,3072]{1,0:T(8,128)(2,1)S(1)} %add_convert_fusion.7), channel_id=1, source_target_pairs={{0,8},{8,16},{16,24},{24,28},{28,20},{20,12},{12,4},{4,0},{2,6},{1... | collective-permute-start | bytes 2359304 | tf_op jit(solution)/shard_map/ppermute | solution.py:67
  693.2 83.7 %collective-permute-start.99 = (bf16[768,1024]{1,0:T(8,128)(2,1)S(1)}, bf16[768,1024]{1,0:T(8,128)(2,1)S(1)}, u32[]{:S(2)}, u32[]{:S(2)}) collective-permute-start(bf16[768,1024]{1,0:T(8,128)(2,1)S(1)} %add_convert_fusion), channel_id=1, source_target_pairs={{0,4},{2,6},{4,0},{6,2},{1,5},{3,7},{5,1},{7,3},{8,12},{10,14},{12... | collective-permute-start | bytes 4718600 | tf_op jit(solution)/shard_map/ppermute | solution.py:1347
  720.1 37.3 %collective-permute-start.129 = (bf16[128,3072]{1,0:T(8,128)(2,1)S(1)}, bf16[128,3072]{1,0:T(8,128)(2,1)S(1)}, u32[]{:S(2)}, u32[]{:S(2)}) collective-permute-start(bf16[128,3072]{1,0:T(8,128)(2,1)S(1)} %add_convert_fusion.13), channel_id=1, source_target_pairs={{0,8},{8,16},{16,24},{24,28},{28,20},{20,12},{12,4},{4,0},{2,6},{1... | collective-permute-start | bytes 2359304 | tf_op jit(solution)/shard_map/ppermute | solution.py:67
  735.6 38.6 %collective-permute-start.126 = (bf16[128,3072]{1,0:T(8,128)(2,1)S(1)}, bf16[128,3072]{1,0:T(8,128)(2,1)S(1)}, u32[]{:S(2)}, u32[]{:S(2)}) collective-permute-start(bf16[128,3072]{1,0:T(8,128)(2,1)S(1)} %add_convert_fusion.15), channel_id=1, source_target_pairs={{0,8},{8,16},{16,24},{24,28},{28,20},{20,12},{12,4},{4,0},{2,6},{1... | collective-permute-start | bytes 2359304 | tf_op jit(solution)/shard_map/ppermute | solution.py:67
  760.0 66.9 %collective-permute-start.130 = (bf16[128,3072]{1,0:T(8,128)(2,1)}, bf16[128,3072]{1,0:T(8,128)(2,1)S(1)}, u32[]{:S(2)}, u32[]{:S(2)}) collective-permute-start(bf16[128,3072]{1,0:T(8,128)(2,1)} %add_convert_fusion.12), channel_id=1, source_target_pairs={{0,8},{8,16},{16,24},{24,28},{28,20},{20,12},{12,4},{4,0},{2,6},{1... | collective-permute-start | bytes 2359304 | tf_op jit(solution)/shard_map/ppermute | solution.py:67
  767.5 67.6 %collective-permute-start.138 = (bf16[128,3072]{1,0:T(8,128)(2,1)S(1)}, bf16[128,3072]{1,0:T(8,128)(2,1)S(1)}, u32[]{:S(2)}, u32[]{:S(2)}) collective-permute-start(bf16[128,3072]{1,0:T(8,128)(2,1)S(1)} %add_convert_fusion.5), channel_id=1, source_target_pairs={{0,8},{8,16},{16,24},{24,28},{28,20},{20,12},{12,4},{4,0},{2,6},{1... | collective-permute-start | bytes 2359304 | tf_op jit(solution)/shard_map/ppermute | solution.py:67
  808.6 55.1 %collective-permute-start.104 = (bf16[1024,1024]{1,0:T(8,128)(2,1)}, bf16[1024,1024]{1,0:T(8,128)(2,1)S(1)}, u32[]{:S(2)}, u32[]{:S(2)}) collective-permute-start(bf16[1024,1024]{1,0:T(8,128)(2,1)} %get-tuple-element.282), channel_id=1, source_target_pairs={{0,2},{2,0},{4,6},{6,4},{1,3},{3,1},{5,7},{7,5},{8,10},{10,8},{12,... | collective-permute-start | bytes 6291464 | tf_op jit(solution)/shard_map/ppermute | solution.py:70
  825.4 40.7 %collective-permute-start.100 = (bf16[1024,1152]{1,0:T(8,128)(2,1)}, bf16[1024,1152]{1,0:T(8,128)(2,1)S(1)}, u32[]{:S(2)}, u32[]{:S(2)}) collective-permute-start(bf16[1024,1152]{1,0:T(8,128)(2,1)} %get-tuple-element.278), channel_id=1, source_target_pairs={{0,2},{2,0},{4,6},{6,4},{1,3},{3,1},{5,7},{7,5},{8,10},{10,8},{12,... | collective-permute-start | bytes 7077896 | tf_op jit(solution)/shard_map/ppermute | solution.py:70
  850.2 62.8 %collective-permute-start.107 = (bf16[384,2048]{1,0:T(8,128)(2,1)}, bf16[384,2048]{1,0:T(8,128)(2,1)}, u32[]{:S(2)}, u32[]{:S(2)}) collective-permute-start(bf16[384,2048]{1,0:T(8,128)(2,1)} %get-tuple-element.280), channel_id=1, source_target_pairs={{0,1},{1,0},{2,3},{3,2},{4,5},{5,4},{6,7},{7,6},{8,9},{9,8},{10,11... | collective-permute-start | bytes 4718600 | tf_op jit(solution)/shard_map/ppermute | solution.py:115
  936.1 38.3 %collective-permute-start.117 = (bf16[384,2048]{1,0:T(8,128)(2,1)S(1)}, bf16[384,2048]{1,0:T(8,128)(2,1)}, u32[]{:S(2)}, u32[]{:S(2)}) collective-permute-start(bf16[384,2048]{1,0:T(8,128)(2,1)S(1)} %copy-done.36), channel_id=1, source_target_pairs={{0,1},{1,0},{2,3},{3,2},{4,5},{5,4},{6,7},{7,6},{8,9},{9,8},{10,11... | collective-permute-start | bytes 4718600 | tf_op jit(solution)/shard_map/ppermute | solution.py:125
  (235 other events, 4120.9 us)

commit v2 on v1

--- a/solution.py
+++ b/solution.py
@@ -18,6 +18,7 @@
 KEY_TILE = 256
 CHUNKS = 3
 COLUMN_TILE = 256
+LAG = 3
 ROW_TILE = 128
 FORWARD_HEADS = 4
 BACKWARD_HEADS = 2
@@ -76,8 +77,11 @@
         self.last = block
         self.pieces = [block, ring.swap(block)]
 
+    def done(self):
+        return len(self.pieces) == 2 * self.ring.length
+
     def step(self, *others):
-        if len(self.pieces) < 2 * self.ring.length:
+        if not self.done():
             self.last = self.ring.hop(hold(self.last, *others))
             self.pieces += [self.last, self.ring.swap(self.last)]
         return self.last
@@ -97,8 +101,11 @@
         here = slice(first, first + self.rows)
         return self.kept[here].astype(F32) + self.other[here].astype(F32)
 
+    def done(self):
+        return self.place == self.ring.length
+
     def step(self, *others):
-        if self.place < self.ring.length:
+        if not self.done():
             self.place += 1
             total = self.ring.hop(hold(self.total, *others)).astype(F32) + self.own()
             self.total = total if self.place == self.ring.length else total.astype(BF16)
@@ -108,6 +115,21 @@
         while self.place < self.ring.length:
             self.step()
         return self.total
+
+
+class Clock:
+    def __init__(self):
+        self.ticks = [[]]
+
+    def tick(self, others, *rings):
+        self.ticks.append([one.step(*others) for one in rings if not one.done()])
+
+    def start(self, reduce):
+        self.ticks[-1].append(reduce.other)
+        return reduce
+
+    def gate(self, value, lag=LAG):
+        return hold(value, *[x for tick in self.ticks[:-lag][-3:] for x in tick])
 
 
 def tp_send(sent, rows, n_tp):
@@ -142,7 +164,9 @@
 
 
 def cost(flops, moved, transcendentals=0):
-    return pl.CostEstimate(flops=flops, bytes_accessed=moved, transcendentals=transcendentals)
+    return pl.CostEstimate(
+        flops=5 * flops, bytes_accessed=5 * moved, transcendentals=transcendentals
+    )
 
 
 def fixed(shape):
@@ -1167,9 +1191,8 @@
     ring_a = Gather(ring, send_a)
     ring_b = Gather(ring, jnp.concatenate([key_matrix, value_matrix], axis=1))
 
-    def tick(others, *rings):
-        for one in rings:
-            one.step(*others)
+    clock = Clock()
+    tick, gate = clock.tick, clock.gate
 
     tick([], ring_a, ring_b)
     tok, cot, scale_in = enter(order, tiles, tile, tokens, cotangent)
@@ -1201,30 +1224,30 @@
     cos, sin = jnp.cos(angles), jnp.sin(angles)
     cos = jnp.concatenate([cos, cos], axis=1)
     sin = jnp.concatenate([-sin, sin], axis=1)
-    tick([cos, sin], ring_a, ring_b)
-    key_pos = hold(key_pos, cos)
+    ring_o = Gather(ring, hold(out_weight.T, cos))
+    tick([cos, sin], ring_a, ring_b, ring_o)
+    key_pos = gate(hold(key_pos, cos))
     q_tiles, key_tiles = row_count // ROW_TILE, key_seg.shape[0] // KEY_TILE
     q_seg, q_pos = (v.reshape(q_tiles, 1, ROW_TILE) for v in (own_seg, own_pos))
     k_seg, k_pos = key_seg[None, :, None], key_pos[None, :, None]
     allowed = ((k_seg == 0) | (k_seg == q_seg)) & (k_pos <= q_pos)
     bias = jnp.where(allowed, 0.0, MASKED).astype(F32)
-    tick([bias], ring_a, ring_b)
+    tick([bias], ring_a, ring_b, ring_o)
     flags = jnp.max(
         allowed.astype(jnp.int32).reshape(q_tiles, key_tiles, KEY_TILE, ROW_TILE), axis=(2, 3)
     ).reshape(-1)
-    ring_o = Gather(ring, hold(out_weight.T, bias))
     tick([flags], ring_a, ring_b, ring_o)
     tick([], ring_a, ring_b, ring_o)
-    ring_c = [Gather(ring, chunk_block(0, ring_o.last))]
+    ring_c = [Gather(ring, chunk_block(0, ring_a.last))]
     tick([], ring_a, ring_b, ring_o)
-    ring_c.append(Gather(ring, chunk_block(1, ring_o.last)))
+    ring_c.append(Gather(ring, chunk_block(1, ring_a.last)))
     tick([ring_a.last], ring_o, ring_c[0], ring_c[1])
 
     wide, head = gather_gains(order, ring_a.pieces, q_width)
     normed, raw_a, raw_b, queries, kv, sg = project(
         row_tiles(rows),
         rows,
-        tok,
+        gate(tok),
         scale_in,
         wide,
         head,
@@ -1242,45 +1265,35 @@
             kvs[m | bit] = lax.ppermute(kvs[m], "ctx", [(i, i ^ bit) for i in range(n_ctx)])
         bit //= 2
     kvs = [kvs[m] for m in block_order]
-    tick([queries], ring_o)
-    cot_turned = flip([hold(cot, queries)], "flip_cot")
+    cot_turned = flip([gate(hold(cot, queries))], "flip_cot")
+    tick([cot_turned], ring_o)
     ring_c.append(Gather(ring, chunk_block(2, cot_turned)))
-    queries = hold(queries, cot_turned, ring_o.last)
-    tick([kvs[-1]], ring_o, *ring_c)
+    tick([kvs[-1]], *ring_c)
     att, gated, lse = attend(
-        flags, ROW_TILE, queries, bias, sg, kvs, q_heads, k_heads, 0, k_heads
-    )
-    while len(ring_o.pieces) < 2 * ring.length:
-        tick([gated], ring_o)
+        flags, ROW_TILE, gate(queries), bias, sg, kvs, q_heads, k_heads, 0, k_heads
+    )
     tick([gated], ring_c[0])
-    own, sent = spread([(gated, ring_o.pieces, 0)], rows, "out_rows")
+    own, sent = spread([(gate(gated), ring_o.pieces, 0)], rows, "out_rows")
     arrived = tp_send(sent, rows, n_tp)
     tick([sent], *ring_c)
-    reached = ring_c[0].last
-    tick([], ring_c[0])
-    own = hold(own, reached)
+    tick([], *ring_c)
     middle, low = by_rows(
-        middle_kernel, rows, tile, [own, tok], wide, arrived, [F32, BF16], "middle"
+        middle_kernel, rows, tile, [gate(own), tok], wide, arrived, [F32, BF16], "middle"
     )
     normed_mid = tp_gather(low, n_tp)
     tick([low], *ring_c)
-    reached = ring_c[0].last
     tick([], *ring_c)
-    normed_mid[0] = hold(normed_mid[0], reached)
-
-    def units(j, *others):
-        normed = [hold(normed_mid[0], *others)] + normed_mid[1:]
+
+    def units(j):
+        normed = [gate(normed_mid[0])] + normed_mid[1:]
         return ff_units(normed, cot, ring_c[j].pieces, 0, chunk)
 
-    def weight_grads(j, *others):
+    def weight_grads(j):
         hidden, dgate, dup = made[j]
         kept, sent = outer(
-            [normed_turned, cot_turned],
-            [hold(dgate, *others), dup, hidden],
-            [0, 0, 1],
-            "unit_grads",
+            [normed_turned, cot_turned], [gate(dgate), dup, hidden], [0, 0, 1], "unit_grads"
         )
-        return Reduce(ring, kept, sent)
+        return clock.start(Reduce(ring, kept, sent))
 
     def mid_terms(j):
         return [
@@ -1288,37 +1301,36 @@
             (made[j][2], ring_c[j].pieces, chunk),
         ]
 
-    for _ in range(2 * ring.length):
-        if len(ring_c[0].pieces) < 2 * ring.length:
-            ring_c[0].step()
     made = [units(0)]
-    tick([made[0][0]], ring_c[1], ring_c[2])
-    normed_turned = flip([hold(normed_mid[0], made[0][0])] + normed_mid[1:], "flip_mid")
+    tick([made[0][0]], *ring_c)
+    normed_turned = flip([gate(hold(normed_mid[0], made[0][0]))] + normed_mid[1:], "flip_mid")
+    tick([normed_turned], *ring_c)
     sums_c = [weight_grads(0)]
-    tick([sums_c[0].kept], ring_c[1], ring_c[2])
-    while len(ring_c[1].pieces) < 2 * ring.length:
-        tick([], ring_c[1], ring_c[2])
-    made.append(units(1, sums_c[0].kept))
+    tick([sums_c[0].kept], *ring_c)
+    normed_mid[0] = hold(normed_mid[0], sums_c[0].kept)
+    made.append(units(1))
     tick([made[1][0]], ring_c[2], sums_c[0])
-    start = spread(mid_terms(0) + mid_terms(1), rows, "mid_start", split=False)[0]
+    (x, *rest), *others = mid_terms(0) + mid_terms(1)
+    start = spread([(gate(x), *rest), *others], rows, "mid_start", split=False)[0]
     tick([start], ring_c[2], sums_c[0])
-    while len(ring_c[2].pieces) < 2 * ring.length:
-        tick([], ring_c[2])
-    made.append(units(2, start))
+    normed_mid[0] = hold(normed_mid[0], start)
+    made.append(units(2))
     tick([made[2][0]], sums_c[0])
-    own, sent = spread(mid_terms(2), rows, "mid_rows", start=start)
+    (x, *rest), *others = mid_terms(2)
+    own, sent = spread([(gate(x), *rest), *others], rows, "mid_rows", start=start)
     arrived = tp_send(sent, rows, n_tp)
     tick([sent], sums_c[0])
-    sums_c.append(weight_grads(1, sent))
-    tick([sums_c[1].kept], sums_c[0])
-    sums_c.append(weight_grads(2, sums_c[1].kept))
-    tick([sums_c[2].kept], *sums_c[:2])
-    own = hold(own, sums_c[2].kept)
+    made[1] = [hold(part, sent) for part in made[1]]
+    sums_c.append(weight_grads(1))
+    tick([sums_c[1].kept], *sums_c)
+    made[2] = [hold(part, sums_c[1].kept) for part in made[2]]
+    sums_c.append(weight_grads(2))
+    tick([sums_c[2].kept], *sums_c)
     dmid, low = by_rows(
         middle_back_kernel,
         rows,
         tile,
-        [own, cot, middle],
+        [gate(hold(own, sums_c[2].kept)), cot, middle],
         wide,
         arrived,
         [F32, BF16],
@@ -1326,17 +1338,17 @@
     )
     dmid_low = tp_gather(low, n_tp)
     tick([low], *sums_c)
-    terms = [(hold(made[j][0], low), ring_c[j].pieces, 2 * chunk) for j in range(CHUNKS)]
+    terms = [(gate(hold(made[j][0], low)), ring_c[j].pieces, 2 * chunk) for j in range(CHUNKS)]
     mixed_own, mixed_sent = spread(terms, rows, "mixed_rows")
     tick([mixed_own], *sums_c)
     mixed_sent = hold(mixed_sent, dmid_low[-1])
     mixed_arrived = tp_send(mixed_sent, rows, n_tp)
     dmid_low[0] = hold(dmid_low[0], mixed_own)
 
-    dout, delta, dlog = attended_back(dmid_low, ring_o.pieces, att, sg)
+    dout, delta, dlog = attended_back([gate(dmid_low[0])] + dmid_low[1:], ring_o.pieces, att, sg)
     tick([dout], *sums_c)
     dq, keep, sent = attend_back(
-        flags, ROW_TILE, queries, dout, bias, lse, delta, kvs, q_heads, k_heads, 0, k_heads
+        flags, ROW_TILE, queries, gate(dout), bias, lse, delta, kvs, q_heads, k_heads, 0, k_heads
     )
     other = ring.swap(sent)
     extra = None
@@ -1346,10 +1358,12 @@
         m = block_order[k]
         came = lax.ppermute(away, "ctx", [(i, i ^ m) for i in range(n_ctx)])
         extra = came if extra is None else (extra.astype(F32) + came.astype(F32)).astype(BF16)
-    tick([dq], *sums_c)
-    dmid_low[0] = hold(dmid_low[0], dq)
-    dmid_turned = flip(dmid_low, "flip_dmid")
-    sum_o = Reduce(ring, *outer([dmid_turned], [hold(gated, dmid_turned)], [0], "out_grad"))
+    dmid_low[0] = hold(dmid_low[0], away)
+    dmid_turned = flip([gate(dmid_low[0])] + dmid_low[1:], "flip_dmid")
+    tick([dmid_turned], *sums_c)
+    sum_o = clock.start(
+        Reduce(ring, *outer([dmid_turned], [gate(gated)], [0], "out_grad"))
+    )
     normed_in_turned = flip([hold(normed, sum_o.kept)], "flip_in")
     output = by_rows(
         output_kernel,
@@ -1363,38 +1377,51 @@
     )[0]
     output_parts = tp_gather(output, n_tp)
     tick([output], sum_o, *sums_c)
-    dq = hold(dq, output)
     d_a, d_b, gain_sums = heads_back(
-        tiles, tile, [dq], [[keep, other, extra]], [dlog], raw_a, raw_b, cos, sin, head, q_heads, k_heads
+        tiles,
+        tile,
+        [gate(hold(dq, output))],
+        [[keep, other, extra]],
+        [dlog],
+        raw_a,
+        raw_b,
+        cos,
+        sin,
+        head,
+        q_heads,
+        k_heads,
     )
     tick([d_a], sum_o, *sums_c)
-    sum_a = Reduce(
-        ring,
-        *outer(
-            [normed_in_turned],
-            [d_a],
-            [0],
-            "query_grad",
-            gains=(order, gain_sums),
-            gained=q_width,
-        ),
-    )
-    tick([sum_a.kept], sum_o)
-    sum_b = Reduce(ring, *outer([normed_in_turned], [hold(d_b, sum_a.kept)], [0], "key_grad"))
+    sum_a = clock.start(
+        Reduce(
+            ring,
+            *outer(
+                [normed_in_turned],
+                [gate(d_a)],
+                [0],
+                "query_grad",
+                gains=(order, gain_sums),
+                gained=q_width,
+            ),
+        )
+    )
+    tick([sum_a.kept], sum_o, *sums_c)
+    sum_b = clock.start(
+        Reduce(ring, *outer([normed_in_turned], [gate(hold(d_b, sum_a.kept))], [0], "key_grad"))
+    )
     tick([sum_b.kept], sum_a, sum_o, *sums_c)
     own, sent = spread(
-        [(hold(d_a, sum_b.kept), ring_a.pieces, 0), (d_b, ring_b.pieces, 0)], rows, "in_rows"
+        [(gate(hold(d_a, sum_b.kept)), ring_a.pieces, 0), (d_b, ring_b.pieces, 0)], rows, "in_rows"
     )
     arrived = tp_send(sent, rows, n_tp)
     tick([sent], sum_a, sum_b, sum_o, *sums_c)
     tick([], sum_a, sum_b, sum_o)
-    own = hold(own, sum_a.total, sum_b.total)
     tick([], sum_a, sum_b, sum_o)
     low = by_rows(
         input_back_kernel,
         rows,
         tile,
-        [own, tok, scale_in, dmid],
+        [gate(own), tok, scale_in, dmid],
         wide,
         arrived,
         [BF16],
@@ -1403,11 +1430,16 @@
     parts = tp_gather(low, n_tp)
     tick([low], sum_a, sum_b, sum_o, *sums_c)
     output = leave(
-        order, tiles, tile, [hold(output_parts[0], low)] + output_parts[1:], BF16, "leave_output"
-    )
-    for _ in range(2):
-        tick([], sum_a, sum_b, sum_o)
-    parts[0] = hold(parts[0], output, sum_a.total, sum_b.total)
+        order,
+        tiles,
+        tile,
+        [gate(hold(output_parts[0], low))] + output_parts[1:],
+        BF16,
+        "leave_output",
+    )
+    tick([output], sum_a, sum_b, sum_o)
+    tick([], sum_a, sum_b, sum_o)
+    parts[0] = gate(hold(parts[0], output))
     input_grad = leave(order, tiles, tile, parts, F32, "leave_grad")
 
     sums_c = [part.finish() for part in sums_c]

time: 995 us -> 964 us (0.969)
  waiting for transfers between devices: 362 us -> 309 us
  starting transfers between devices: 109 us -> 132 us
    ppermute x84, waiting for transfers between devices: 305 us -> 221 us  [hop(): return lax.ppermute(value, ('shard', 'ctx'), self.hops)]
    ppermute x4, waiting for transfers between devices: 2.87 us -> 21.6 us  [tp_send(): lax.ppermute(sent[(j - 1) * rows:j * rows], 'tp', [(i, (i + j) % n_tp) fo...]
    ppermute x55, starting transfers between devices: 31.1 us -> 46.4 us  [swap(): return lax.ppermute(value, 'ctx', self.swaps)]
  transfers between devices with their start and end apart: 152 -> 152, of which waited for: 52 -> 54; matrix products, arithmetic and copies ran while one was open for 12% -> 12% of each run, Pallas kernels for 36% -> 38%
where the time goes in v2:
time: 964 us; the launch traced here: 954 us
  Pallas kernels  377 us (39%)
  waiting for transfers between devices  309 us (32%)
  starting transfers between devices  132 us (14%)
  other arithmetic  103 us (11%)
  local copies, waits for them, and re-layouts  31 us (3%)
    ppermute x84, waiting for transfers between devices, hop(): return lax.ppermute(value, ('shard', 'ctx'), self.hops)  221 us
    pallas_call x6, Pallas kernels, outer(): pl.pallas_call(functools.partial(outer_kernel, which, steps, gained), gri...  78.2 us
    pallas_call x5, Pallas kernels, spread(): pl.pallas_call(functools.partial(spread_kernel, sizes, count, rows, start...  78.1 us
    ppermute x84, starting transfers between devices, hop(): return lax.ppermute(value, ('shard', 'ctx'), self.hops)  70.6 us
    convert_element_type x36, other arithmetic, step(): self.total = total if self.place == self.ring.length else total.astype(BF16)  60.2 us
    pallas_call x3, Pallas kernels, ff_units(): pl.pallas_call(functools.partial(units_kernel, len(normed), count), grid=...  49.4 us
    ppermute x55, starting transfers between devices, swap(): return lax.ppermute(value, 'ctx', self.swaps)  46.4 us
    ppermute x3, waiting for transfers between devices, per_device(): lax.ppermute(kvs[m], 'ctx', [(i, i ^ bit) for i in range(n_ctx)])  36.5 us
  transfers between devices with their start and end apart: 152, of which 54 were waited for; matrix products, arithmetic and copies ran while one was open for 12% of the time, Pallas kernels for 38%

profile of v2, /device:TPU:0, one launch (start us, length us, event | category | flops | bytes accessed | tf_op | source)
XLA Modules:
  0.0 953.9 jit_solution(16588421668588238191)
XLA Ops:
  19.3 8.3 enter.1
  91.5 14.9 %project.1 = (bf16[768,2048]{1,0:T(8,128)(2,1)}, f32[768,1152]{1,0:T(8,128)}, f32[768,1024]{1,0:T(8,128)}, bf16[768,1024]{1,0:T(8,128)(2,1)}, bf16[768,1024]{1,0:T(8,128)(2,1)}, /*index=5*/f32[768,128]{1,0:T(8,128)}) custom-call(s32[2]{0:T(128)} %and_select_fusion.1.tiles_ref, bf16[768,2048]{1,0:T(8,128)(2,1)} %get-tuple-element.209.refs_0_.tok_ref, ...), custom_call_target="tpu_custom_call" | custom-call | flops 34225520640 | bytes 170393600 | tf_op jit(solution)/shard_map/project/pallas_call | solution.py:355
  107.0 36.5 %collective-permute-done.35.refs_4_.refs_6_ = bf16[768,1024]{1,0:T(8,128)(2,1)} collective-permute-done((bf16[768,1024]{1,0:T(8,128)(2,1)}, bf16[768,1024]{1,0:T(8,128)(2,1)}, u32[]{:S(2)}, u32[]{:S(2)}) %collective-permute-start.35) | collective-permute-done | bytes 1572896 | tf_op jit(solution)/shard_map/ppermute | solution.py:1265
  151.8 10.5 %collective-permute-done.34.refs_11_.refs_12_ = bf16[128,1024]{1,0:T(8,128)(2,1)S(1)} collective-permute-done((bf16[128,1024]{1,0:T(8,128)(2,1)}, bf16[128,1024]{1,0:T(8,128)(2,1)S(1)}, u32[]{:S(2)}, u32[]{:S(2)}) %collective-permute-start.34) | collective-permute-done | bytes 262176 | tf_op jit(solution)/shard_map/ppermute | solution.py:68
  177.5 10.8 %collective-permute-done.48.refs_15_.refs_16_ = bf16[128,1024]{1,0:T(8,128)(2,1)S(1)} collective-permute-done((bf16[128,1024]{1,0:T(8,128)(2,1)S(1)}, bf16[128,1024]{1,0:T(8,128)(2,1)S(1)}, u32[]{:S(2)}, u32[]{:S(2)}) %collective-permute-start.48) | collective-permute-done | bytes 262176 | tf_op jit(solution)/shard_map/ppermute | solution.py:68
  189.4 23.4 %attend.1 = (f32[768,1024]{1,0:T(8,128)}, bf16[768,1024]{1,0:T(8,128)(2,1)}, f32[8,768]{1,0:T(8,128)}) custom-call(s32[72]{0:T(128)} %reshape.105.flags_ref, bf16[768,1024]{1,0:T(8,128)(2,1)} %get-tuple-element.214.refs_0_, f32[6,3072,128]{2,1,0:T(8,128)} %and_select_fusion.refs_1_.refs_2_, f32[768,128]{1,0:T(8,128)} %get-tuple-element.215.refs_2_.refs_19_, ...), custom_call_target="tpu_custom_call" | custom-call | flops 48318382080 | bytes 47185920 | tf_op jit(solution)/shard_map/attend/pallas_call | solution.py:945
  215.3 9.9 %out_rows.1 = (f32[384,2048]{1,0:T(8,128)}, bf16[384,2048]{1,0:T(8,128)(2,1)}) custom-call(bf16[768,1024]{1,0:T(8,128)(2,1)} %get-tuple-element.322.refs_0_.refs_1_, bf16[128,1024]{1,0:T(8,128)(2,1)} %bitcast.50, bf16[128,1024]{1,0:T(8,128)(2,1)} %copy-done.100, bf16[128,1024]{1,0:T(8,128)(2,1)} %copy-done.83, bf16[128,1024]{1,0:T(8,128)(2,1)} %copy-done.101, ...), custom_call_target="tpu_custom_call" | custom-call | flops 16106127360 | bytes 68157440 | tf_op jit(solution)/shard_map/out_rows/pallas_call | solution.py:467
  227.4 13.5 %collective-permute-done.54.refs_9_.refs_25_.refs_41_.refs_7_.refs_24_ = bf16[128,3072]{1,0:T(8,128)(2,1)S(1)} collective-permute-done((bf16[128,3072]{1,0:T(8,128)(2,1)}, bf16[128,3072]{1,0:T(8,128)(2,1)S(1)}, u32[]{:S(2)}, u32[]{:S(2)}) %collective-permute-start.54) | collective-permute-done | bytes 786464 | tf_op jit(solution)/shard_map/ppermute | solution.py:68
  241.0 8.3 collective-permute-done.52.refs_5_.refs_21_.refs_37_.refs_3_.refs_20_
  249.3 8.5 collective-permute-done.55.refs_11_.refs_27_.refs_43_.refs_9_.refs_26_
  274.7 8.4 collective-permute-done.64.refs_13_.refs_29_.refs_45_.refs_11_.refs_28_
  341.0 16.5 %ff_units.3 = (bf16[768,1024]{1,0:T(8,128)(2,1)}, bf16[768,1024]{1,0:T(8,128)(2,1)}, bf16[768,1024]{1,0:T(8,128)(2,1)}) custom-call(bf16[384,2048]{1,0:T(8,128)(2,1)} %get-tuple-element.267.refs_0_, bf16[384,2048]{1,0:T(8,128)(2,1)} %copy-done.14, bf16[768,2048]{1,0:T(8,128)(2,1)} %get-tuple-element.230.refs_0_.refs_2_.cot_ref, ...), custom_call_target="tpu_custom_call" | custom-call | flops 48318382080 | bytes 94371840 | tf_op jit(solution)/shard_map/ff_units/pallas_call | solution.py:513
  364.3 18.1 %unit_grads.3 = (bf16[1024,3072]{1,0:T(8,128)(2,1)}, bf16[1024,3072]{1,0:T(8,128)(2,1)}) custom-call(bf16[2048,768]{1,0:T(8,128)(2,1)} %flip_mid.1.refs_0_, bf16[2048,768]{1,0:T(8,128)(2,1)} %flip_cot.1.refs_1_, bf16[768,1024]{1,0:T(8,128)(2,1)} %get-tuple-element.260.refs_2_.refs_0_, bf16[768,1024]{1,0:T(8,128)(2,1)} %get-tuple-element.255.refs_3_.refs_17_, ...), custom_call_target="tpu_custom_call" | custom-call | flops 48318382080 | bytes 102236160 | tf_op jit(solution)/shard_map/unit_grads/pallas_call | solution.py:676
  397.0 8.5 collective-permute-done.77.refs_15_.refs_31_.refs_47_.refs_13_.refs_30_
  410.3 16.4 %ff_units.4 = (bf16[768,1024]{1,0:T(8,128)(2,1)}, bf16[768,1024]{1,0:T(8,128)(2,1)}, bf16[768,1024]{1,0:T(8,128)(2,1)}) custom-call(bf16[384,2048]{1,0:T(8,128)(2,1)} %get-tuple-element.267.refs_0_, bf16[384,2048]{1,0:T(8,128)(2,1)} %copy-done.14, bf16[768,2048]{1,0:T(8,128)(2,1)} %get-tuple-element.230.refs_0_.refs_2_.cot_ref, ...), custom_call_target="tpu_custom_call" | custom-call | flops 48318382080 | bytes 94371840 | tf_op jit(solution)/shard_map/ff_units/pallas_call | solution.py:513
  427.9 23.3 %mid_start.1.refs_34_ = f32[768,2048]{1,0:T(8,128)} custom-call(bf16[768,1024]{1,0:T(8,128)(2,1)} %get-tuple-element.260.refs_2_.refs_0_, bf16[128,3072]{1,0:T(8,128)(2,1)} %copy-done.21, bf16[128,3072]{1,0:T(8,128)(2,1)} %collective-permute-done.59.refs_4_.refs_20_.refs_36_.refs_2_.refs_19_, ...), custom_call_target="tpu_custom_call" | custom-call | flops 64424509440 | bytes 131072000 | tf_op jit(solution)/shard_map/mid_start/pallas_call | solution.py:467
  452.9 16.5 %ff_units.5 = (bf16[768,1024]{1,0:T(8,128)(2,1)}, bf16[768,1024]{1,0:T(8,128)(2,1)}, bf16[768,1024]{1,0:T(8,128)(2,1)}) custom-call(bf16[384,2048]{1,0:T(8,128)(2,1)} %get-tuple-element.267.refs_0_, bf16[384,2048]{1,0:T(8,128)(2,1)} %copy-done.14, bf16[768,2048]{1,0:T(8,128)(2,1)} %get-tuple-element.230.refs_0_.refs_2_.cot_ref, ...), custom_call_target="tpu_custom_call" | custom-call | flops 48318382080 | bytes 94371840 | tf_op jit(solution)/shard_map/ff_units/pallas_call | solution.py:513
  472.4 14.3 %mid_rows.1 = (f32[384,2048]{1,0:T(8,128)}, bf16[384,2048]{1,0:T(8,128)(2,1)}) custom-call(bf16[768,1024]{1,0:T(8,128)(2,1)} %get-tuple-element.282.refs_0_.refs_2_, bf16[128,3072]{1,0:T(8,128)(2,1)} %copy-done.22, bf16[128,3072]{1,0:T(8,128)(2,1)} %collective-permute-done.88.refs_4_.refs_20_.refs_36_.refs_2_.refs_19_, bf16[128,3072]{1,0:T(8,128)(2,1)} %copy-done.57, ...), custom_call_target="tpu_custom_call" | custom-call | flops 32212254720 | bytes 89128960 | tf_op jit(solution)/shard_map/mid_rows/pallas_call | solution.py:467
  489.6 18.2 %unit_grads.4 = (bf16[1024,3072]{1,0:T(8,128)(2,1)}, bf16[1024,3072]{1,0:T(8,128)(2,1)}) custom-call(bf16[2048,768]{1,0:T(8,128)(2,1)} %flip_mid.1.refs_0_, bf16[2048,768]{1,0:T(8,128)(2,1)} %flip_cot.1.refs_1_, bf16[768,1024]{1,0:T(8,128)(2,1)} %get-tuple-element.276.refs_34_.refs_2_, bf16[768,1024]{1,0:T(8,128)(2,1)} %get-tuple-element.277.refs_51_.refs_3_, ...), custom_call_target="tpu_custom_call" | custom-call | flops 48318382080 | bytes 102236160 | tf_op jit(solution)/shard_map/unit_grads/pallas_call | solution.py:676
  511.3 18.1 %unit_grads.5 = (bf16[1024,3072]{1,0:T(8,128)(2,1)}, bf16[1024,3072]{1,0:T(8,128)(2,1)}) custom-call(bf16[2048,768]{1,0:T(8,128)(2,1)} %flip_mid.1.refs_0_, bf16[2048,768]{1,0:T(8,128)(2,1)} %flip_cot.1.refs_1_, bf16[768,1024]{1,0:T(8,128)(2,1)} %get-tuple-element.282.refs_0_.refs_2_, bf16[768,1024]{1,0:T(8,128)(2,1)} %get-tuple-element.283.refs_17_.refs_3_, ...), custom_call_target="tpu_custom_call" | custom-call | flops 48318382080 | bytes 102236160 | tf_op jit(solution)/shard_map/unit_grads/pallas_call | solution.py:676
  533.4 9.9 %collective-permute-done.102 = bf16[128,3072]{1,0:T(8,128)(2,1)S(1)} collective-permute-done((bf16[128,3072]{1,0:T(8,128)(2,1)S(1)}, bf16[128,3072]{1,0:T(8,128)(2,1)S(1)}, u32[]{:S(2)}, u32[]{:S(2)}) %collective-permute-start.102) | collective-permute-done | bytes 786464 | tf_op jit(solution)/shard_map/ppermute | solution.py:68
  546.5 21.6 %collective-permute-done.99.refs_0_ = bf16[384,2048]{1,0:T(8,128)(2,1)S(1)} collective-permute-done((bf16[384,2048]{1,0:T(8,128)(2,1)S(1)}, bf16[384,2048]{1,0:T(8,128)(2,1)S(1)}, u32[]{:S(2)}, u32[]{:S(2)}) %collective-permute-start.99) | collective-permute-done | bytes 1572896 | tf_op jit(solution)/shard_map/ppermute | solution.py:137
  569.3 7.8 middle_back.1
  608.0 17.0 %mixed_rows.1 = (f32[384,2048]{1,0:T(8,128)}, bf16[384,2048]{1,0:T(8,128)(2,1)}) custom-call(bf16[768,1024]{1,0:T(8,128)(2,1)} %get-tuple-element.295.refs_4_.refs_0_, bf16[128,3072]{1,0:T(8,128)(2,1)} %copy-done.21, bf16[128,3072]{1,0:T(8,128)(2,1)} %collective-permute-done.59.refs_4_.refs_20_.refs_36_.refs_2_.refs_19_, ...), custom_call_target="tpu_custom_call" | custom-call | flops 48318382080 | bytes 110100480 | tf_op jit(solution)/shard_map/mixed_rows/pallas_call | solution.py:467
  632.4 9.8 %attended_back.1 = (bf16[768,1024]{1,0:T(8,128)(2,1)}, f32[8,768]{1,0:T(8,128)}, bf16[768,128]{1,0:T(8,128)(2,1)}) custom-call(bf16[384,2048]{1,0:T(8,128)(2,1)} %get-tuple-element.318.refs_0_, bf16[384,2048]{1,0:T(8,128)(2,1)} %collective-permute-done.105.refs_1_, bf16[128,1024]{1,0:T(8,128)(2,1)} %bitcast.51, bf16[128,1024]{1,0:T(8,128)(2,1)} %copy-done.100, ...), custom_call_target="tpu_custom_call" | custom-call | flops 16106127360 | bytes 60293120 | tf_op jit(solution)/shard_map/attended_back/pallas_call | solution.py:571
  652.6 34.0 %attend_back.1 = (f32[768,1024]{1,0:T(8,128)}, bf16[1536,1024]{1,0:T(8,128)(2,1)}, bf16[1536,1024]{1,0:T(8,128)(2,1)}) custom-call(s32[72]{0:T(128)} %reshape.105.flags_ref, bf16[768,1024]{1,0:T(8,128)(2,1)} %get-tuple-element.214.refs_0_, bf16[768,1024]{1,0:T(8,128)(2,1)} %get-tuple-element.312.refs_1_, f32[6,3072,128]{2,1,0:T(8,128)} %and_select_fusion.refs_1_.refs_2_, ...), custom_call_target="tpu_custom_call" | custom-call | flops 120795955200 | bytes 47185920 | tf_op jit(solution)/shard_map/attend_back/pallas_call | solution.py:1085
  697.9 20.9 %collective-permute-done.117 = bf16[128,3072]{1,0:T(8,128)(2,1)S(1)} collective-permute-done((bf16[128,3072]{1,0:T(8,128)(2,1)S(1)}, bf16[128,3072]{1,0:T(8,128)(2,1)S(1)}, u32[]{:S(2)}, u32[]{:S(2)}) %collective-permute-start.117) | collective-permute-done | bytes 786464 | tf_op jit(solution)/shard_map/ppermute | solution.py:68
  762.8 12.6 %collective-permute-done.119 = bf16[128,3072]{1,0:T(8,128)(2,1)} collective-permute-done((bf16[128,3072]{1,0:T(8,128)(2,1)}, bf16[128,3072]{1,0:T(8,128)(2,1)}, u32[]{:S(2)}, u32[]{:S(2)}) %collective-permute-start.119) | collective-permute-done | bytes 786464 | tf_op jit(solution)/shard_map/ppermute | solution.py:68
  785.7 12.8 %heads_back.1 = (bf16[768,1152]{1,0:T(8,128)(2,1)}, bf16[768,1024]{1,0:T(8,128)(2,1)}, f32[8,128]{1,0:T(8,128)}) custom-call(s32[6]{0:T(128)} %fusion.3.rows_ref.tiles_ref, f32[768,1024]{1,0:T(8,128)} %get-tuple-element.332.refs_0_, bf16[1536,1024]{1,0:T(8,128)(2,1)} %get-tuple-element.315.refs_1_, bf16[1536,1024]{1,0:T(8,128)(2,1)} %copy-done.1, ...), custom_call_target="tpu_custom_call" | custom-call | flops 176947200 | bytes 122880000 | tf_op jit(solution)/shard_map/heads_back/pallas_call | solution.py:810
  798.5 9.0 query_grad.1
  827.3 13.6 %in_rows.1 = (f32[384,2048]{1,0:T(8,128)}, bf16[384,2048]{1,0:T(8,128)(2,1)}) custom-call(bf16[768,1152]{1,0:T(8,128)(2,1)} %get-tuple-element.353.refs_3_.refs_0_, bf16[128,1152]{1,0:T(8,128)(2,1)} %copy-done.18, bf16[128,1152]{1,0:T(8,128)(2,1)} %copy-done.31, bf16[128,1152]{1,0:T(8,128)(2,1)} %copy-done.26, bf16[128,1152]{1,0:T(8,128)(2,1)} %copy-done.32, ...), custom_call_target="tpu_custom_call" | custom-call | flops 34225520640 | bytes 91750400 | tf_op jit(solution)/shard_map/in_rows/pallas_call | solution.py:467
  927.3 17.9 %collective-permute-done.143.refs_1_ = bf16[384,2048]{1,0:T(8,128)(2,1)} collective-permute-done((bf16[384,2048]{1,0:T(8,128)(2,1)S(1)}, bf16[384,2048]{1,0:T(8,128)(2,1)}, u32[]{:S(2)}, u32[]{:S(2)}) %collective-permute-start.143) | collective-permute-done | bytes 1572896 | tf_op jit(solution)/shard_map/ppermute | solution.py:147
  (645 shorter events, 461.3 us)
Async XLA Ops:
  15.9 36.4 %collective-permute-start.6 = (bf16[128,1024]{1,0:T(8,128)(2,1)S(1)}, bf16[128,1024]{1,0:T(8,128)(2,1)S(1)}, u32[]{:S(2)}, u32[]{:S(2)}) collective-permute-start(bf16[128,1024]{1,0:T(8,128)(2,1)S(1)} %bitcast.49), channel_id=1, source_target_pairs={{0,8},{8,16},{16,24},{24,28},{28,20},{20,12},{12,4},{4,0},{2,6},{1... | collective-permute-start | bytes 786440 | tf_op jit(solution)/shard_map/ppermute | solution.py:68
  106.4 37.1 %collective-permute-start.35 = (bf16[768,1024]{1,0:T(8,128)(2,1)}, bf16[768,1024]{1,0:T(8,128)(2,1)}, u32[]{:S(2)}, u32[]{:S(2)}) collective-permute-start(bf16[768,1024]{1,0:T(8,128)(2,1)} %get-tuple-element.216.refs_3_.refs_5_), channel_id=1, source_target_pairs={{0,4},{2,6},{4,0},{6,2},{1,5},{3,7},{5,1},{7,3},{8,12},{10,14},{12... | collective-permute-start | bytes 4718600 | tf_op jit(solution)/shard_map/ppermute | solution.py:1265
  145.7 43.1 %collective-permute-start.36 = (bf16[768,1024]{1,0:T(8,128)(2,1)}, bf16[768,1024]{1,0:T(8,128)(2,1)}, u32[]{:S(2)}, u32[]{:S(2)}) collective-permute-start(bf16[768,1024]{1,0:T(8,128)(2,1)} %get-tuple-element.216.refs_3_.refs_5_), channel_id=1, source_target_pairs={{0,2},{2,0},{4,6},{6,4},{1,3},{3,1},{5,7},{7,5},{8,10},{10,8},{12,... | collective-permute-start | bytes 4718600 | tf_op jit(solution)/shard_map/ppermute | solution.py:1265
  177.1 35.7 %collective-permute-start.44 = (bf16[128,1024]{1,0:T(8,128)(2,1)S(1)}, bf16[128,1024]{1,0:T(8,128)(2,1)S(1)}, u32[]{:S(2)}, u32[]{:S(2)}) collective-permute-start(bf16[128,1024]{1,0:T(8,128)(2,1)S(1)} %copy-done.97), channel_id=1, source_target_pairs={{0,2},{2,0},{4,6},{6,4},{1,3},{3,1},{5,7},{7,5},{8,10},{10,8},{12,... | collective-permute-start | bytes 786440 | tf_op jit(solution)/shard_map/ppermute | solution.py:71
  225.2 38.2 %collective-permute-start.53 = (bf16[384,2048]{1,0:T(8,128)(2,1)}, bf16[384,2048]{1,0:T(8,128)(2,1)S(1)}, u32[]{:S(2)}, u32[]{:S(2)}) collective-permute-start(bf16[384,2048]{1,0:T(8,128)(2,1)} %get-tuple-element.240), channel_id=1, source_target_pairs={{0,1},{1,0},{2,3},{3,2},{4,5},{5,4},{6,7},{7,6},{8,9},{9,8},{10,11... | collective-permute-start | bytes 4718600 | tf_op jit(solution)/shard_map/ppermute | solution.py:137
  271.5 39.4 %collective-permute-start.58 = (bf16[384,2048]{1,0:T(8,128)(2,1)}, bf16[384,2048]{1,0:T(8,128)(2,1)S(1)}, u32[]{:S(2)}, u32[]{:S(2)}) collective-permute-start(bf16[384,2048]{1,0:T(8,128)(2,1)} %get-tuple-element.267.refs_0_), channel_id=1, source_target_pairs={{0,1},{1,0},{2,3},{3,2},{4,5},{5,4},{6,7},{7,6},{8,9},{9,8},{10,11... | collective-permute-start | bytes 4718600 | tf_op jit(solution)/shard_map/ppermute | solution.py:147
  328.8 56.0 %collective-permute-start.78 = (bf16[128,3072]{1,0:T(8,128)(2,1)}, bf16[128,3072]{1,0:T(8,128)(2,1)}, u32[]{:S(2)}, u32[]{:S(2)}) collective-permute-start(bf16[128,3072]{1,0:T(8,128)(2,1)} %pad_maximum_fusion.4.refs_3_.refs_19_.refs_35_.refs_52_.refs_18_), channel_id=1, source_target_pairs={{0,2},{2,0},{4,6},{6,4},{1,3},{3,1},{5,7},{7,5},{8,10},{10,8},{12,... | collective-permute-start | bytes 2359304 | tf_op jit(solution)/shard_map/ppermute | solution.py:71
  337.3 48.9 %collective-permute-start.79 = (bf16[128,3072]{1,0:T(8,128)(2,1)}, bf16[128,3072]{1,0:T(8,128)(2,1)}, u32[]{:S(2)}, u32[]{:S(2)}) collective-permute-start(bf16[128,3072]{1,0:T(8,128)(2,1)} %collective-permute-done.40.refs_5_.refs_21_.refs_37_.refs_54_.refs_20_), channel_id=1, source_target_pairs={{0,2},{2,0},{4,6},{6,4},{1,3},{3,1},{5,7},{7,5},{8,10},{10,8},{12,... | collective-permute-start | bytes 2359304 | tf_op jit(solution)/shard_map/ppermute | solution.py:71
  339.8 44.5 %collective-permute-start.74 = (bf16[128,3072]{1,0:T(8,128)(2,1)}, bf16[128,3072]{1,0:T(8,128)(2,1)}, u32[]{:S(2)}, u32[]{:S(2)}) collective-permute-start(bf16[128,3072]{1,0:T(8,128)(2,1)} %collective-permute-done.72.refs_13_.refs_29_.refs_45_.refs_62_.refs_28_), channel_id=1, source_target_pairs={{0,8},{8,16},{16,24},{24,28},{28,20},{20,12},{12,4},{4,0},{2,6},{1... | collective-permute-start | bytes 2359304 | tf_op jit(solution)/shard_map/ppermute | solution.py:68
  339.8 44.5 %collective-permute-start.75 = (bf16[128,3072]{1,0:T(8,128)(2,1)}, bf16[128,3072]{1,0:T(8,128)(2,1)}, u32[]{:S(2)}, u32[]{:S(2)}) collective-permute-start(bf16[128,3072]{1,0:T(8,128)(2,1)} %collective-permute-done.73.refs_11_.refs_27_.refs_43_.refs_9_.refs_26_), channel_id=1, source_target_pairs={{0,8},{8,16},{16,24},{24,28},{28,20},{20,12},{12,4},{4,0},{2,6},{1... | collective-permute-start | bytes 2359304 | tf_op jit(solution)/shard_map/ppermute | solution.py:68
  382.5 45.4 %collective-permute-start.87 = (bf16[1024,3072]{1,0:T(8,128)(2,1)}, bf16[1024,3072]{1,0:T(8,128)(2,1)S(1)}, u32[]{:S(2)}, u32[]{:S(2)}) collective-permute-start(bf16[1024,3072]{1,0:T(8,128)(2,1)} %get-tuple-element.266), channel_id=1, source_target_pairs={{0,2},{2,0},{4,6},{6,4},{1,3},{3,1},{5,7},{7,5},{8,10},{10,8},{12,... | collective-permute-start | bytes 18874376 | tf_op jit(solution)/shard_map/ppermute | solution.py:71
  507.8 73.8 %collective-permute-start.101 = (bf16[1024,3072]{1,0:T(8,128)(2,1)}, bf16[1024,3072]{1,0:T(8,128)(2,1)S(1)}, u32[]{:S(2)}, u32[]{:S(2)}) collective-permute-start(bf16[1024,3072]{1,0:T(8,128)(2,1)} %get-tuple-element.294), channel_id=1, source_target_pairs={{0,2},{2,0},{4,6},{6,4},{1,3},{3,1},{5,7},{7,5},{8,10},{10,8},{12,... | collective-permute-start | bytes 18874376 | tf_op jit(solution)/shard_map/ppermute | solution.py:71
  529.4 75.4 %collective-permute-start.104 = (bf16[1024,3072]{1,0:T(8,128)(2,1)}, bf16[1024,3072]{1,0:T(8,128)(2,1)}, u32[]{:S(2)}, u32[]{:S(2)}) collective-permute-start(bf16[1024,3072]{1,0:T(8,128)(2,1)} %get-tuple-element.305), channel_id=1, source_target_pairs={{0,2},{2,0},{4,6},{6,4},{1,3},{3,1},{5,7},{7,5},{8,10},{10,8},{12,... | collective-permute-start | bytes 18874376 | tf_op jit(solution)/shard_map/ppermute | solution.py:71
  531.9 36.2 %collective-permute-start.99 = (bf16[384,2048]{1,0:T(8,128)(2,1)S(1)}, bf16[384,2048]{1,0:T(8,128)(2,1)S(1)}, u32[]{:S(2)}, u32[]{:S(2)}) collective-permute-start(bf16[384,2048]{1,0:T(8,128)(2,1)S(1)} %copy-done.53), channel_id=1, source_target_pairs={{0,1},{1,0},{2,3},{3,2},{4,5},{5,4},{6,7},{7,6},{8,9},{9,8},{10,11... | collective-permute-start | bytes 4718600 | tf_op jit(solution)/shard_map/ppermute | solution.py:137
  546.0 31.1 %collective-permute-start.106 = (bf16[128,3072]{1,0:T(8,128)(2,1)}, bf16[128,3072]{1,0:T(8,128)(2,1)}, u32[]{:S(2)}, u32[]{:S(2)}) collective-permute-start(bf16[128,3072]{1,0:T(8,128)(2,1)} %add_convert_fusion.16), channel_id=1, source_target_pairs={{0,8},{8,16},{16,24},{24,28},{28,20},{20,12},{12,4},{4,0},{2,6},{1... | collective-permute-start | bytes 2359304 | tf_op jit(solution)/shard_map/ppermute | solution.py:68
  587.9 44.4 %collective-permute-start.105 = (bf16[384,2048]{1,0:T(8,128)(2,1)S(1)}, bf16[384,2048]{1,0:T(8,128)(2,1)}, u32[]{:S(2)}, u32[]{:S(2)}) collective-permute-start(bf16[384,2048]{1,0:T(8,128)(2,1)S(1)} %copy-done.15), channel_id=1, source_target_pairs={{0,1},{1,0},{2,3},{3,2},{4,5},{5,4},{6,7},{7,6},{8,9},{9,8},{10,11... | collective-permute-start | bytes 4718600 | tf_op jit(solution)/shard_map/ppermute | solution.py:147
  644.2 46.5 %collective-permute-start.114 = (bf16[128,3072]{1,0:T(8,128)(2,1)S(1)}, bf16[128,3072]{1,0:T(8,128)(2,1)S(1)}, u32[]{:S(2)}, u32[]{:S(2)}) collective-permute-start(bf16[128,3072]{1,0:T(8,128)(2,1)S(1)} %add_convert_fusion.9), channel_id=1, source_target_pairs={{0,8},{8,16},{16,24},{24,28},{28,20},{20,12},{12,4},{4,0},{2,6},{1... | collective-permute-start | bytes 2359304 | tf_op jit(solution)/shard_map/ppermute | solution.py:68
  651.3 41.1 %collective-permute-start.115 = (bf16[128,3072]{1,0:T(8,128)(2,1)}, bf16[128,3072]{1,0:T(8,128)(2,1)}, u32[]{:S(2)}, u32[]{:S(2)}) collective-permute-start(bf16[128,3072]{1,0:T(8,128)(2,1)} %add_convert_fusion.8), channel_id=1, source_target_pairs={{0,8},{8,16},{16,24},{24,28},{28,20},{20,12},{12,4},{4,0},{2,6},{1... | collective-permute-start | bytes 2359304 | tf_op jit(solution)/shard_map/ppermute | solution.py:68
  686.6 42.1 %collective-permute-start.109 = (bf16[1536,1024]{1,0:T(8,128)(2,1)}, bf16[1536,1024]{1,0:T(8,128)(2,1)S(1)}, u32[]{:S(2)}, u32[]{:S(2)}) collective-permute-start(bf16[1536,1024]{1,0:T(8,128)(2,1)} %get-tuple-element.316), channel_id=1, source_target_pairs={{0,2},{2,0},{4,6},{6,4},{1,3},{3,1},{5,7},{7,5},{8,10},{10,8},{12,... | collective-permute-start | bytes 9437192 | tf_op jit(solution)/shard_map/ppermute | solution.py:71
  694.3 32.8 %collective-permute-start.118 = (bf16[128,3072]{1,0:T(8,128)(2,1)S(1)}, bf16[128,3072]{1,0:T(8,128)(2,1)S(1)}, u32[]{:S(2)}, u32[]{:S(2)}) collective-permute-start(bf16[128,3072]{1,0:T(8,128)(2,1)S(1)} %add_convert_fusion.6), channel_id=1, source_target_pairs={{0,8},{8,16},{16,24},{24,28},{28,20},{20,12},{12,4},{4,0},{2,6},{1... | collective-permute-start | bytes 2359304 | tf_op jit(solution)/shard_map/ppermute | solution.py:68
  696.3 60.0 %collective-permute-start.113 = (bf16[384,2048]{1,0:T(8,128)(2,1)}, bf16[384,2048]{1,0:T(8,128)(2,1)}, u32[]{:S(2)}, u32[]{:S(2)}) collective-permute-start(bf16[384,2048]{1,0:T(8,128)(2,1)} %get-tuple-element.327), channel_id=1, source_target_pairs={{0,1},{1,0},{2,3},{3,2},{4,5},{5,4},{6,7},{7,6},{8,9},{9,8},{10,11... | collective-permute-start | bytes 4718600 | tf_op jit(solution)/shard_map/ppermute | solution.py:137
  730.8 54.8 %collective-permute-start.116 = (bf16[768,1024]{1,0:T(8,128)(2,1)}, bf16[768,1024]{1,0:T(8,128)(2,1)}, u32[]{:S(2)}, u32[]{:S(2)}) collective-permute-start(bf16[768,1024]{1,0:T(8,128)(2,1)} %add_convert_fusion), channel_id=1, source_target_pairs={{0,4},{2,6},{4,0},{6,2},{1,5},{3,7},{5,1},{7,3},{8,12},{10,14},{12... | collective-permute-start | bytes 4718600 | tf_op jit(solution)/shard_map/ppermute | solution.py:1359
  739.6 35.8 %collective-permute-start.119 = (bf16[128,3072]{1,0:T(8,128)(2,1)}, bf16[128,3072]{1,0:T(8,128)(2,1)}, u32[]{:S(2)}, u32[]{:S(2)}) collective-permute-start(bf16[128,3072]{1,0:T(8,128)(2,1)} %add_convert_fusion.5), channel_id=1, source_target_pairs={{0,8},{8,16},{16,24},{24,28},{28,20},{20,12},{12,4},{4,0},{2,6},{1... | collective-permute-start | bytes 2359304 | tf_op jit(solution)/shard_map/ppermute | solution.py:68
  739.9 44.0 %collective-permute-start.120 = (bf16[128,3072]{1,0:T(8,128)(2,1)S(1)}, bf16[128,3072]{1,0:T(8,128)(2,1)}, u32[]{:S(2)}, u32[]{:S(2)}) collective-permute-start(bf16[128,3072]{1,0:T(8,128)(2,1)S(1)} %add_convert_fusion.4), channel_id=1, source_target_pairs={{0,8},{8,16},{16,24},{24,28},{28,20},{20,12},{12,4},{4,0},{2,6},{1... | collective-permute-start | bytes 2359304 | tf_op jit(solution)/shard_map/ppermute | solution.py:68
  761.2 129.7 %collective-permute-start.136 = (bf16[384,2048]{1,0:T(8,128)(2,1)}, bf16[384,2048]{1,0:T(8,128)(2,1)}, u32[]{:S(2)}, u32[]{:S(2)}) collective-permute-start(bf16[384,2048]{1,0:T(8,128)(2,1)} %output.1.refs_0_), channel_id=1, source_target_pairs={{0,1},{1,0},{2,3},{3,2},{4,5},{5,4},{6,7},{7,6},{8,9},{9,8},{10,11... | collective-permute-start | bytes 4718600 | tf_op jit(solution)/shard_map/ppermute | solution.py:147
  762.8 51.9 %collective-permute-start.121 = (bf16[1024,1024]{1,0:T(8,128)(2,1)}, bf16[1024,1024]{1,0:T(8,128)(2,1)}, u32[]{:S(2)}, u32[]{:S(2)}) collective-permute-start(bf16[1024,1024]{1,0:T(8,128)(2,1)} %get-tuple-element.346), channel_id=1, source_target_pairs={{0,2},{2,0},{4,6},{6,4},{1,3},{3,1},{5,7},{7,5},{8,10},{10,8},{12,... | collective-permute-start | bytes 6291464 | tf_op jit(solution)/shard_map/ppermute | solution.py:71
  778.3 33.4 %collective-permute-start.123 = (bf16[128,3072]{1,0:T(8,128)(2,1)}, bf16[128,3072]{1,0:T(8,128)(2,1)}, u32[]{:S(2)}, u32[]{:S(2)}) collective-permute-start(bf16[128,3072]{1,0:T(8,128)(2,1)} %add_convert_fusion.3), channel_id=1, source_target_pairs={{0,8},{8,16},{16,24},{24,28},{28,20},{20,12},{12,4},{4,0},{2,6},{1... | collective-permute-start | bytes 2359304 | tf_op jit(solution)/shard_map/ppermute | solution.py:68
  810.1 30.9 %collective-permute-start.126 = (bf16[128,3072]{1,0:T(8,128)(2,1)}, bf16[128,3072]{1,0:T(8,128)(2,1)}, u32[]{:S(2)}, u32[]{:S(2)}) collective-permute-start(bf16[128,3072]{1,0:T(8,128)(2,1)} %add_convert_fusion.1), channel_id=1, source_target_pairs={{0,8},{8,16},{16,24},{24,28},{28,20},{20,12},{12,4},{4,0},{2,6},{1... | collective-permute-start | bytes 2359304 | tf_op jit(solution)/shard_map/ppermute | solution.py:68
  810.1 36.9 %collective-permute-start.127 = (bf16[1024,1152]{1,0:T(8,128)(2,1)}, bf16[1024,1152]{1,0:T(8,128)(2,1)}, u32[]{:S(2)}, u32[]{:S(2)}) collective-permute-start(bf16[1024,1152]{1,0:T(8,128)(2,1)} %get-tuple-element.357), channel_id=1, source_target_pairs={{0,2},{2,0},{4,6},{6,4},{1,3},{3,1},{5,7},{7,5},{8,10},{10,8},{12,... | collective-permute-start | bytes 7077896 | tf_op jit(solution)/shard_map/ppermute | solution.py:71
  826.4 32.0 %collective-permute-start.125 = (bf16[128,1024]{1,0:T(8,128)(2,1)S(1)}, bf16[128,1024]{1,0:T(8,128)(2,1)}, u32[]{:S(2)}, u32[]{:S(2)}) collective-permute-start(bf16[128,1024]{1,0:T(8,128)(2,1)S(1)} %add_convert_fusion.41), channel_id=1, source_target_pairs={{0,8},{8,16},{16,24},{24,28},{28,20},{20,12},{12,4},{4,0},{2,6},{1... | collective-permute-start | bytes 786440 | tf_op jit(solution)/shard_map/ppermute | solution.py:68
  841.0 38.0 %collective-permute-start.132 = (bf16[384,2048]{1,0:T(8,128)(2,1)}, bf16[384,2048]{1,0:T(8,128)(2,1)}, u32[]{:S(2)}, u32[]{:S(2)}) collective-permute-start(bf16[384,2048]{1,0:T(8,128)(2,1)} %get-tuple-element.364), channel_id=1, source_target_pairs={{0,1},{1,0},{2,3},{3,2},{4,5},{5,4},{6,7},{7,6},{8,9},{9,8},{10,11... | collective-permute-start | bytes 4718600 | tf_op jit(solution)/shard_map/ppermute | solution.py:137
  912.6 32.6 %collective-permute-start.143 = (bf16[384,2048]{1,0:T(8,128)(2,1)S(1)}, bf16[384,2048]{1,0:T(8,128)(2,1)}, u32[]{:S(2)}, u32[]{:S(2)}) collective-permute-start(bf16[384,2048]{1,0:T(8,128)(2,1)S(1)} %copy-done.2), channel_id=1, source_target_pairs={{0,1},{1,0},{2,3},{3,2},{4,5},{5,4},{6,7},{7,6},{8,9},{9,8},{10,11... | collective-permute-start | bytes 4718600 | tf_op jit(solution)/shard_map/ppermute | solution.py:147
  (231 other events, 3909.9 us)
